TPU v7x, 256 devices: a whole 4x4x8 slice. The times are simulated.
256 devices in a mesh: dp: 32 (over z, y), cuts: 8 (over x, core).
Axes of the slice: x: 4, y: 4, z: 8, core: 2. Of those that a mesh axis runs over, the one named last changes fastest.
Arguments:
- tokens: bfloat16 [512, 6144], P('dp', 'cuts'), may hold values from -6 to 6
- out_grad: bfloat16 [512, 6144], P('dp', 'cuts'), may hold values from -6 to 6
- gate_values: float32 [512, 2], P('dp'), may hold values from 0.2 to 1
- routing: int32 [512, 2], P('dp'), may hold values from 0 to 7, all different within a row; in each aligned block of 16 rows (0 to 15, 16 to 31, ...) at most 8 rows name the same one
- gate_weight: bfloat16 [32, 6144, 2816], P('dp', None, 'cuts'), may hold values from -0.078125 to 0.078125
- up_weight: bfloat16 [32, 6144, 2816], P('dp', None, 'cuts'), may hold values from -0.078125 to 0.078125
- down_weight: bfloat16 [32, 2816, 6144], P('dp', 'cuts'), may hold values from -0.0546875 to 0.0546875
Outputs:
- mixed: bfloat16 [512, 6144], P('dp', 'cuts')
- token_grad: bfloat16 [512, 6144], P('dp', 'cuts')
Inputs may be any that keep to these rules, and one draw needn't show every extreme that they name: `routing`: each row names 2 different experts; in each aligned block of 16 rows (the rows of one index of dp) no expert is named by more than 8 rows, and in some block one expert is named by exactly 8 rows.
All inputs are finite; a program needn't handle non-finite values.
Results may differ from a plain program's by a relative error of at most 0.019.
Values may be sent and summed in bfloat16 or wider, within the bound.
No kernel may reach another device: no remote copies, remote signals or barrier semaphores. Data moves between devices by JAX's collectives and lax.ppermute only.
A program may use at most 64 MiB of HBM per device.

v0:
```python
import jax
import jax.numpy as jnp
from jax import lax
from jax.experimental import pallas as pl
from jax.experimental.pallas import tpu as pltpu
from jax.sharding import PartitionSpec as P

E = 8
NY = 4
NX = 4
CAP = 8
BF = jnp.bfloat16
F32 = jnp.float32
NT = (((1,), (1,)), ((), ()))
VMEM_LIMIT = 20 << 20


def swap_z(v):
    groups = [[z * NY + y for z in range(E)] for y in range(NY)]
    return lax.all_to_all(v, "dp", 0, 0, axis_index_groups=groups, tiled=True)


def to_y(v, d):
    perm = [(z * NY + y, z * NY + (y + d) % NY) for z in range(E) for y in range(NY)]
    return lax.ppermute(v, "dp", perm)


def to_x(v, d):
    perm = [(x * 2 + c, (x + d) % NX * 2 + c) for x in range(NX) for c in range(2)]
    return lax.ppermute(v, "cuts", perm)


def to_core(v):
    return lax.ppermute(v, "cuts", [(i, i ^ 1) for i in range(2 * NX)])


def slots_of(routing, gate_values):
    hit = routing[:, :, None] == jnp.arange(E, dtype=jnp.int32)
    chosen = jnp.any(hit, axis=1)
    gates = jnp.sum(jnp.where(hit, gate_values[:, :, None], 0.0), axis=1)
    rows = routing.shape[0]
    below = jnp.arange(rows)[:, None] > jnp.arange(rows)[None, :]
    position = jnp.sum(
        jnp.where(below[:, :, None] & chosen[None, :, :], 1, 0), axis=1
    )
    slot = position[:, :, None] == jnp.arange(CAP, dtype=jnp.int32)
    select = chosen[:, :, None] & slot
    weight = jnp.where(select, gates[:, :, None], 0.0)
    return select.reshape(rows, E * CAP), weight.reshape(rows, E * CAP)


def first_gather(a, b):
    order = (1, 3, 2)
    ra, rb = {0: a}, {0: b}
    for d in order:
        ra[d] = to_y(a, d)
        rb[d] = to_x(b, d)
    return [ra[d] for d in range(4)], [rb[d] for d in range(4)]


def second_gather(a, b):
    a, b = lax.optimization_barrier((a, b))
    ra, rb = {0: a}, {0: b}
    for d in (2, 1, 3):
        ra[d] = to_x(a, d)
        rb[d] = to_y(b, d)
    own = [ra[d] for d in range(4)] + [rb[d] for d in range(4)]
    return own, [to_core(v) for v in own]


def add(*parts):
    total = parts[0].astype(F32)
    for p in parts[1:]:
        total = total + p.astype(F32)
    return total.astype(BF)


def first_scatter(sa, sb):
    sa, sb = lax.optimization_barrier((sa, sb))
    ra, rb = [sa[0]], [sb[0]]
    for d in (2, 1, 3):
        ra.append(to_x(sa[d], d))
        rb.append(to_y(sb[d], -d))
    return add(*ra), add(*rb)


def second_scatter(ta, tb):
    ta, tb = lax.optimization_barrier((ta, tb))
    ra, rb = [ta[0]], [tb[0]]
    for d in (2, 1, 3):
        ra.append(to_y(ta[d], -d))
        rb.append(to_x(tb[d], d))
    return add(*ra), add(*rb)


def weight_copies(cols, width, weights, buf, sem):
    copies = []
    for k in range(NX):
        at = pl.ds(pl.multiple_of(cols[k] * width, 128), width)
        copies.append(
            [
                pltpu.make_async_copy(w.at[:, at], buf.at[i, k], sem.at[i, k])
                for i, w in enumerate(weights)
            ]
        )
    return copies


def fetch_weights(cols, weights, buf, sem):
    width = buf.shape[-1]
    for block in weight_copies(cols, width, weights, buf, sem):
        for copy in block:
            copy.start()

    def wait(k):
        for i, w in enumerate(weights):
            at = pl.ds(0, width)
            pltpu.make_async_copy(w.at[:, at], buf.at[i, k], sem.at[i, k]).wait()

    return wait


def load_rows(pieces, rows):
    half = rows.shape[2] // 2
    step = half // NY
    for i in range(2):
        for k in range(NX):
            rows[k, i, :half] = pieces[k][i].reshape(half, -1)
            for j in range(NY):
                at = half + j * step
                rows[k, i, at : at + step] = pieces[NX + j][i, k]


def contract(wait, rows, buf, gate, up, hid):
    @pl.loop(0, NX)
    def _(k):
        wait(k)
        r = rows[k, 0]
        gate[...] += lax.dot_general(r, buf[0, k], NT, preferred_element_type=F32)
        up[...] += lax.dot_general(r, buf[1, k], NT, preferred_element_type=F32)
        hid[...] += lax.dot_general(
            rows[k, 1], buf[2, k], NT, preferred_element_type=F32
        )


def expand(wait, hidden, gate_grad, up_grad, buf, out_a, out_b):
    half = hidden.shape[0] // 2
    step = half // NY

    def put(k, i, value):
        out_a[k, i] = value[:half].reshape(NY, step, -1)
        for j in range(NY):
            out_b[j, i, k] = value[half + j * step : half + (j + 1) * step]

    @pl.loop(0, NX)
    def _(k):
        at = (NX - k) & (NX - 1)
        if wait is not None:
            wait(at)
        o = jnp.dot(hidden[...], buf[2, at], preferred_element_type=F32)
        put(k, 0, o.astype(BF))
        o = jnp.dot(gate_grad[...], buf[0, at], preferred_element_type=F32)
        o = o + jnp.dot(up_grad[...], buf[1, at], preferred_element_type=F32)
        put(k, 1, o.astype(BF))


def own_kernel(cols, *refs):
    pieces, weights, (gate, up, hid, rows, buf, sem) = refs[:8], refs[8:11], refs[11:]
    wait = fetch_weights(cols, weights, buf, sem)
    load_rows(pieces, rows)
    for ref in (gate, up, hid):
        ref[...] = jnp.zeros_like(ref)
    contract(wait, rows, buf, gate, up, hid)


def other_kernel(cols, *refs):
    pieces, weights, partial, rest = refs[:8], refs[8:11], refs[11:14], refs[14:]
    out_a, out_b, hidden, gate_grad, up_grad, rows, gate, up, hid, buf, sem = rest
    wait = fetch_weights(cols, weights, buf, sem)
    load_rows(pieces, rows)
    for ref, part in zip((gate, up, hid), partial):
        ref[...] = part[...]
    contract(wait, rows, buf, gate, up, hid)
    g, h = gate[...], hid[...]
    sigma = jax.nn.sigmoid(g)
    hidden[...] = (g * sigma * up[...]).astype(BF)
    gate_grad[...] = (h * up[...] * sigma * (1.0 + g * (1.0 - sigma))).astype(BF)
    up_grad[...] = (h * g * sigma).astype(BF)
    expand(None, hidden, gate_grad, up_grad, buf, out_a, out_b)


def last_kernel(cols, *refs):
    (hidden, gate_grad, up_grad), weights, (out_a, out_b, buf, sem) = (
        refs[:3],
        refs[3:6],
        refs[6:],
    )
    wait = fetch_weights(cols, weights, buf, sem)
    expand(wait, hidden, gate_grad, up_grad, buf, out_a, out_b)


def call(body, name, cols, arrays, weights, partial, out, scratch, products):
    hidden, width = weights[0].shape[0], weights[0].shape[1] // (2 * NX)
    rows = E * CAP * NY
    return pl.pallas_call(
        body,
        name=name,
        out_shape=out,
        in_specs=[pl.BlockSpec(memory_space=pltpu.SMEM)]
        + [pl.BlockSpec(memory_space=pltpu.VMEM)] * len(arrays)
        + [pl.BlockSpec(memory_space=pl.ANY)] * 3
        + [pl.BlockSpec(memory_space=pltpu.VMEM)] * len(partial),
        out_specs=[pl.BlockSpec(memory_space=pltpu.VMEM)] * len(out),
        scratch_shapes=scratch
        + [
            pltpu.VMEM((3, NX, hidden, width), BF),
            pltpu.SemaphoreType.DMA((3, NX)),
        ],
        compiler_params=pltpu.CompilerParams(vmem_limit_bytes=VMEM_LIMIT),
        cost_estimate=pl.CostEstimate(
            flops=2 * products * rows * width * NX * hidden,
            bytes_accessed=7 << 20,
            transcendentals=0,
        ),
    )(cols, *arrays, *weights, *partial)


def on_device(tokens, out_grad, gate_values, routing, gate_weight, up_weight, down_weight):
    width = tokens.shape[1]
    cut = lax.axis_index("cuts")
    x, c = cut // 2, cut % 2
    wg = jnp.swapaxes(gate_weight[0], 0, 1)
    wu = jnp.swapaxes(up_weight[0], 0, 1)
    w2 = down_weight[0]
    hidden = w2.shape[0]
    k = jnp.arange(NX, dtype=jnp.int32)
    own_cols = (x - k + NX) % NX * 2 + c
    other_cols = (x - k + NX) % NX * 2 + (1 - c)
    rows = NY * E * CAP

    select, weight = slots_of(routing, gate_values)
    pick = select.astype(BF).T
    send_x = jnp.dot(pick, tokens, preferred_element_type=F32).astype(BF)
    slot_gate = jnp.sum(weight, axis=0)
    send_dy = jnp.dot(pick, out_grad, preferred_element_type=F32)
    send_dy = (slot_gate[:, None] * send_dy).astype(BF)
    send = jnp.concatenate(
        [send_x.reshape(E, CAP, width), send_dy.reshape(E, CAP, width)], axis=1
    )
    got = swap_z(send).reshape(2, E // 2, 2, CAP, width)
    got = jnp.swapaxes(got, 1, 2).reshape(2, 2, -1, width)

    fa, fb = first_gather(got[0], got[1])

    own, other = second_gather(jnp.stack(fa, axis=1), jnp.stack(fb, axis=1))

    weights = (wg, wu, w2)
    pre = [jax.ShapeDtypeStruct((rows, hidden), F32)] * 3
    act = [jax.ShapeDtypeStruct((rows, hidden), BF)] * 3
    pieces = [jax.ShapeDtypeStruct((4, 2, 4, rows // 8, width), BF)] * 2
    row_buf = [pltpu.VMEM((NX, 2, rows, width), BF)]
    pre_buf = [pltpu.VMEM((rows, hidden), F32)] * 3
    partial = call(own_kernel, "own", own_cols, own, weights, [], pre, row_buf, 3)
    far_a, far_b, *act = call(
        other_kernel, "other", other_cols, other, weights, partial,
        pieces + act, row_buf + pre_buf, 6,
    )
    near_a, near_b = call(
        last_kernel, "last", own_cols, act, weights, [], pieces, [], 3
    )
    got_a, got_b = to_core(far_a), to_core(far_b)
    sa = [add(near_a[d], got_a[d]) for d in range(4)]
    sb = [add(near_b[d], got_b[d]) for d in range(4)]
    ta, tb = first_scatter(sa, sb)
    ra, rb = second_scatter(
        [ta[:, d] for d in range(4)], [tb[:, d] for d in range(4)]
    )
    back = jnp.stack([ra, rb]).reshape(2, 2, E // 2, CAP, width)
    back = jnp.swapaxes(back, 1, 2).reshape(E, 2 * CAP, width)
    back = swap_z(back)
    back_y = back[:, :CAP].reshape(E * CAP, width)
    back_dx = back[:, CAP:].reshape(E * CAP, width)
    mixed = jnp.dot(weight, back_y.astype(F32), precision=lax.Precision.HIGHEST)
    grad = jnp.dot(select.astype(BF), back_dx, preferred_element_type=F32)
    return mixed.astype(BF), grad.astype(BF)


def solution(mesh):
    return jax.shard_map(
        on_device,
        mesh=mesh,
        in_specs=(
            P("dp", "cuts"),
            P("dp", "cuts"),
            P("dp", None),
            P("dp", None),
            P("dp", None, "cuts"),
            P("dp", None, "cuts"),
            P("dp", "cuts", None),
        ),
        out_specs=(P("dp", "cuts"), P("dp", "cuts")),
        check_vma=False,
    )
```

profile of v0, /device:TPU:6, one launch (start us, length us, event | category | flops | bytes accessed | tf_op | source)
XLA Modules:
  0.0 156.5 jit_solution(8204892479543483360)
XLA Ops:
  0.7 0.7 fusion.36
  1.3 0.7 select_reduce_fusion.2
  3.0 1.0 fusion.1
  3.9 18.7 %all_to_all.10 = bf16[8,16,768]{2,1,0:T(8,128)(2,1)S(1)} all-to-all(bf16[8,16,768]{2,1,0:T(8,128)(2,1)S(1)} %pad_maximum_fusion.2), channel_id=1, replica_groups={{0,32,64,96,128,160,192,224},{8,40,72,104,136,168,200,232},{16,48,80,11..., dimensions={0} | all-to-all | bytes 393216 | tf_op jit(solution)/shard_map/all_to_all | solution.py:20
  22.7 3.3 %collective-permute-start.1 = (bf16[2,32,768]{2,1,0:T(8,128)(2,1)S(1)}, bf16[2,32,768]{2,1,0:T(8,128)(2,1)S(1)}, u32[]{:S(2)}, u32[]{:S(2)}) collective-permute-start(bf16[2,32,768]{2,1,0:T(8,128)(2,1)S(1)} %bitcast.122), channel_id=1, source_target_pairs={{0,16},{8,24},{16,0},{24,8},{32,48},{40,56},{48,32},{56,40},{64,80... | collective-permute-start | bytes 294920 | tf_op jit(solution)/shard_map/ppermute | solution.py:25
  26.0 0.7 collective-permute-start
  26.7 2.6 %collective-permute-start.2 = (bf16[2,32,768]{2,1,0:T(8,128)(2,1)S(1)}, bf16[2,32,768]{2,1,0:T(8,128)(2,1)S(1)}, u32[]{:S(2)}, u32[]{:S(2)}) collective-permute-start(bf16[2,32,768]{2,1,0:T(8,128)(2,1)S(1)} %bitcast.124), channel_id=1, source_target_pairs={{0,24},{8,0},{16,8},{24,16},{32,56},{40,32},{48,40},{56,48},{64,88... | collective-permute-start | bytes 294920 | tf_op jit(solution)/shard_map/ppermute | solution.py:25
  29.2 1.5 collective-permute-start.4
  30.7 2.1 %collective-permute-start.3 = (bf16[2,32,768]{2,1,0:T(8,128)(2,1)S(1)}, bf16[2,32,768]{2,1,0:T(8,128)(2,1)S(1)}, u32[]{:S(2)}, u32[]{:S(2)}) collective-permute-start(bf16[2,32,768]{2,1,0:T(8,128)(2,1)S(1)} %bitcast.127), channel_id=1, source_target_pairs={{0,2},{1,3},{2,4},{3,5},{4,6},{5,7},{6,0},{7,1},{8,10},{9,11},{10,... | collective-permute-start | bytes 294920 | tf_op jit(solution)/shard_map/ppermute | solution.py:30
  32.9 2.5 %collective-permute-done.4 = bf16[2,32,768]{2,1,0:T(8,128)(2,1)S(1)} collective-permute-done((bf16[2,32,768]{2,1,0:T(8,128)(2,1)S(1)}, bf16[2,32,768]{2,1,0:T(8,128)(2,1)S(1)}, u32[]{:S(2)}, u32[]{:S(2)}) %collective-permute-start.4) | collective-permute-done | bytes 98336 | tf_op jit(solution)/shard_map/ppermute | solution.py:30
  35.5 4.0 %collective-permute-done.5 = bf16[2,32,768]{2,1,0:T(8,128)(2,1)S(1)} collective-permute-done((bf16[2,32,768]{2,1,0:T(8,128)(2,1)S(1)}, bf16[2,32,768]{2,1,0:T(8,128)(2,1)S(1)}, u32[]{:S(2)}, u32[]{:S(2)}) %collective-permute-start.5) | collective-permute-done | bytes 98336 | tf_op jit(solution)/shard_map/ppermute | solution.py:30
  39.6 1.0 collective-permute-start.9
  40.7 2.2 %collective-permute-start.7 = (bf16[2,4,32,768]{3,2,1,0:T(8,128)(2,1)S(1)}, bf16[2,4,32,768]{3,2,1,0:T(8,128)(2,1)S(1)}, u32[]{:S(2)}, u32[]{:S(2)}) collective-permute-start(bf16[2,4,32,768]{3,2,1,0:T(8,128)(2,1)S(1)} %pad_maximum_fusion.refs_0_), channel_id=1, source_target_pairs={{0,2},{1,3},{2,4},{3,5},{4,6},{5,7},{6,0},{7,1},{8,10},{9,11},{10,... | collective-permute-start | bytes 1179656 | tf_op jit(solution)/shard_map/ppermute | solution.py:30
  42.8 12.7 %collective-permute-done.11.refs_3_ = bf16[2,4,32,768]{3,2,1,0:T(8,128)(2,1)S(1)} collective-permute-done((bf16[2,4,32,768]{3,2,1,0:T(8,128)(2,1)S(1)}, bf16[2,4,32,768]{3,2,1,0:T(8,128)(2,1)S(1)}, u32[]{:S(2)}, u32[]{:S(2)}) %collective-permute-start.11) | collective-permute-done | bytes 393248 | tf_op jit(solution)/shard_map/ppermute | solution.py:30
  55.5 0.9 collective-permute-start.14
  56.4 0.5 collective-permute-start.12
  57.0 8.0 %collective-permute-done.16.refs_6_ = bf16[2,4,32,768]{3,2,1,0:T(8,128)(2,1)} collective-permute-done((bf16[2,4,32,768]{3,2,1,0:T(8,128)(2,1)S(1)}, bf16[2,4,32,768]{3,2,1,0:T(8,128)(2,1)}, u32[]{:S(2)}, u32[]{:S(2)}) %collective-permute-start.16) | collective-permute-done | bytes 393248 | tf_op jit(solution)/shard_map/ppermute | solution.py:25
  65.0 3.8 %collective-permute-done.14.refs_5_ = bf16[2,4,32,768]{3,2,1,0:T(8,128)(2,1)} collective-permute-done((bf16[2,4,32,768]{3,2,1,0:T(8,128)(2,1)S(1)}, bf16[2,4,32,768]{3,2,1,0:T(8,128)(2,1)}, u32[]{:S(2)}, u32[]{:S(2)}) %collective-permute-start.14) | collective-permute-done | bytes 393248 | tf_op jit(solution)/shard_map/ppermute | solution.py:25
  68.8 0.5 collective-permute-start.17
  69.4 0.8 copy-done.7
  70.2 2.2 %copy-done.1 = bf16[1,6144,352]{1,2,0:T(8,128)(2,1)S(1)} copy-done((bf16[1,6144,352]{1,2,0:T(8,128)(2,1)S(1)}, bf16[1,6144,352]{1,2,0:T(8,128)(2,1)}, u32[]{:S(2)}) %copy-start.1) | copy-done | bytes 4325400
  72.4 2.2 %copy-done.3 = bf16[1,6144,352]{1,2,0:T(8,128)(2,1)S(1)} copy-done((bf16[1,6144,352]{1,2,0:T(8,128)(2,1)S(1)}, bf16[1,6144,352]{1,2,0:T(8,128)(2,1)}, u32[]{:S(2)}) %copy-start.3) | copy-done | bytes 4325400
  74.6 2.2 %copy-done.5 = bf16[1,352,6144]{2,1,0:T(8,128)(2,1)S(1)} copy-done((bf16[1,352,6144]{2,1,0:T(8,128)(2,1)S(1)}, bf16[1,352,6144]{2,1,0:T(8,128)(2,1)}, u32[]{:S(2)}) %copy-start.5) | copy-done | bytes 4325400
  76.8 5.5 %own.1 = (f32[256,352]{1,0:T(8,128)S(1)}, f32[256,352]{1,0:T(8,128)S(1)}, f32[256,352]{1,0:T(8,128)S(1)}) custom-call(s32[4]{0:T(128)S(1)} %get-tuple-element.81.cols, bf16[2,4,32,768]{3,2,1,0:T(8,128)(2,1)S(1)} %pad_maximum_fusion.refs_0_, bf16[2,4,32,768]{3,2,1,0:T(8,128)(2,1)S(1)} %collective-permute-done.7.refs_1_, ...), custom_call_target="tpu_custom_call" | custom-call | flops 1660944384 | bytes 7340032 | tf_op jit(solution)/shard_map/own/pallas_call | solution.py:205
  82.4 2.2 %copy-done.2 = bf16[1,6144,352]{1,2,0:T(8,128)(2,1)S(1)} copy-done((bf16[1,6144,352]{1,2,0:T(8,128)(2,1)S(1)}, bf16[1,6144,352]{1,2,0:T(8,128)(2,1)}, u32[]{:S(2)}) %copy-start.2) | copy-done | bytes 4325400
  84.6 2.2 %copy-done.4 = bf16[1,6144,352]{1,2,0:T(8,128)(2,1)S(1)} copy-done((bf16[1,6144,352]{1,2,0:T(8,128)(2,1)S(1)}, bf16[1,6144,352]{1,2,0:T(8,128)(2,1)}, u32[]{:S(2)}) %copy-start.4) | copy-done | bytes 4325400
  86.8 2.2 %copy-done.6 = bf16[1,352,6144]{2,1,0:T(8,128)(2,1)S(1)} copy-done((bf16[1,352,6144]{2,1,0:T(8,128)(2,1)S(1)}, bf16[1,352,6144]{2,1,0:T(8,128)(2,1)}, u32[]{:S(2)}) %copy-start.6) | copy-done | bytes 4325400
  89.1 9.0 %other.1 = (bf16[4,2,4,32,768]{4,3,2,1,0:T(8,128)(2,1)S(1)}, bf16[4,2,4,32,768]{4,3,2,1,0:T(8,128)(2,1)S(1)}, bf16[256,352]{1,0:T(8,128)(2,1)S(1)}, bf16[256,352]{1,0:T(8,128)(2,1)S(1)}, bf16[256,352]{1,0:T(8,128)(2,1)S(1)}) custom-call(s32[4]{0:T(128)S(1)} %get-tuple-element.80.cols, bf16[2,4,32,768]{3,2,1,0:T(8,128)(2,1)S(1)} %collective-permute-done.6.refs_0_, ...), custom_call_target="tpu_custom_call" | custom-call | flops 3321888768 | bytes 7340032 | tf_op jit(solution)/shard_map/other/pallas_call | solution.py:205
  98.1 0.6 collective-permute-start.20
  98.8 4.4 %last.1 = (bf16[4,2,4,32,768]{4,3,2,1,0:T(8,128)(2,1)S(1)}, bf16[4,2,4,32,768]{4,3,2,1,0:T(8,128)(2,1)S(1)}) custom-call(s32[4]{0:T(128)S(1)} %get-tuple-element.81.cols, bf16[256,352]{1,0:T(8,128)(2,1)S(1)} %get-tuple-element.35.refs_0_, bf16[256,352]{1,0:T(8,128)(2,1)S(1)} %get-tuple-element.36.refs_1_, bf16[256,352]{1,0:T(8,128)(2,1)S(1)} %get-tuple-element.37.refs_2_, ...), custom_call_target="tpu_custom_call" | custom-call | flops 1660944384 | bytes 7340032 | tf_op jit(solution)/shard_map/last/pallas_call | solution.py:205
  103.2 0.6 fusion.8
  104.0 0.6 fusion.12
  104.7 2.0 %collective-permute-start.24 = (bf16[2,4,32,768]{3,2,1,0:T(8,128)(2,1)S(1)}, bf16[2,4,32,768]{3,2,1,0:T(8,128)(2,1)S(1)}, u32[]{:S(2)}, u32[]{:S(2)}) collective-permute-start(bf16[2,4,32,768]{3,2,1,0:T(8,128)(2,1)S(1)} %get-tuple-element.45), channel_id=1, source_target_pairs={{0,6},{1,7},{2,0},{3,1},{4,2},{5,3},{6,4},{7,5},{8,14},{9,15},{10,... | collective-permute-start | bytes 1179656 | tf_op jit(solution)/shard_map/ppermute | solution.py:30
  107.1 1.2 collective-permute-start.26
  108.3 9.9 %collective-permute-done.22 = bf16[2,4,32,768]{3,2,1,0:T(8,128)(2,1)S(1)} collective-permute-done((bf16[2,4,32,768]{3,2,1,0:T(8,128)(2,1)S(1)}, bf16[2,4,32,768]{3,2,1,0:T(8,128)(2,1)S(1)}, u32[]{:S(2)}, u32[]{:S(2)}) %collective-permute-start.22) | collective-permute-done | bytes 393248 | tf_op jit(solution)/shard_map/ppermute | solution.py:30
  118.1 4.8 %collective-permute-done.23 = bf16[2,4,32,768]{3,2,1,0:T(8,128)(2,1)S(1)} collective-permute-done((bf16[2,4,32,768]{3,2,1,0:T(8,128)(2,1)S(1)}, bf16[2,4,32,768]{3,2,1,0:T(8,128)(2,1)S(1)}, u32[]{:S(2)}, u32[]{:S(2)}) %collective-permute-start.23) | collective-permute-done | bytes 393248 | tf_op jit(solution)/shard_map/ppermute | solution.py:30
  122.9 3.1 %collective-permute-done.24 = bf16[2,4,32,768]{3,2,1,0:T(8,128)(2,1)S(1)} collective-permute-done((bf16[2,4,32,768]{3,2,1,0:T(8,128)(2,1)S(1)}, bf16[2,4,32,768]{3,2,1,0:T(8,128)(2,1)S(1)}, u32[]{:S(2)}, u32[]{:S(2)}) %collective-permute-start.24) | collective-permute-done | bytes 393248 | tf_op jit(solution)/shard_map/ppermute | solution.py:30
  126.2 3.1 %collective-permute-done.27 = bf16[2,4,32,768]{3,2,1,0:T(8,128)(2,1)S(1)} collective-permute-done((bf16[2,4,32,768]{3,2,1,0:T(8,128)(2,1)S(1)}, bf16[2,4,32,768]{3,2,1,0:T(8,128)(2,1)S(1)}, u32[]{:S(2)}, u32[]{:S(2)}) %collective-permute-start.27) | collective-permute-done | bytes 393248 | tf_op jit(solution)/shard_map/ppermute | solution.py:25
  129.7 1.7 %collective-permute-start.29 = (bf16[2,32,768]{2,1,0:T(8,128)(2,1)S(1)}, bf16[2,32,768]{2,1,0:T(8,128)(2,1)S(1)}, u32[]{:S(2)}, u32[]{:S(2)}) collective-permute-start(bf16[2,32,768]{2,1,0:T(8,128)(2,1)S(1)} %get-tuple-element.52), channel_id=1, source_target_pairs={{0,24},{8,0},{16,8},{24,16},{32,56},{40,32},{48,40},{56,48},{64,88... | collective-permute-start | bytes 294920 | tf_op jit(solution)/shard_map/ppermute | solution.py:25
  131.8 1.7 %collective-permute-start.31 = (bf16[2,32,768]{2,1,0:T(8,128)(2,1)S(1)}, bf16[2,32,768]{2,1,0:T(8,128)(2,1)S(1)}, u32[]{:S(2)}, u32[]{:S(2)}) collective-permute-start(bf16[2,32,768]{2,1,0:T(8,128)(2,1)S(1)} %get-tuple-element.55), channel_id=1, source_target_pairs={{0,4},{1,5},{2,6},{3,7},{4,0},{5,1},{6,2},{7,3},{8,12},{9,13},{10,... | collective-permute-start | bytes 294920 | tf_op jit(solution)/shard_map/ppermute | solution.py:30
  133.5 0.7 collective-permute-start.32
  134.2 1.6 %collective-permute-done.28 = bf16[2,32,768]{2,1,0:T(8,128)(2,1)S(1)} collective-permute-done((bf16[2,32,768]{2,1,0:T(8,128)(2,1)S(1)}, bf16[2,32,768]{2,1,0:T(8,128)(2,1)S(1)}, u32[]{:S(2)}, u32[]{:S(2)}) %collective-permute-start.28) | collective-permute-done | bytes 98336 | tf_op jit(solution)/shard_map/ppermute | solution.py:25
  136.1 1.2 collective-permute-done.30
  137.3 1.3 collective-permute-done.31
  138.6 3.0 %collective-permute-done.33 = bf16[2,32,768]{2,1,0:T(8,128)(2,1)S(1)} collective-permute-done((bf16[2,32,768]{2,1,0:T(8,128)(2,1)S(1)}, bf16[2,32,768]{2,1,0:T(8,128)(2,1)S(1)}, u32[]{:S(2)}, u32[]{:S(2)}) %collective-permute-start.33) | collective-permute-done | bytes 98336 | tf_op jit(solution)/shard_map/ppermute | solution.py:30
  141.7 13.1 %all_to_all.11 = bf16[8,16,768]{2,1,0:T(8,128)(2,1)S(1)} all-to-all(bf16[8,16,768]{2,1,0:T(8,128)(2,1)S(1)} %bitcast.121), channel_id=1, replica_groups={{0,32,64,96,128,160,192,224},{8,40,72,104,136,168,200,232},{16,48,80,11..., dimensions={0} | all-to-all | bytes 393216 | tf_op jit(solution)/shard_map/all_to_all | solution.py:20
  154.9 0.8 fusion.3
  155.7 0.8 fusion.4
  (78 shorter events, 3.4 us)
Async XLA Ops:
  0.6 2.1 %copy-start = (bf16[16,768]{1,0:T(8,128)(2,1)S(1)}, bf16[16,768]{1,0:T(8,128)(2,1)}, u32[]{:S(2)}) copy-start(bf16[16,768]{1,0:T(8,128)(2,1)} %param.7) | copy-start | bytes 73732
  22.7 10.1 %collective-permute-start.1 = (bf16[2,32,768]{2,1,0:T(8,128)(2,1)S(1)}, bf16[2,32,768]{2,1,0:T(8,128)(2,1)S(1)}, u32[]{:S(2)}, u32[]{:S(2)}) collective-permute-start(bf16[2,32,768]{2,1,0:T(8,128)(2,1)S(1)} %bitcast.122), channel_id=1, source_target_pairs={{0,16},{8,24},{16,0},{24,8},{32,48},{40,56},{48,32},{56,40},{64,80... | collective-permute-start | bytes 294920 | tf_op jit(solution)/shard_map/ppermute | solution.py:25
  26.0 6.8 %collective-permute-start = (bf16[2,32,768]{2,1,0:T(8,128)(2,1)S(1)}, bf16[2,32,768]{2,1,0:T(8,128)(2,1)S(1)}, u32[]{:S(2)}, u32[]{:S(2)}) collective-permute-start(bf16[2,32,768]{2,1,0:T(8,128)(2,1)S(1)} %bitcast.123), channel_id=1, source_target_pairs={{0,8},{8,16},{16,24},{24,0},{32,40},{40,48},{48,56},{56,32},{64,72... | collective-permute-start | bytes 294920 | tf_op jit(solution)/shard_map/ppermute | solution.py:25
  26.7 6.2 %collective-permute-start.2 = (bf16[2,32,768]{2,1,0:T(8,128)(2,1)S(1)}, bf16[2,32,768]{2,1,0:T(8,128)(2,1)S(1)}, u32[]{:S(2)}, u32[]{:S(2)}) collective-permute-start(bf16[2,32,768]{2,1,0:T(8,128)(2,1)S(1)} %bitcast.124), channel_id=1, source_target_pairs={{0,24},{8,0},{16,8},{24,16},{32,56},{40,32},{48,40},{56,48},{64,88... | collective-permute-start | bytes 294920 | tf_op jit(solution)/shard_map/ppermute | solution.py:25
  29.2 6.2 %collective-permute-start.4 = (bf16[2,32,768]{2,1,0:T(8,128)(2,1)S(1)}, bf16[2,32,768]{2,1,0:T(8,128)(2,1)S(1)}, u32[]{:S(2)}, u32[]{:S(2)}) collective-permute-start(bf16[2,32,768]{2,1,0:T(8,128)(2,1)S(1)} %bitcast.126), channel_id=1, source_target_pairs={{0,4},{1,5},{2,6},{3,7},{4,0},{5,1},{6,2},{7,3},{8,12},{9,13},{10,... | collective-permute-start | bytes 294920 | tf_op jit(solution)/shard_map/ppermute | solution.py:30
  30.7 4.7 %collective-permute-start.3 = (bf16[2,32,768]{2,1,0:T(8,128)(2,1)S(1)}, bf16[2,32,768]{2,1,0:T(8,128)(2,1)S(1)}, u32[]{:S(2)}, u32[]{:S(2)}) collective-permute-start(bf16[2,32,768]{2,1,0:T(8,128)(2,1)S(1)} %bitcast.127), channel_id=1, source_target_pairs={{0,2},{1,3},{2,4},{3,5},{4,6},{5,7},{6,0},{7,1},{8,10},{9,11},{10,... | collective-permute-start | bytes 294920 | tf_op jit(solution)/shard_map/ppermute | solution.py:30
  32.8 6.6 %collective-permute-start.5 = (bf16[2,32,768]{2,1,0:T(8,128)(2,1)S(1)}, bf16[2,32,768]{2,1,0:T(8,128)(2,1)S(1)}, u32[]{:S(2)}, u32[]{:S(2)}) collective-permute-start(bf16[2,32,768]{2,1,0:T(8,128)(2,1)S(1)} %bitcast.128), channel_id=1, source_target_pairs={{0,6},{1,7},{2,0},{3,1},{4,2},{5,3},{6,4},{7,5},{8,14},{9,15},{10,... | collective-permute-start | bytes 294920 | tf_op jit(solution)/shard_map/ppermute | solution.py:30
  39.5 16.0 %collective-permute-start.11 = (bf16[2,4,32,768]{3,2,1,0:T(8,128)(2,1)S(1)}, bf16[2,4,32,768]{3,2,1,0:T(8,128)(2,1)S(1)}, u32[]{:S(2)}, u32[]{:S(2)}) collective-permute-start(bf16[2,4,32,768]{3,2,1,0:T(8,128)(2,1)S(1)} %pad_maximum_fusion.refs_0_), channel_id=1, source_target_pairs={{0,6},{1,7},{2,0},{3,1},{4,2},{5,3},{6,4},{7,5},{8,14},{9,15},{10,... | collective-permute-start | bytes 1179656 | tf_op jit(solution)/shard_map/ppermute | solution.py:30
  39.6 15.9 %collective-permute-start.9 = (bf16[2,4,32,768]{3,2,1,0:T(8,128)(2,1)S(1)}, bf16[2,4,32,768]{3,2,1,0:T(8,128)(2,1)S(1)}, u32[]{:S(2)}, u32[]{:S(2)}) collective-permute-start(bf16[2,4,32,768]{3,2,1,0:T(8,128)(2,1)S(1)} %pad_maximum_fusion.refs_0_), channel_id=1, source_target_pairs={{0,4},{1,5},{2,6},{3,7},{4,0},{5,1},{6,2},{7,3},{8,12},{9,13},{10,... | collective-permute-start | bytes 1179656 | tf_op jit(solution)/shard_map/ppermute | solution.py:30
  40.7 15.7 %collective-permute-start.7 = (bf16[2,4,32,768]{3,2,1,0:T(8,128)(2,1)S(1)}, bf16[2,4,32,768]{3,2,1,0:T(8,128)(2,1)S(1)}, u32[]{:S(2)}, u32[]{:S(2)}) collective-permute-start(bf16[2,4,32,768]{3,2,1,0:T(8,128)(2,1)S(1)} %pad_maximum_fusion.refs_0_), channel_id=1, source_target_pairs={{0,2},{1,3},{2,4},{3,5},{4,6},{5,7},{6,0},{7,1},{8,10},{9,11},{10,... | collective-permute-start | bytes 1179656 | tf_op jit(solution)/shard_map/ppermute | solution.py:30
  42.8 13.6 %collective-permute-start.6 = (bf16[2,4,32,768]{3,2,1,0:T(8,128)(2,1)S(1)}, bf16[2,4,32,768]{3,2,1,0:T(8,128)(2,1)S(1)}, u32[]{:S(2)}, u32[]{:S(2)}) collective-permute-start(bf16[2,4,32,768]{3,2,1,0:T(8,128)(2,1)S(1)} %pad_maximum_fusion.refs_0_), channel_id=1, source_target_pairs={{0,1},{1,0},{2,3},{3,2},{4,5},{5,4},{6,7},{7,6},{8,9},{9,8},{10,11... | collective-permute-start | bytes 1179656 | tf_op jit(solution)/shard_map/ppermute | solution.py:34
  42.8 14.1 %collective-permute-start.18 = (bf16[2,4,32,768]{3,2,1,0:T(8,128)(2,1)S(1)}, bf16[2,4,32,768]{3,2,1,0:T(8,128)(2,1)S(1)}, u32[]{:S(2)}, u32[]{:S(2)}) collective-permute-start(bf16[2,4,32,768]{3,2,1,0:T(8,128)(2,1)S(1)} %pad_maximum_fusion.1.refs_4_), channel_id=1, source_target_pairs={{0,24},{8,0},{16,8},{24,16},{32,56},{40,32},{48,40},{56,48},{64,88... | collective-permute-start | bytes 1179656 | tf_op jit(solution)/shard_map/ppermute | solution.py:25
  55.5 9.5 %collective-permute-start.16 = (bf16[2,4,32,768]{3,2,1,0:T(8,128)(2,1)S(1)}, bf16[2,4,32,768]{3,2,1,0:T(8,128)(2,1)}, u32[]{:S(2)}, u32[]{:S(2)}) collective-permute-start(bf16[2,4,32,768]{3,2,1,0:T(8,128)(2,1)S(1)} %pad_maximum_fusion.1.refs_4_), channel_id=1, source_target_pairs={{0,16},{8,24},{16,0},{24,8},{32,48},{40,56},{48,32},{56,40},{64,80... | collective-permute-start | bytes 1179656 | tf_op jit(solution)/shard_map/ppermute | solution.py:25
  55.5 13.3 %collective-permute-start.14 = (bf16[2,4,32,768]{3,2,1,0:T(8,128)(2,1)S(1)}, bf16[2,4,32,768]{3,2,1,0:T(8,128)(2,1)}, u32[]{:S(2)}, u32[]{:S(2)}) collective-permute-start(bf16[2,4,32,768]{3,2,1,0:T(8,128)(2,1)S(1)} %pad_maximum_fusion.1.refs_4_), channel_id=1, source_target_pairs={{0,8},{8,16},{16,24},{24,0},{32,40},{40,48},{48,56},{56,32},{64,72... | collective-permute-start | bytes 1179656 | tf_op jit(solution)/shard_map/ppermute | solution.py:25
  56.4 12.4 %collective-permute-start.13 = (bf16[2,4,32,768]{3,2,1,0:T(8,128)(2,1)S(1)}, bf16[2,4,32,768]{3,2,1,0:T(8,128)(2,1)S(1)}, u32[]{:S(2)}, u32[]{:S(2)}) collective-permute-start(bf16[2,4,32,768]{3,2,1,0:T(8,128)(2,1)S(1)} %pad_maximum_fusion.1.refs_4_), channel_id=1, source_target_pairs={{0,1},{1,0},{2,3},{3,2},{4,5},{5,4},{6,7},{7,6},{8,9},{9,8},{10,11... | collective-permute-start | bytes 1179656 | tf_op jit(solution)/shard_map/ppermute | solution.py:34
  56.4 12.9 %collective-permute-start.12 = (bf16[2,4,32,768]{3,2,1,0:T(8,128)(2,1)S(1)}, bf16[2,4,32,768]{3,2,1,0:T(8,128)(2,1)S(1)}, u32[]{:S(2)}, u32[]{:S(2)}) collective-permute-start(bf16[2,4,32,768]{3,2,1,0:T(8,128)(2,1)S(1)} %collective-permute-done.11.refs_3_), channel_id=1, source_target_pairs={{0,1},{1,0},{2,3},{3,2},{4,5},{5,4},{6,7},{7,6},{8,9},{9,8},{10,11... | collective-permute-start | bytes 1179656 | tf_op jit(solution)/shard_map/ppermute | solution.py:34
  56.9 25.4 %collective-permute-start.10 = (bf16[2,4,32,768]{3,2,1,0:T(8,128)(2,1)S(1)}, bf16[2,4,32,768]{3,2,1,0:T(8,128)(2,1)}, u32[]{:S(2)}, u32[]{:S(2)}) collective-permute-start(bf16[2,4,32,768]{3,2,1,0:T(8,128)(2,1)S(1)} %collective-permute-done.9.refs_2_), channel_id=1, source_target_pairs={{0,1},{1,0},{2,3},{3,2},{4,5},{5,4},{6,7},{7,6},{8,9},{9,8},{10,11... | collective-permute-start | bytes 1179656 | tf_op jit(solution)/shard_map/ppermute | solution.py:34
  65.0 17.3 %collective-permute-start.8 = (bf16[2,4,32,768]{3,2,1,0:T(8,128)(2,1)S(1)}, bf16[2,4,32,768]{3,2,1,0:T(8,128)(2,1)}, u32[]{:S(2)}, u32[]{:S(2)}) collective-permute-start(bf16[2,4,32,768]{3,2,1,0:T(8,128)(2,1)S(1)} %collective-permute-done.7.refs_1_), channel_id=1, source_target_pairs={{0,1},{1,0},{2,3},{3,2},{4,5},{5,4},{6,7},{7,6},{8,9},{9,8},{10,11... | collective-permute-start | bytes 1179656 | tf_op jit(solution)/shard_map/ppermute | solution.py:34
  68.8 13.5 %collective-permute-start.19 = (bf16[2,4,32,768]{3,2,1,0:T(8,128)(2,1)S(1)}, bf16[2,4,32,768]{3,2,1,0:T(8,128)(2,1)}, u32[]{:S(2)}, u32[]{:S(2)}) collective-permute-start(bf16[2,4,32,768]{3,2,1,0:T(8,128)(2,1)S(1)} %collective-permute-done.18.refs_7_), channel_id=1, source_target_pairs={{0,1},{1,0},{2,3},{3,2},{4,5},{5,4},{6,7},{7,6},{8,9},{9,8},{10,11... | collective-permute-start | bytes 1179656 | tf_op jit(solution)/shard_map/ppermute | solution.py:34
  68.8 13.5 %collective-permute-start.17 = (bf16[2,4,32,768]{3,2,1,0:T(8,128)(2,1)}, bf16[2,4,32,768]{3,2,1,0:T(8,128)(2,1)}, u32[]{:S(2)}, u32[]{:S(2)}) collective-permute-start(bf16[2,4,32,768]{3,2,1,0:T(8,128)(2,1)} %collective-permute-done.16.refs_6_), channel_id=1, source_target_pairs={{0,1},{1,0},{2,3},{3,2},{4,5},{5,4},{6,7},{7,6},{8,9},{9,8},{10,11... | collective-permute-start | bytes 1179656 | tf_op jit(solution)/shard_map/ppermute | solution.py:34
  69.3 0.8 copy-start.7
  70.1 12.2 %collective-permute-start.15 = (bf16[2,4,32,768]{3,2,1,0:T(8,128)(2,1)}, bf16[2,4,32,768]{3,2,1,0:T(8,128)(2,1)}, u32[]{:S(2)}, u32[]{:S(2)}) collective-permute-start(bf16[2,4,32,768]{3,2,1,0:T(8,128)(2,1)} %collective-permute-done.14.refs_5_), channel_id=1, source_target_pairs={{0,1},{1,0},{2,3},{3,2},{4,5},{5,4},{6,7},{7,6},{8,9},{9,8},{10,11... | collective-permute-start | bytes 1179656 | tf_op jit(solution)/shard_map/ppermute | solution.py:34
  70.1 2.2 %copy-start.1 = (bf16[1,6144,352]{1,2,0:T(8,128)(2,1)S(1)}, bf16[1,6144,352]{1,2,0:T(8,128)(2,1)}, u32[]{:S(2)}) copy-start(bf16[1,6144,352]{1,2,0:T(8,128)(2,1)} %param.11) | copy-start | bytes 12976132
  72.4 2.2 %copy-start.3 = (bf16[1,6144,352]{1,2,0:T(8,128)(2,1)S(1)}, bf16[1,6144,352]{1,2,0:T(8,128)(2,1)}, u32[]{:S(2)}) copy-start(bf16[1,6144,352]{1,2,0:T(8,128)(2,1)} %param.12) | copy-start | bytes 12976132
  74.6 2.2 %copy-start.5 = (bf16[1,352,6144]{2,1,0:T(8,128)(2,1)S(1)}, bf16[1,352,6144]{2,1,0:T(8,128)(2,1)}, u32[]{:S(2)}) copy-start(bf16[1,352,6144]{2,1,0:T(8,128)(2,1)} %param.13) | copy-start | bytes 12976132
  76.8 5.6 %copy-start.8 = (bf16[2,4,32,768]{3,2,1,0:T(8,128)(2,1)S(1)}, bf16[2,4,32,768]{3,2,1,0:T(8,128)(2,1)}, u32[]{:S(2)}) copy-start(bf16[2,4,32,768]{3,2,1,0:T(8,128)(2,1)} %copy-done.7) | copy-start | bytes 1179652
  76.8 22.0 %slice-start = ((s8[4325376]{0:T(1024)(128)(4,1)}), s8[4194304]{0:T(1024)(128)(4,1)S(1)}, s32[]{:S(2)}) async-start(s8[4325376]{0:T(1024)(128)(4,1)} %bitcast.111), calls=%async_computation.2 | async-start | bytes 8388608
  82.4 2.2 %copy-start.2 = (bf16[1,6144,352]{1,2,0:T(8,128)(2,1)S(1)}, bf16[1,6144,352]{1,2,0:T(8,128)(2,1)}, u32[]{:S(2)}) copy-start(bf16[1,6144,352]{1,2,0:T(8,128)(2,1)} %param.11) | copy-start | bytes 12976132
  84.6 2.2 %copy-start.4 = (bf16[1,6144,352]{1,2,0:T(8,128)(2,1)S(1)}, bf16[1,6144,352]{1,2,0:T(8,128)(2,1)}, u32[]{:S(2)}) copy-start(bf16[1,6144,352]{1,2,0:T(8,128)(2,1)} %param.12) | copy-start | bytes 12976132
  86.8 2.2 %copy-start.6 = (bf16[1,352,6144]{2,1,0:T(8,128)(2,1)S(1)}, bf16[1,352,6144]{2,1,0:T(8,128)(2,1)}, u32[]{:S(2)}) copy-start(bf16[1,352,6144]{2,1,0:T(8,128)(2,1)} %param.13) | copy-start | bytes 12976132
  89.1 9.7 %slice-start.1 = ((s8[4325376]{0:T(1024)(128)(4,1)}), s8[131072]{0:T(1024)(128)(4,1)S(1)}, s32[]{:S(2)}) async-start(s8[4325376]{0:T(1024)(128)(4,1)} %bitcast.111), calls=%async_computation.3 | async-start | bytes 262144
  98.1 5.1 %collective-permute-start.20 = (bf16[4,2,4,32,768]{4,3,2,1,0:T(8,128)(2,1)S(1)}, bf16[4,2,4,32,768]{4,3,2,1,0:T(8,128)(2,1)S(1)}, u32[]{:S(2)}, u32[]{:S(2)}) collective-permute-start(bf16[4,2,4,32,768]{4,3,2,1,0:T(8,128)(2,1)S(1)} %get-tuple-element.39), channel_id=1, source_target_pairs={{0,1},{1,0},{2,3},{3,2},{4,5},{5,4},{6,7},{7,6},{8,9},{9,8},{10,11... | collective-permute-start | bytes 4718600 | tf_op jit(solution)/shard_map/ppermute | solution.py:34
  98.7 5.3 %collective-permute-start.21 = (bf16[4,2,4,32,768]{4,3,2,1,0:T(8,128)(2,1)S(1)}, bf16[4,2,4,32,768]{4,3,2,1,0:T(8,128)(2,1)S(1)}, u32[]{:S(2)}, u32[]{:S(2)}) collective-permute-start(bf16[4,2,4,32,768]{4,3,2,1,0:T(8,128)(2,1)S(1)} %get-tuple-element.41), channel_id=1, source_target_pairs={{0,1},{1,0},{2,3},{3,2},{4,5},{5,4},{6,7},{7,6},{8,9},{9,8},{10,11... | collective-permute-start | bytes 4718600 | tf_op jit(solution)/shard_map/ppermute | solution.py:34
  104.5 13.6 %collective-permute-start.22 = (bf16[2,4,32,768]{3,2,1,0:T(8,128)(2,1)S(1)}, bf16[2,4,32,768]{3,2,1,0:T(8,128)(2,1)S(1)}, u32[]{:S(2)}, u32[]{:S(2)}) collective-permute-start(bf16[2,4,32,768]{3,2,1,0:T(8,128)(2,1)S(1)} %get-tuple-element.43), channel_id=1, source_target_pairs={{0,4},{1,5},{2,6},{3,7},{4,0},{5,1},{6,2},{7,3},{8,12},{9,13},{10,... | collective-permute-start | bytes 1179656 | tf_op jit(solution)/shard_map/ppermute | solution.py:30
  104.6 18.3 %collective-permute-start.23 = (bf16[2,4,32,768]{3,2,1,0:T(8,128)(2,1)S(1)}, bf16[2,4,32,768]{3,2,1,0:T(8,128)(2,1)S(1)}, u32[]{:S(2)}, u32[]{:S(2)}) collective-permute-start(bf16[2,4,32,768]{3,2,1,0:T(8,128)(2,1)S(1)} %get-tuple-element.44), channel_id=1, source_target_pairs={{0,2},{1,3},{2,4},{3,5},{4,6},{5,7},{6,0},{7,1},{8,10},{9,11},{10,... | collective-permute-start | bytes 1179656 | tf_op jit(solution)/shard_map/ppermute | solution.py:30
  104.7 21.2 %collective-permute-start.24 = (bf16[2,4,32,768]{3,2,1,0:T(8,128)(2,1)S(1)}, bf16[2,4,32,768]{3,2,1,0:T(8,128)(2,1)S(1)}, u32[]{:S(2)}, u32[]{:S(2)}) collective-permute-start(bf16[2,4,32,768]{3,2,1,0:T(8,128)(2,1)S(1)} %get-tuple-element.45), channel_id=1, source_target_pairs={{0,6},{1,7},{2,0},{3,1},{4,2},{5,3},{6,4},{7,5},{8,14},{9,15},{10,... | collective-permute-start | bytes 1179656 | tf_op jit(solution)/shard_map/ppermute | solution.py:30
  106.8 19.4 %collective-permute-start.25 = (bf16[2,4,32,768]{3,2,1,0:T(8,128)(2,1)S(1)}, bf16[2,4,32,768]{3,2,1,0:T(8,128)(2,1)S(1)}, u32[]{:S(2)}, u32[]{:S(2)}) collective-permute-start(bf16[2,4,32,768]{3,2,1,0:T(8,128)(2,1)S(1)} %get-tuple-element.47), channel_id=1, source_target_pairs={{0,16},{8,24},{16,0},{24,8},{32,48},{40,56},{48,32},{56,40},{64,80... | collective-permute-start | bytes 1179656 | tf_op jit(solution)/shard_map/ppermute | solution.py:25
  107.1 19.2 %collective-permute-start.26 = (bf16[2,4,32,768]{3,2,1,0:T(8,128)(2,1)S(1)}, bf16[2,4,32,768]{3,2,1,0:T(8,128)(2,1)S(1)}, u32[]{:S(2)}, u32[]{:S(2)}) collective-permute-start(bf16[2,4,32,768]{3,2,1,0:T(8,128)(2,1)S(1)} %get-tuple-element.48), channel_id=1, source_target_pairs={{0,24},{8,0},{16,8},{24,16},{32,56},{40,32},{48,40},{56,48},{64,88... | collective-permute-start | bytes 1179656 | tf_op jit(solution)/shard_map/ppermute | solution.py:25
  118.1 11.2 %collective-permute-start.27 = (bf16[2,4,32,768]{3,2,1,0:T(8,128)(2,1)S(1)}, bf16[2,4,32,768]{3,2,1,0:T(8,128)(2,1)S(1)}, u32[]{:S(2)}, u32[]{:S(2)}) collective-permute-start(bf16[2,4,32,768]{3,2,1,0:T(8,128)(2,1)S(1)} %get-tuple-element.49), channel_id=1, source_target_pairs={{0,8},{8,16},{16,24},{24,0},{32,40},{40,48},{48,56},{56,32},{64,72... | collective-permute-start | bytes 1179656 | tf_op jit(solution)/shard_map/ppermute | solution.py:25
  129.6 6.2 %collective-permute-start.28 = (bf16[2,32,768]{2,1,0:T(8,128)(2,1)S(1)}, bf16[2,32,768]{2,1,0:T(8,128)(2,1)S(1)}, u32[]{:S(2)}, u32[]{:S(2)}) collective-permute-start(bf16[2,32,768]{2,1,0:T(8,128)(2,1)S(1)} %get-tuple-element.51), channel_id=1, source_target_pairs={{0,16},{8,24},{16,0},{24,8},{32,48},{40,56},{48,32},{56,40},{64,80... | collective-permute-start | bytes 294920 | tf_op jit(solution)/shard_map/ppermute | solution.py:25
  129.7 6.4 %collective-permute-start.29 = (bf16[2,32,768]{2,1,0:T(8,128)(2,1)S(1)}, bf16[2,32,768]{2,1,0:T(8,128)(2,1)S(1)}, u32[]{:S(2)}, u32[]{:S(2)}) collective-permute-start(bf16[2,32,768]{2,1,0:T(8,128)(2,1)S(1)} %get-tuple-element.52), channel_id=1, source_target_pairs={{0,24},{8,0},{16,8},{24,16},{32,56},{40,32},{48,40},{56,48},{64,88... | collective-permute-start | bytes 294920 | tf_op jit(solution)/shard_map/ppermute | solution.py:25
  131.4 5.8 %collective-permute-start.30 = (bf16[2,32,768]{2,1,0:T(8,128)(2,1)S(1)}, bf16[2,32,768]{2,1,0:T(8,128)(2,1)S(1)}, u32[]{:S(2)}, u32[]{:S(2)}) collective-permute-start(bf16[2,32,768]{2,1,0:T(8,128)(2,1)S(1)} %get-tuple-element.53), channel_id=1, source_target_pairs={{0,8},{8,16},{16,24},{24,0},{32,40},{40,48},{48,56},{56,32},{64,72... | collective-permute-start | bytes 294920 | tf_op jit(solution)/shard_map/ppermute | solution.py:25
  131.8 6.8 %collective-permute-start.31 = (bf16[2,32,768]{2,1,0:T(8,128)(2,1)S(1)}, bf16[2,32,768]{2,1,0:T(8,128)(2,1)S(1)}, u32[]{:S(2)}, u32[]{:S(2)}) collective-permute-start(bf16[2,32,768]{2,1,0:T(8,128)(2,1)S(1)} %get-tuple-element.55), channel_id=1, source_target_pairs={{0,4},{1,5},{2,6},{3,7},{4,0},{5,1},{6,2},{7,3},{8,12},{9,13},{10,... | collective-permute-start | bytes 294920 | tf_op jit(solution)/shard_map/ppermute | solution.py:30
  133.5 5.2 %collective-permute-start.32 = (bf16[2,32,768]{2,1,0:T(8,128)(2,1)S(1)}, bf16[2,32,768]{2,1,0:T(8,128)(2,1)S(1)}, u32[]{:S(2)}, u32[]{:S(2)}) collective-permute-start(bf16[2,32,768]{2,1,0:T(8,128)(2,1)S(1)} %get-tuple-element.56), channel_id=1, source_target_pairs={{0,2},{1,3},{2,4},{3,5},{4,6},{5,7},{6,0},{7,1},{8,10},{9,11},{10,... | collective-permute-start | bytes 294920 | tf_op jit(solution)/shard_map/ppermute | solution.py:30
  135.8 5.8 %collective-permute-start.33 = (bf16[2,32,768]{2,1,0:T(8,128)(2,1)S(1)}, bf16[2,32,768]{2,1,0:T(8,128)(2,1)S(1)}, u32[]{:S(2)}, u32[]{:S(2)}) collective-permute-start(bf16[2,32,768]{2,1,0:T(8,128)(2,1)S(1)} %get-tuple-element.57), channel_id=1, source_target_pairs={{0,6},{1,7},{2,0},{3,1},{4,2},{5,3},{6,4},{7,5},{8,14},{9,15},{10,... | collective-permute-start | bytes 294920 | tf_op jit(solution)/shard_map/ppermute | solution.py:30
where the time goes:
time: 157 us
  waiting for transfers between devices  59.2 us (38%)
  blocking collectives  31.9 us (20%)
  starting transfers between devices  24.7 us (16%)
  Pallas kernels  18.9 us (12%)
  local copies, waits for them, and re-layouts  14.5 us (9%)
  other arithmetic  3.63 us (2%)
  matrix products  2.83 us (2%)
    ppermute x12, waiting for transfers between devices, to_x(): return lax.ppermute(v, 'cuts', perm)  41.2 us
    all_to_all x2, blocking collectives, swap_z(): return lax.all_to_all(v, 'dp', 0, 0, axis_index_groups=groups, tiled=True)  31.9 us
    pallas_call x3, Pallas kernels, call(): pl.pallas_call(body, name=name, out_shape=out, in_specs=[pl.BlockSpec(mem...  18.9 us
    ppermute x12, waiting for transfers between devices, to_y(): return lax.ppermute(v, 'dp', perm)  17.8 us
    unnamed x22, local copies, waits for them, and re-layouts  14.1 us
    ppermute x12, starting transfers between devices, to_x(): return lax.ppermute(v, 'cuts', perm)  11.8 us
    ppermute x12, starting transfers between devices, to_y(): return lax.ppermute(v, 'dp', perm)  11.1 us
  transfers between devices with their start and end apart: 34, of which 14 were waited for; matrix products, arithmetic and copies ran while one was open for 1% of the time, Pallas kernels for 6%

commit v1 on v0

v1 whole, which is shorter than its diff:
```python
import jax
import jax.numpy as jnp
from jax import lax
from jax.experimental import pallas as pl
from jax.experimental.pallas import tpu as pltpu
from jax.sharding import PartitionSpec as P

E = 8
NY = 4
NX = 4
CAP = 8
BF = jnp.bfloat16
F32 = jnp.float32
NT = (((1,), (1,)), ((), ()))
VMEM_LIMIT = {"own": 20, "other": 24, "last": 16}


def swap_z(v):
    groups = [[z * NY + y for z in range(E)] for y in range(NY)]
    return lax.all_to_all(v, "dp", 0, 0, axis_index_groups=groups, tiled=True)


def partner(i, q):
    if q == 1:
        return i ^ 1
    return (i + (1 if i % 2 else 3)) % 4 if q == 2 else i ^ 2


def to_y(v, q):
    perm = [(z * NY + y, z * NY + partner(y, q)) for z in range(E) for y in range(NY)]
    return lax.ppermute(v, "dp", perm)


def to_x(v, q):
    perm = [(x * 2 + c, partner(x, q) * 2 + c) for x in range(NX) for c in range(2)]
    return lax.ppermute(v, "cuts", perm)


def to_core(v):
    return lax.ppermute(v, "cuts", [(i, i ^ 1) for i in range(2 * NX)])


def slots_of(routing, gate_values):
    hit = routing[:, :, None] == jnp.arange(E, dtype=jnp.int32)
    chosen = jnp.any(hit, axis=1)
    gates = jnp.sum(jnp.where(hit, gate_values[:, :, None], 0.0), axis=1)
    rows = routing.shape[0]
    below = jnp.arange(rows)[:, None] > jnp.arange(rows)[None, :]
    position = jnp.sum(
        jnp.where(below[:, :, None] & chosen[None, :, :], 1, 0), axis=1
    )
    slot = position[:, :, None] == jnp.arange(CAP, dtype=jnp.int32)
    select = chosen[:, :, None] & slot
    weight = jnp.where(select, gates[:, :, None], 0.0)
    return select.reshape(rows, E * CAP), weight.reshape(rows, E * CAP)


def first_gather(a, b):
    a, b = a[:, None], b[:, None]
    for q in (1, 2):
        ga, gb = lax.optimization_barrier((to_y(a, q), to_x(b, q)))
        a = jnp.concatenate([a, ga], axis=1)
        b = jnp.concatenate([b, gb], axis=1)
    return a, b


def second_gather(a, b):
    a, b = lax.optimization_barrier((a, b))
    got = {}
    for q in (3, 1, 2):
        got[q] = to_x(a, q), to_y(b, q)
    got = lax.optimization_barrier(got)
    own = [a] + [got[q][0] for q in (1, 2, 3)] + [b] + [got[q][1] for q in (1, 2, 3)]
    own = list(lax.optimization_barrier(tuple(own)))
    return own, [to_core(v) for v in own]


def add(*parts):
    total = parts[0].astype(F32)
    for p in parts[1:]:
        total = total + p.astype(F32)
    return total.astype(BF)


def first_scatter(sa, sb):
    sa, sb = lax.optimization_barrier((sa, sb))
    got = {}
    for q in (3, 1, 2):
        got[q] = to_x(sa[q], q), to_y(sb[q], q)
    got = lax.optimization_barrier(got)
    ra = add(sa[0], *[got[q][0] for q in (1, 2, 3)])
    rb = add(sb[0], *[got[q][1] for q in (1, 2, 3)])
    return ra, rb


def second_scatter(a, b):
    for q in (2, 1):
        keep = a.shape[1] // 2
        a, b = lax.optimization_barrier((a, b))
        got = to_y(a[:, keep:], q), to_x(b[:, keep:], q)
        ga, gb = lax.optimization_barrier(got)
        a, b = add(a[:, :keep], ga), add(b[:, :keep], gb)
    return a[:, 0], b[:, 0]


def fetch_weights(cols, weights, buf, sem):
    hidden, width = weights[0].shape[0], buf.shape[-1]

    def copy(i, k, at):
        rows = pl.ds(i * hidden, hidden)
        return pltpu.make_async_copy(
            weights[i].at[:, pl.ds(at, width)], buf.at[k, rows], sem.at[k, i]
        )

    for k in range(NX):
        for i in range(3):
            copy(i, k, pl.multiple_of(cols[k] * width, 128)).start()

    def wait(k):
        for i in range(3):
            copy(i, k, 0).wait()

    return wait


def load_rows(pieces, rows):
    half = rows.shape[2] // 2
    step = half // NY
    for i in range(2):
        for k in range(NX):
            rows[k, i, :half] = pieces[k][i].reshape(half, -1)
            for j in range(NY):
                at = half + j * step
                rows[k, i, at : at + step] = pieces[NX + j][i, k]


def contract(wait, rows, buf, acc):
    two = acc.shape[0] // 3 * 2

    @pl.loop(0, NX)
    def _(k):
        wait(k)
        acc[:two] += lax.dot_general(
            buf[k, :two], rows[k, 0], NT, preferred_element_type=F32
        )
        acc[two:] += lax.dot_general(
            buf[k, two:], rows[k, 1], NT, preferred_element_type=F32
        )


def expand(wait, hidden, grads, buf, out_a, out_b):
    half = hidden.shape[0] // 2
    step = half // NY
    two = grads.shape[1]

    def put(k, i, value):
        out_a[k, i] = value[:half].reshape(NY, step, -1)
        for j in range(NY):
            out_b[j, i, k] = value[half + j * step : half + (j + 1) * step]

    @pl.loop(0, NX)
    def _(k):
        if wait is not None:
            wait(k)
        o = jnp.dot(hidden[...], buf[k, two:], preferred_element_type=F32)
        put(k, 0, o.astype(BF))
        o = jnp.dot(grads[...], buf[k, :two], preferred_element_type=F32)
        put(k, 1, o.astype(BF))


def own_kernel(cols, *refs):
    pieces, weights, (acc, rows, buf, sem) = refs[:8], refs[8:11], refs[11:]
    wait = fetch_weights(cols, weights, buf, sem)
    load_rows(pieces, rows)
    acc[...] = jnp.zeros_like(acc)
    contract(wait, rows, buf, acc)


def other_kernel(cols, *refs):
    pieces, weights, partial, rest = refs[:8], refs[8:11], refs[11], refs[12:]
    out_a, out_b, hidden, grads, rows, acc, buf, sem = rest
    wait = fetch_weights(cols, weights, buf, sem)
    load_rows(pieces, rows)
    acc[...] = partial[...]
    contract(wait, rows, buf, acc)
    one = acc.shape[0] // 3
    g, u, h = acc[:one], acc[one : 2 * one], acc[2 * one :]
    sigma = jax.nn.sigmoid(g)
    hidden[...] = (g * sigma * u).T.astype(BF)
    gate_grad = h * u * sigma * (1.0 + g * (1.0 - sigma))
    grads[...] = jnp.concatenate([gate_grad, h * g * sigma], axis=0).T.astype(BF)
    expand(None, hidden, grads, buf, out_a, out_b)


def last_kernel(cols, *refs):
    (hidden, grads), weights, (out_a, out_b, buf, sem) = refs[:2], refs[2:5], refs[5:]
    wait = fetch_weights(cols, weights, buf, sem)
    expand(wait, hidden, grads, buf, out_a, out_b)


def call(body, name, cols, arrays, weights, partial, out, scratch, products):
    hidden, width = weights[0].shape[0], weights[0].shape[1] // (2 * NX)
    rows = E * CAP * NY
    return pl.pallas_call(
        body,
        name=name,
        out_shape=out,
        in_specs=[pl.BlockSpec(memory_space=pltpu.SMEM)]
        + [pl.BlockSpec(memory_space=pltpu.VMEM)] * len(arrays)
        + [pl.BlockSpec(memory_space=pltpu.HBM)] * 3
        + [pl.BlockSpec(memory_space=pltpu.VMEM)] * len(partial),
        out_specs=[pl.BlockSpec(memory_space=pltpu.VMEM)] * len(out),
        scratch_shapes=scratch
        + [
            pltpu.VMEM((NX, 3 * hidden, width), BF),
            pltpu.SemaphoreType.DMA((NX, 3)),
        ],
        compiler_params=pltpu.CompilerParams(vmem_limit_bytes=VMEM_LIMIT[name] << 20),
        cost_estimate=pl.CostEstimate(
            flops=2 * products * rows * width * NX * hidden,
            bytes_accessed=7 << 20,
            transcendentals=0,
        ),
    )(cols, *arrays, *weights, *partial)


def on_device(tokens, out_grad, gate_values, routing, gate_weight, up_weight, down_weight):
    width = tokens.shape[1]
    cut = lax.axis_index("cuts")
    x, c = cut // 2, cut % 2
    wg = jnp.swapaxes(gate_weight[0], 0, 1)
    wu = jnp.swapaxes(up_weight[0], 0, 1)
    w2 = down_weight[0]
    hidden = w2.shape[0]
    own_cols = jnp.stack([x, x ^ 1, (x + 3 + 2 * (x % 2)) % NX, x ^ 2]) * 2 + c
    other_cols = own_cols ^ 1
    rows = NY * E * CAP

    select, weight = slots_of(routing, gate_values)
    pick = select.astype(BF).T
    send_x = jnp.dot(pick, tokens, preferred_element_type=F32).astype(BF)
    slot_gate = jnp.sum(weight, axis=0)
    send_dy = jnp.dot(pick, out_grad, preferred_element_type=F32)
    send_dy = (slot_gate[:, None] * send_dy).astype(BF)
    send = jnp.concatenate(
        [send_x.reshape(E, CAP, width), send_dy.reshape(E, CAP, width)], axis=1
    )
    got = swap_z(send).reshape(2, E // 2, 2, CAP, width)
    got = jnp.swapaxes(got, 1, 2).reshape(2, 2, -1, width)

    own, other = second_gather(*first_gather(got[0], got[1]))

    weights = [pltpu.with_memory_space_constraint(w, pltpu.HBM) for w in (wg, wu, w2)]
    pre = jax.ShapeDtypeStruct((3 * hidden, rows), F32)
    act = [
        jax.ShapeDtypeStruct((rows, hidden), BF),
        jax.ShapeDtypeStruct((rows, 2 * hidden), BF),
    ]
    pieces = [jax.ShapeDtypeStruct((4, 2, 4, rows // 8, width), BF)] * 2
    row_buf = [pltpu.VMEM((NX, 2, rows, width), BF)]
    acc_buf = [pltpu.VMEM(pre.shape, F32)]
    partial = call(own_kernel, "own", own_cols, own, weights, [], [pre], row_buf, 3)
    far_a, far_b, *act = call(
        other_kernel, "other", other_cols, other, weights, partial,
        pieces + act, row_buf + acc_buf, 6,
    )
    near_a, near_b = call(
        last_kernel, "last", own_cols, act, weights, [], pieces, [], 3
    )
    got_a, got_b = to_core(far_a), to_core(far_b)
    sa = [add(near_a[d], got_a[d]) for d in range(4)]
    sb = [add(near_b[d], got_b[d]) for d in range(4)]
    ta, tb = first_scatter(sa, sb)
    ra, rb = second_scatter(ta, tb)
    back = jnp.stack([ra, rb]).reshape(2, 2, E // 2, CAP, width)
    back = jnp.swapaxes(back, 1, 2).reshape(E, 2 * CAP, width)
    back = swap_z(back)
    back_y = back[:, :CAP].reshape(E * CAP, width)
    back_dx = back[:, CAP:].reshape(E * CAP, width)
    mixed = jnp.dot(weight, back_y.astype(F32), precision=lax.Precision.HIGHEST)
    grad = jnp.dot(select.astype(BF), back_dx, preferred_element_type=F32)
    return mixed.astype(BF), grad.astype(BF)


def solution(mesh):
    return jax.shard_map(
        on_device,
        mesh=mesh,
        in_specs=(
            P("dp", "cuts"),
            P("dp", "cuts"),
            P("dp", None),
            P("dp", None),
            P("dp", None, "cuts"),
            P("dp", None, "cuts"),
            P("dp", "cuts", None),
        ),
        out_specs=(P("dp", "cuts"), P("dp", "cuts")),
        check_vma=False,
    )
```

time: 157 us -> 136 us (0.87)
  waiting for transfers between devices: 59.2 us -> 45.3 us
  local copies, waits for them, and re-layouts: 14.5 us -> 2.59 us
  starting transfers between devices: 24.7 us -> 30.1 us
    unnamed x22 -> x14, local copies, waits for them, and re-layouts: 14.1 us -> 2.27 us
    ppermute x12 -> x10, waiting for transfers between devices: 17.8 us -> 9.27 us  [to_y(): return lax.ppermute(v, 'dp', perm)]
    ppermute x12 -> x10, waiting for transfers between devices: 41.2 us -> 34.8 us  [to_x(): return lax.ppermute(v, 'cuts', perm)]
    ppermute x12 -> x10, starting transfers between devices: 11.1 us -> 15.8 us  [to_y(): return lax.ppermute(v, 'dp', perm)]
    ppermute x12 -> x10, starting transfers between devices: 11.8 us -> 12.2 us  [to_x(): return lax.ppermute(v, 'cuts', perm)]
  transfers between devices with their start and end apart: 34 -> 30, of which waited for: 14 -> 17; matrix products, arithmetic and copies ran while one was open for 1% -> 1% of each run, Pallas kernels for 6% -> 7%
where the time goes in v1:
time: 136 us; the launch traced here: 135 us
  waiting for transfers between devices  45.3 us (33%)
  blocking collectives  31.2 us (23%)
  starting transfers between devices  30.1 us (22%)
  Pallas kernels  17.8 us (13%)
  other arithmetic  3.87 us (3%)
  matrix products  2.83 us (2%)
  local copies, waits for them, and re-layouts  2.59 us (2%)
    ppermute x10, waiting for transfers between devices, to_x(): return lax.ppermute(v, 'cuts', perm)  34.8 us
    all_to_all x2, blocking collectives, swap_z(): return lax.all_to_all(v, 'dp', 0, 0, axis_index_groups=groups, tiled=True)  31.2 us
    pallas_call x3, Pallas kernels, call(): pl.pallas_call(body, name=name, out_shape=out, in_specs=[pl.BlockSpec(mem...  17.8 us
    ppermute x10, starting transfers between devices, to_y(): return lax.ppermute(v, 'dp', perm)  15.8 us
    ppermute x10, starting transfers between devices, to_x(): return lax.ppermute(v, 'cuts', perm)  12.2 us
    ppermute x10, waiting for transfers between devices, to_y(): return lax.ppermute(v, 'dp', perm)  9.27 us
  transfers between devices with their start and end apart: 30, of which 17 were waited for; matrix products, arithmetic and copies ran while one was open for 1% of the time, Pallas kernels for 7%

profile of v1, /device:TPU:6, one launch (start us, length us, event | category | flops | bytes accessed | tf_op | source)
XLA Modules:
  0.0 134.7 jit_solution(3020831692042541201)
XLA Ops:
  0.7 0.7 fusion.36
  1.3 0.7 select_reduce_fusion.2
  2.1 0.4 select_reduce_fusion
  3.0 1.0 fusion.1
  3.9 18.7 %all_to_all.10 = bf16[8,16,768]{2,1,0:T(8,128)(2,1)S(1)} all-to-all(bf16[8,16,768]{2,1,0:T(8,128)(2,1)S(1)} %pad_maximum_fusion.2), channel_id=1, replica_groups={{0,32,64,96,128,160,192,224},{8,40,72,104,136,168,200,232},{16,48,80,11..., dimensions={0} | all-to-all | bytes 393216 | tf_op jit(solution)/shard_map/all_to_all | solution.py:20
  22.7 1.7 %collective-permute-start = (bf16[2,1,32,768]{3,2,1,0:T(8,128)(2,1)S(1)}, bf16[2,1,32,768]{3,2,1,0:T(8,128)(2,1)S(1)}, u32[]{:S(2)}, u32[]{:S(2)}) collective-permute-start(bf16[2,1,32,768]{3,2,1,0:T(8,128)(2,1)S(1)} %bitcast.79), channel_id=1, source_target_pairs={{0,8},{8,0},{16,24},{24,16},{32,40},{40,32},{48,56},{56,48},{64,72... | collective-permute-start | bytes 294920 | tf_op jit(solution)/shard_map/ppermute | solution.py:31
  24.4 0.8 collective-permute-start.1
  25.2 2.2 %collective-permute-done = bf16[2,1,32,768]{3,2,1,0:T(8,128)(2,1)S(1)} collective-permute-done((bf16[2,1,32,768]{3,2,1,0:T(8,128)(2,1)S(1)}, bf16[2,1,32,768]{3,2,1,0:T(8,128)(2,1)S(1)}, u32[]{:S(2)}, u32[]{:S(2)}) %collective-permute-start) | collective-permute-done | bytes 98336 | tf_op jit(solution)/shard_map/ppermute | solution.py:31
  27.4 1.6 %collective-permute-done.1 = bf16[2,1,32,768]{3,2,1,0:T(8,128)(2,1)S(1)} collective-permute-done((bf16[2,1,32,768]{3,2,1,0:T(8,128)(2,1)S(1)}, bf16[2,1,32,768]{3,2,1,0:T(8,128)(2,1)S(1)}, u32[]{:S(2)}, u32[]{:S(2)}) %collective-permute-start.1) | collective-permute-done | bytes 98336 | tf_op jit(solution)/shard_map/ppermute | solution.py:36
  29.1 0.6 collective-permute-start.3
  29.6 2.2 %collective-permute-start.2 = (bf16[2,2,32,768]{3,2,1,0:T(8,128)(2,1)S(1)}, bf16[2,2,32,768]{3,2,1,0:T(8,128)(2,1)S(1)}, u32[]{:S(2)}, u32[]{:S(2)}) collective-permute-start(bf16[2,2,32,768]{3,2,1,0:T(8,128)(2,1)S(1)} %pad_maximum_fusion.3), channel_id=1, source_target_pairs={{0,24},{8,16},{16,8},{24,0},{32,56},{40,48},{48,40},{56,32},{64,88... | collective-permute-start | bytes 589832 | tf_op jit(solution)/shard_map/ppermute | solution.py:31
  31.8 8.5 %collective-permute-done.3 = bf16[2,2,32,768]{3,2,1,0:T(8,128)(2,1)S(1)} collective-permute-done((bf16[2,2,32,768]{3,2,1,0:T(8,128)(2,1)S(1)}, bf16[2,2,32,768]{3,2,1,0:T(8,128)(2,1)S(1)}, u32[]{:S(2)}, u32[]{:S(2)}) %collective-permute-start.3) | collective-permute-done | bytes 196640 | tf_op jit(solution)/shard_map/ppermute | solution.py:36
  40.6 3.4 %collective-permute-start.4 = (bf16[2,4,32,768]{3,2,1,0:T(8,128)(2,1)S(1)}, bf16[2,4,32,768]{3,2,1,0:T(8,128)(2,1)S(1)}, u32[]{:S(2)}, u32[]{:S(2)}) collective-permute-start(bf16[2,4,32,768]{3,2,1,0:T(8,128)(2,1)S(1)} %get-tuple-element.62.refs_0_), channel_id=1, source_target_pairs={{0,2},{1,3},{2,0},{3,1},{4,6},{5,7},{6,4},{7,5},{8,10},{9,11},{10,... | collective-permute-start | bytes 1179656 | tf_op jit(solution)/shard_map/ppermute | solution.py:36
  43.9 3.1 %collective-permute-start.9 = (bf16[2,4,32,768]{3,2,1,0:T(8,128)(2,1)S(1)}, bf16[2,4,32,768]{3,2,1,0:T(8,128)(2,1)S(1)}, u32[]{:S(2)}, u32[]{:S(2)}) collective-permute-start(bf16[2,4,32,768]{3,2,1,0:T(8,128)(2,1)S(1)} %get-tuple-element.66.refs_4_), channel_id=1, source_target_pairs={{0,16},{8,24},{16,0},{24,8},{32,48},{40,56},{48,32},{56,40},{64,80... | collective-permute-start | bytes 1179656 | tf_op jit(solution)/shard_map/ppermute | solution.py:31
  47.3 2.6 %collective-permute-done.8.refs_3_ = bf16[2,4,32,768]{3,2,1,0:T(8,128)(2,1)S(1)} collective-permute-done((bf16[2,4,32,768]{3,2,1,0:T(8,128)(2,1)S(1)}, bf16[2,4,32,768]{3,2,1,0:T(8,128)(2,1)S(1)}, u32[]{:S(2)}, u32[]{:S(2)}) %collective-permute-start.8) | collective-permute-done | bytes 393248 | tf_op jit(solution)/shard_map/ppermute | solution.py:36
  49.8 0.6 collective-permute-start.5
  50.5 3.3 %collective-permute-done.6.refs_2_ = bf16[2,4,32,768]{3,2,1,0:T(8,128)(2,1)S(1)} collective-permute-done((bf16[2,4,32,768]{3,2,1,0:T(8,128)(2,1)S(1)}, bf16[2,4,32,768]{3,2,1,0:T(8,128)(2,1)S(1)}, u32[]{:S(2)}, u32[]{:S(2)}) %collective-permute-start.6) | collective-permute-done | bytes 393248 | tf_op jit(solution)/shard_map/ppermute | solution.py:36
  53.8 3.7 %collective-permute-done.7.refs_6_ = bf16[2,4,32,768]{3,2,1,0:T(8,128)(2,1)S(1)} collective-permute-done((bf16[2,4,32,768]{3,2,1,0:T(8,128)(2,1)S(1)}, bf16[2,4,32,768]{3,2,1,0:T(8,128)(2,1)S(1)}, u32[]{:S(2)}, u32[]{:S(2)}) %collective-permute-start.7) | collective-permute-done | bytes 393248 | tf_op jit(solution)/shard_map/ppermute | solution.py:31
  57.6 0.5 collective-permute-start.11
  58.1 0.5 collective-permute-start.13
  58.7 0.7 collective-permute-done.10.refs_0_
  59.4 0.8 copy-done.1
  60.5 0.7 copy-done.3
  61.6 0.7 copy-done.5
  62.6 4.5 %own.1.refs_11_ = f32[1056,256]{1,0:T(8,128)S(1)} custom-call(s32[4]{0:T(128)S(1)} %get-tuple-element.99.cols, bf16[2,4,32,768]{3,2,1,0:T(8,128)(2,1)S(1)} %get-tuple-element.62.refs_0_, bf16[2,4,32,768]{3,2,1,0:T(8,128)(2,1)S(1)} %collective-permute-done.4.refs_1_, bf16[2,4,32,768]{3,2,1,0:T(8,128)(2,1)S(1)} %collective-permute-done.6.refs_2_, ...), custom_call_target="tpu_custom_call" | custom-call | flops 1660944384 | bytes 7340032 | tf_op jit(solution)/shard_map/own/pallas_call | solution.py:204
  67.2 8.5 %other.1 = (bf16[4,2,4,32,768]{4,3,2,1,0:T(8,128)(2,1)S(1)}, bf16[4,2,4,32,768]{4,3,2,1,0:T(8,128)(2,1)S(1)}, bf16[256,352]{1,0:T(8,128)(2,1)S(1)}, bf16[256,704]{1,0:T(8,128)(2,1)S(1)}) custom-call(s32[4]{0:T(128)S(1)} %get-tuple-element.98.cols, bf16[2,4,32,768]{3,2,1,0:T(8,128)(2,1)S(1)} %copy-done.2, bf16[2,4,32,768]{3,2,1,0:T(8,128)(2,1)S(1)} %copy-done.4, ...), custom_call_target="tpu_custom_call" | custom-call | flops 3321888768 | bytes 7340032 | tf_op jit(solution)/shard_map/other/pallas_call | solution.py:204
  75.7 0.4 collective-permute-start.18
  76.3 4.8 %last.1 = (bf16[4,2,4,32,768]{4,3,2,1,0:T(8,128)(2,1)S(1)}, bf16[4,2,4,32,768]{4,3,2,1,0:T(8,128)(2,1)S(1)}) custom-call(s32[4]{0:T(128)S(1)} %get-tuple-element.99.cols, bf16[256,352]{1,0:T(8,128)(2,1)S(1)} %get-tuple-element.70.refs_0_, bf16[256,704]{1,0:T(8,128)(2,1)S(1)} %get-tuple-element.71.refs_1_, bf16[352,6144]{1,0:T(8,128)(2,1)} %bitcast.69, ...), custom_call_target="tpu_custom_call" | custom-call | flops 1660944384 | bytes 7340032 | tf_op jit(solution)/shard_map/last/pallas_call | solution.py:204
  81.1 0.6 fusion.8
  81.8 0.6 fusion.12
  82.6 2.0 %collective-permute-start.21 = (bf16[2,4,32,768]{3,2,1,0:T(8,128)(2,1)S(1)}, bf16[2,4,32,768]{3,2,1,0:T(8,128)(2,1)S(1)}, u32[]{:S(2)}, u32[]{:S(2)}) collective-permute-start(bf16[2,4,32,768]{3,2,1,0:T(8,128)(2,1)S(1)} %get-tuple-element.78), channel_id=1, source_target_pairs={{0,8},{8,0},{16,24},{24,16},{32,40},{40,32},{48,56},{56,48},{64,72... | collective-permute-start | bytes 1179656 | tf_op jit(solution)/shard_map/ppermute | solution.py:31
  84.5 1.3 collective-permute-start.22
  85.8 1.0 collective-permute-start.23
  86.8 3.5 %collective-permute-start.24 = (bf16[2,4,32,768]{3,2,1,0:T(8,128)(2,1)S(1)}, bf16[2,4,32,768]{3,2,1,0:T(8,128)(2,1)S(1)}, u32[]{:S(2)}, u32[]{:S(2)}) collective-permute-start(bf16[2,4,32,768]{3,2,1,0:T(8,128)(2,1)S(1)} %get-tuple-element.81), channel_id=1, source_target_pairs={{0,4},{1,5},{2,6},{3,7},{4,0},{5,1},{6,2},{7,3},{8,12},{9,13},{10,... | collective-permute-start | bytes 1179656 | tf_op jit(solution)/shard_map/ppermute | solution.py:36
  90.2 4.2 %collective-permute-done.20 = bf16[2,4,32,768]{3,2,1,0:T(8,128)(2,1)S(1)} collective-permute-done((bf16[2,4,32,768]{3,2,1,0:T(8,128)(2,1)S(1)}, bf16[2,4,32,768]{3,2,1,0:T(8,128)(2,1)S(1)}, u32[]{:S(2)}, u32[]{:S(2)}) %collective-permute-start.20) | collective-permute-done | bytes 393248 | tf_op jit(solution)/shard_map/ppermute | solution.py:36
  94.4 3.1 %collective-permute-start.25 = (bf16[2,4,32,768]{3,2,1,0:T(8,128)(2,1)S(1)}, bf16[2,4,32,768]{3,2,1,0:T(8,128)(2,1)S(1)}, u32[]{:S(2)}, u32[]{:S(2)}) collective-permute-start(bf16[2,4,32,768]{3,2,1,0:T(8,128)(2,1)S(1)} %get-tuple-element.82), channel_id=1, source_target_pairs={{0,16},{8,24},{16,0},{24,8},{32,48},{40,56},{48,32},{56,40},{64,80... | collective-permute-start | bytes 1179656 | tf_op jit(solution)/shard_map/ppermute | solution.py:31
  97.5 7.5 %collective-permute-done.22 = bf16[2,4,32,768]{3,2,1,0:T(8,128)(2,1)S(1)} collective-permute-done((bf16[2,4,32,768]{3,2,1,0:T(8,128)(2,1)S(1)}, bf16[2,4,32,768]{3,2,1,0:T(8,128)(2,1)S(1)}, u32[]{:S(2)}, u32[]{:S(2)}) %collective-permute-start.22) | collective-permute-done | bytes 393248 | tf_op jit(solution)/shard_map/ppermute | solution.py:36
  105.0 1.0 collective-permute-done.25
  106.5 2.0 %collective-permute-start.27 = (bf16[2,2,32,768]{3,2,1,0:T(8,128)(2,1)S(1)}, bf16[2,2,32,768]{3,2,1,0:T(8,128)(2,1)S(1)}, u32[]{:S(2)}, u32[]{:S(2)}) collective-permute-start(bf16[2,2,32,768]{3,2,1,0:T(8,128)(2,1)S(1)} %slice.106), channel_id=1, source_target_pairs={{0,6},{1,7},{2,4},{3,5},{4,2},{5,3},{6,0},{7,1},{8,14},{9,15},{10,... | collective-permute-start | bytes 589832 | tf_op jit(solution)/shard_map/ppermute | solution.py:36
  108.5 2.0 %collective-permute-start.26 = (bf16[2,2,32,768]{3,2,1,0:T(8,128)(2,1)S(1)}, bf16[2,2,32,768]{3,2,1,0:T(8,128)(2,1)S(1)}, u32[]{:S(2)}, u32[]{:S(2)}) collective-permute-start(bf16[2,2,32,768]{3,2,1,0:T(8,128)(2,1)S(1)} %slice.105), channel_id=1, source_target_pairs={{0,24},{8,16},{16,8},{24,0},{32,56},{40,48},{48,40},{56,32},{64,88... | collective-permute-start | bytes 589832 | tf_op jit(solution)/shard_map/ppermute | solution.py:31
  110.5 2.9 %collective-permute-done.27 = bf16[2,2,32,768]{3,2,1,0:T(8,128)(2,1)S(1)} collective-permute-done((bf16[2,2,32,768]{3,2,1,0:T(8,128)(2,1)S(1)}, bf16[2,2,32,768]{3,2,1,0:T(8,128)(2,1)S(1)}, u32[]{:S(2)}, u32[]{:S(2)}) %collective-permute-start.27) | collective-permute-done | bytes 196640 | tf_op jit(solution)/shard_map/ppermute | solution.py:36
  113.4 2.0 %collective-permute-done.26 = bf16[2,2,32,768]{3,2,1,0:T(8,128)(2,1)S(1)} collective-permute-done((bf16[2,2,32,768]{3,2,1,0:T(8,128)(2,1)S(1)}, bf16[2,2,32,768]{3,2,1,0:T(8,128)(2,1)S(1)}, u32[]{:S(2)}, u32[]{:S(2)}) %collective-permute-start.26) | collective-permute-done | bytes 196640 | tf_op jit(solution)/shard_map/ppermute | solution.py:31
  115.5 0.3 collective-permute-start.29
  115.9 4.4 %collective-permute-done.29 = bf16[2,1,32,768]{3,2,1,0:T(8,128)(2,1)S(1)} collective-permute-done((bf16[2,1,32,768]{3,2,1,0:T(8,128)(2,1)S(1)}, bf16[2,1,32,768]{3,2,1,0:T(8,128)(2,1)S(1)}, u32[]{:S(2)}, u32[]{:S(2)}) %collective-permute-start.29) | collective-permute-done | bytes 98336 | tf_op jit(solution)/shard_map/ppermute | solution.py:36
  120.2 0.2 collective-permute-done.28
  120.6 12.4 %all_to_all.11 = bf16[8,16,768]{2,1,0:T(8,128)(2,1)S(1)} all-to-all(bf16[8,16,768]{2,1,0:T(8,128)(2,1)S(1)} %bitcast.83), channel_id=1, replica_groups={{0,32,64,96,128,160,192,224},{8,40,72,104,136,168,200,232},{16,48,80,11..., dimensions={0} | all-to-all | bytes 393216 | tf_op jit(solution)/shard_map/all_to_all | solution.py:20
  133.0 0.8 fusion.3
  133.9 0.8 fusion.4
  (66 shorter events, 3.3 us)
Async XLA Ops:
  0.6 2.1 %copy-start = (bf16[16,768]{1,0:T(8,128)(2,1)S(1)}, bf16[16,768]{1,0:T(8,128)(2,1)}, u32[]{:S(2)}) copy-start(bf16[16,768]{1,0:T(8,128)(2,1)} %param.7) | copy-start | bytes 73732
  22.7 4.7 %collective-permute-start = (bf16[2,1,32,768]{3,2,1,0:T(8,128)(2,1)S(1)}, bf16[2,1,32,768]{3,2,1,0:T(8,128)(2,1)S(1)}, u32[]{:S(2)}, u32[]{:S(2)}) collective-permute-start(bf16[2,1,32,768]{3,2,1,0:T(8,128)(2,1)S(1)} %bitcast.79), channel_id=1, source_target_pairs={{0,8},{8,0},{16,24},{24,16},{32,40},{40,32},{48,56},{56,48},{64,72... | collective-permute-start | bytes 294920 | tf_op jit(solution)/shard_map/ppermute | solution.py:31
  24.4 4.6 %collective-permute-start.1 = (bf16[2,1,32,768]{3,2,1,0:T(8,128)(2,1)S(1)}, bf16[2,1,32,768]{3,2,1,0:T(8,128)(2,1)S(1)}, u32[]{:S(2)}, u32[]{:S(2)}) collective-permute-start(bf16[2,1,32,768]{3,2,1,0:T(8,128)(2,1)S(1)} %bitcast.76), channel_id=1, source_target_pairs={{0,2},{1,3},{2,0},{3,1},{4,6},{5,7},{6,4},{7,5},{8,10},{9,11},{10,... | collective-permute-start | bytes 294920 | tf_op jit(solution)/shard_map/ppermute | solution.py:36
  29.1 11.2 %collective-permute-start.3 = (bf16[2,2,32,768]{3,2,1,0:T(8,128)(2,1)S(1)}, bf16[2,2,32,768]{3,2,1,0:T(8,128)(2,1)S(1)}, u32[]{:S(2)}, u32[]{:S(2)}) collective-permute-start(bf16[2,2,32,768]{3,2,1,0:T(8,128)(2,1)S(1)} %pad_maximum_fusion.4), channel_id=1, source_target_pairs={{0,6},{1,7},{2,4},{3,5},{4,2},{5,3},{6,0},{7,1},{8,14},{9,15},{10,... | collective-permute-start | bytes 589832 | tf_op jit(solution)/shard_map/ppermute | solution.py:36
  29.6 10.7 %collective-permute-start.2 = (bf16[2,2,32,768]{3,2,1,0:T(8,128)(2,1)S(1)}, bf16[2,2,32,768]{3,2,1,0:T(8,128)(2,1)S(1)}, u32[]{:S(2)}, u32[]{:S(2)}) collective-permute-start(bf16[2,2,32,768]{3,2,1,0:T(8,128)(2,1)S(1)} %pad_maximum_fusion.3), channel_id=1, source_target_pairs={{0,24},{8,16},{16,8},{24,0},{32,56},{40,48},{48,40},{56,32},{64,88... | collective-permute-start | bytes 589832 | tf_op jit(solution)/shard_map/ppermute | solution.py:31
  40.4 9.5 %collective-permute-start.8 = (bf16[2,4,32,768]{3,2,1,0:T(8,128)(2,1)S(1)}, bf16[2,4,32,768]{3,2,1,0:T(8,128)(2,1)S(1)}, u32[]{:S(2)}, u32[]{:S(2)}) collective-permute-start(bf16[2,4,32,768]{3,2,1,0:T(8,128)(2,1)S(1)} %get-tuple-element.62.refs_0_), channel_id=1, source_target_pairs={{0,4},{1,5},{2,6},{3,7},{4,0},{5,1},{6,2},{7,3},{8,12},{9,13},{10,... | collective-permute-start | bytes 1179656 | tf_op jit(solution)/shard_map/ppermute | solution.py:36
  40.5 13.3 %collective-permute-start.6 = (bf16[2,4,32,768]{3,2,1,0:T(8,128)(2,1)S(1)}, bf16[2,4,32,768]{3,2,1,0:T(8,128)(2,1)S(1)}, u32[]{:S(2)}, u32[]{:S(2)}) collective-permute-start(bf16[2,4,32,768]{3,2,1,0:T(8,128)(2,1)S(1)} %get-tuple-element.62.refs_0_), channel_id=1, source_target_pairs={{0,6},{1,7},{2,4},{3,5},{4,2},{5,3},{6,0},{7,1},{8,14},{9,15},{10,... | collective-permute-start | bytes 1179656 | tf_op jit(solution)/shard_map/ppermute | solution.py:36
  40.6 13.2 %collective-permute-start.4 = (bf16[2,4,32,768]{3,2,1,0:T(8,128)(2,1)S(1)}, bf16[2,4,32,768]{3,2,1,0:T(8,128)(2,1)S(1)}, u32[]{:S(2)}, u32[]{:S(2)}) collective-permute-start(bf16[2,4,32,768]{3,2,1,0:T(8,128)(2,1)S(1)} %get-tuple-element.62.refs_0_), channel_id=1, source_target_pairs={{0,2},{1,3},{2,0},{3,1},{4,6},{5,7},{6,4},{7,5},{8,10},{9,11},{10,... | collective-permute-start | bytes 1179656 | tf_op jit(solution)/shard_map/ppermute | solution.py:36
  43.9 9.8 %collective-permute-start.9 = (bf16[2,4,32,768]{3,2,1,0:T(8,128)(2,1)S(1)}, bf16[2,4,32,768]{3,2,1,0:T(8,128)(2,1)S(1)}, u32[]{:S(2)}, u32[]{:S(2)}) collective-permute-start(bf16[2,4,32,768]{3,2,1,0:T(8,128)(2,1)S(1)} %get-tuple-element.66.refs_4_), channel_id=1, source_target_pairs={{0,16},{8,24},{16,0},{24,8},{32,48},{40,56},{48,32},{56,40},{64,80... | collective-permute-start | bytes 1179656 | tf_op jit(solution)/shard_map/ppermute | solution.py:31
  47.0 10.4 %collective-permute-start.7 = (bf16[2,4,32,768]{3,2,1,0:T(8,128)(2,1)S(1)}, bf16[2,4,32,768]{3,2,1,0:T(8,128)(2,1)S(1)}, u32[]{:S(2)}, u32[]{:S(2)}) collective-permute-start(bf16[2,4,32,768]{3,2,1,0:T(8,128)(2,1)S(1)} %get-tuple-element.66.refs_4_), channel_id=1, source_target_pairs={{0,24},{8,16},{16,8},{24,0},{32,56},{40,48},{48,40},{56,32},{64,88... | collective-permute-start | bytes 1179656 | tf_op jit(solution)/shard_map/ppermute | solution.py:31
  49.8 7.8 %collective-permute-start.5 = (bf16[2,4,32,768]{3,2,1,0:T(8,128)(2,1)S(1)}, bf16[2,4,32,768]{3,2,1,0:T(8,128)(2,1)S(1)}, u32[]{:S(2)}, u32[]{:S(2)}) collective-permute-start(bf16[2,4,32,768]{3,2,1,0:T(8,128)(2,1)S(1)} %get-tuple-element.66.refs_4_), channel_id=1, source_target_pairs={{0,8},{8,0},{16,24},{24,16},{32,40},{40,32},{48,56},{56,48},{64,72... | collective-permute-start | bytes 1179656 | tf_op jit(solution)/shard_map/ppermute | solution.py:31
  57.6 1.7 %collective-permute-start.10 = (bf16[2,4,32,768]{3,2,1,0:T(8,128)(2,1)S(1)}, bf16[2,4,32,768]{3,2,1,0:T(8,128)(2,1)S(1)}, u32[]{:S(2)}, u32[]{:S(2)}) collective-permute-start(bf16[2,4,32,768]{3,2,1,0:T(8,128)(2,1)S(1)} %get-tuple-element.62.refs_0_), channel_id=1, source_target_pairs={{0,1},{1,0},{2,3},{3,2},{4,5},{5,4},{6,7},{7,6},{8,9},{9,8},{10,11... | collective-permute-start | bytes 1179656 | tf_op jit(solution)/shard_map/ppermute | solution.py:40
  57.6 2.8 %collective-permute-start.11 = (bf16[2,4,32,768]{3,2,1,0:T(8,128)(2,1)S(1)}, bf16[2,4,32,768]{3,2,1,0:T(8,128)(2,1)S(1)}, u32[]{:S(2)}, u32[]{:S(2)}) collective-permute-start(bf16[2,4,32,768]{3,2,1,0:T(8,128)(2,1)S(1)} %collective-permute-done.4.refs_1_), channel_id=1, source_target_pairs={{0,1},{1,0},{2,3},{3,2},{4,5},{5,4},{6,7},{7,6},{8,9},{9,8},{10,11... | collective-permute-start | bytes 1179656 | tf_op jit(solution)/shard_map/ppermute | solution.py:40
  58.1 3.5 %collective-permute-start.12 = (bf16[2,4,32,768]{3,2,1,0:T(8,128)(2,1)S(1)}, bf16[2,4,32,768]{3,2,1,0:T(8,128)(2,1)S(1)}, u32[]{:S(2)}, u32[]{:S(2)}) collective-permute-start(bf16[2,4,32,768]{3,2,1,0:T(8,128)(2,1)S(1)} %collective-permute-done.6.refs_2_), channel_id=1, source_target_pairs={{0,1},{1,0},{2,3},{3,2},{4,5},{5,4},{6,7},{7,6},{8,9},{9,8},{10,11... | collective-permute-start | bytes 1179656 | tf_op jit(solution)/shard_map/ppermute | solution.py:40
  58.1 9.0 %collective-permute-start.13 = (bf16[2,4,32,768]{3,2,1,0:T(8,128)(2,1)S(1)}, bf16[2,4,32,768]{3,2,1,0:T(8,128)(2,1)}, u32[]{:S(2)}, u32[]{:S(2)}) collective-permute-start(bf16[2,4,32,768]{3,2,1,0:T(8,128)(2,1)S(1)} %collective-permute-done.8.refs_3_), channel_id=1, source_target_pairs={{0,1},{1,0},{2,3},{3,2},{4,5},{5,4},{6,7},{7,6},{8,9},{9,8},{10,11... | collective-permute-start | bytes 1179656 | tf_op jit(solution)/shard_map/ppermute | solution.py:40
  58.6 8.5 %collective-permute-start.14 = (bf16[2,4,32,768]{3,2,1,0:T(8,128)(2,1)S(1)}, bf16[2,4,32,768]{3,2,1,0:T(8,128)(2,1)}, u32[]{:S(2)}, u32[]{:S(2)}) collective-permute-start(bf16[2,4,32,768]{3,2,1,0:T(8,128)(2,1)S(1)} %get-tuple-element.66.refs_4_), channel_id=1, source_target_pairs={{0,1},{1,0},{2,3},{3,2},{4,5},{5,4},{6,7},{7,6},{8,9},{9,8},{10,11... | collective-permute-start | bytes 1179656 | tf_op jit(solution)/shard_map/ppermute | solution.py:40
  59.3 0.8 copy-start.1
  60.1 7.0 %collective-permute-start.15 = (bf16[2,4,32,768]{3,2,1,0:T(8,128)(2,1)S(1)}, bf16[2,4,32,768]{3,2,1,0:T(8,128)(2,1)}, u32[]{:S(2)}, u32[]{:S(2)}) collective-permute-start(bf16[2,4,32,768]{3,2,1,0:T(8,128)(2,1)S(1)} %collective-permute-done.5.refs_5_), channel_id=1, source_target_pairs={{0,1},{1,0},{2,3},{3,2},{4,5},{5,4},{6,7},{7,6},{8,9},{9,8},{10,11... | collective-permute-start | bytes 1179656 | tf_op jit(solution)/shard_map/ppermute | solution.py:40
  60.5 0.7 copy-start.3
  61.2 5.9 %collective-permute-start.16 = (bf16[2,4,32,768]{3,2,1,0:T(8,128)(2,1)S(1)}, bf16[2,4,32,768]{3,2,1,0:T(8,128)(2,1)}, u32[]{:S(2)}, u32[]{:S(2)}) collective-permute-start(bf16[2,4,32,768]{3,2,1,0:T(8,128)(2,1)S(1)} %collective-permute-done.7.refs_6_), channel_id=1, source_target_pairs={{0,1},{1,0},{2,3},{3,2},{4,5},{5,4},{6,7},{7,6},{8,9},{9,8},{10,11... | collective-permute-start | bytes 1179656 | tf_op jit(solution)/shard_map/ppermute | solution.py:40
  61.6 0.7 copy-start.5
  62.3 4.8 %collective-permute-start.17 = (bf16[2,4,32,768]{3,2,1,0:T(8,128)(2,1)S(1)}, bf16[2,4,32,768]{3,2,1,0:T(8,128)(2,1)}, u32[]{:S(2)}, u32[]{:S(2)}) collective-permute-start(bf16[2,4,32,768]{3,2,1,0:T(8,128)(2,1)S(1)} %collective-permute-done.9.refs_7_), channel_id=1, source_target_pairs={{0,1},{1,0},{2,3},{3,2},{4,5},{5,4},{6,7},{7,6},{8,9},{9,8},{10,11... | collective-permute-start | bytes 1179656 | tf_op jit(solution)/shard_map/ppermute | solution.py:40
  62.6 4.6 %copy-start.2 = (bf16[2,4,32,768]{3,2,1,0:T(8,128)(2,1)S(1)}, bf16[2,4,32,768]{3,2,1,0:T(8,128)(2,1)}, u32[]{:S(2)}) copy-start(bf16[2,4,32,768]{3,2,1,0:T(8,128)(2,1)} %copy-done.1) | copy-start | bytes 1179652
  62.6 4.6 %copy-start.4 = (bf16[2,4,32,768]{3,2,1,0:T(8,128)(2,1)S(1)}, bf16[2,4,32,768]{3,2,1,0:T(8,128)(2,1)}, u32[]{:S(2)}) copy-start(bf16[2,4,32,768]{3,2,1,0:T(8,128)(2,1)} %copy-done.3) | copy-start | bytes 1179652
  62.6 4.6 %copy-start.6 = (bf16[2,4,32,768]{3,2,1,0:T(8,128)(2,1)S(1)}, bf16[2,4,32,768]{3,2,1,0:T(8,128)(2,1)}, u32[]{:S(2)}) copy-start(bf16[2,4,32,768]{3,2,1,0:T(8,128)(2,1)} %copy-done.5) | copy-start | bytes 1179652
  75.7 5.4 %collective-permute-start.18 = (bf16[4,2,4,32,768]{4,3,2,1,0:T(8,128)(2,1)S(1)}, bf16[4,2,4,32,768]{4,3,2,1,0:T(8,128)(2,1)S(1)}, u32[]{:S(2)}, u32[]{:S(2)}) collective-permute-start(bf16[4,2,4,32,768]{4,3,2,1,0:T(8,128)(2,1)S(1)} %get-tuple-element.73), channel_id=1, source_target_pairs={{0,1},{1,0},{2,3},{3,2},{4,5},{5,4},{6,7},{7,6},{8,9},{9,8},{10,11... | collective-permute-start | bytes 4718600 | tf_op jit(solution)/shard_map/ppermute | solution.py:40
  76.2 5.6 %collective-permute-start.19 = (bf16[4,2,4,32,768]{4,3,2,1,0:T(8,128)(2,1)S(1)}, bf16[4,2,4,32,768]{4,3,2,1,0:T(8,128)(2,1)S(1)}, u32[]{:S(2)}, u32[]{:S(2)}) collective-permute-start(bf16[4,2,4,32,768]{4,3,2,1,0:T(8,128)(2,1)S(1)} %get-tuple-element.75), channel_id=1, source_target_pairs={{0,1},{1,0},{2,3},{3,2},{4,5},{5,4},{6,7},{7,6},{8,9},{9,8},{10,11... | collective-permute-start | bytes 4718600 | tf_op jit(solution)/shard_map/ppermute | solution.py:40
  82.4 12.0 %collective-permute-start.20 = (bf16[2,4,32,768]{3,2,1,0:T(8,128)(2,1)S(1)}, bf16[2,4,32,768]{3,2,1,0:T(8,128)(2,1)S(1)}, u32[]{:S(2)}, u32[]{:S(2)}) collective-permute-start(bf16[2,4,32,768]{3,2,1,0:T(8,128)(2,1)S(1)} %get-tuple-element.77), channel_id=1, source_target_pairs={{0,2},{1,3},{2,0},{3,1},{4,6},{5,7},{6,4},{7,5},{8,10},{9,11},{10,... | collective-permute-start | bytes 1179656 | tf_op jit(solution)/shard_map/ppermute | solution.py:36
  82.6 15.0 %collective-permute-start.21 = (bf16[2,4,32,768]{3,2,1,0:T(8,128)(2,1)S(1)}, bf16[2,4,32,768]{3,2,1,0:T(8,128)(2,1)S(1)}, u32[]{:S(2)}, u32[]{:S(2)}) collective-permute-start(bf16[2,4,32,768]{3,2,1,0:T(8,128)(2,1)S(1)} %get-tuple-element.78), channel_id=1, source_target_pairs={{0,8},{8,0},{16,24},{24,16},{32,40},{40,32},{48,56},{56,48},{64,72... | collective-permute-start | bytes 1179656 | tf_op jit(solution)/shard_map/ppermute | solution.py:31
  84.5 20.4 %collective-permute-start.22 = (bf16[2,4,32,768]{3,2,1,0:T(8,128)(2,1)S(1)}, bf16[2,4,32,768]{3,2,1,0:T(8,128)(2,1)S(1)}, u32[]{:S(2)}, u32[]{:S(2)}) collective-permute-start(bf16[2,4,32,768]{3,2,1,0:T(8,128)(2,1)S(1)} %get-tuple-element.79), channel_id=1, source_target_pairs={{0,6},{1,7},{2,4},{3,5},{4,2},{5,3},{6,0},{7,1},{8,14},{9,15},{10,... | collective-permute-start | bytes 1179656 | tf_op jit(solution)/shard_map/ppermute | solution.py:36
  85.8 19.2 %collective-permute-start.23 = (bf16[2,4,32,768]{3,2,1,0:T(8,128)(2,1)S(1)}, bf16[2,4,32,768]{3,2,1,0:T(8,128)(2,1)S(1)}, u32[]{:S(2)}, u32[]{:S(2)}) collective-permute-start(bf16[2,4,32,768]{3,2,1,0:T(8,128)(2,1)S(1)} %get-tuple-element.80), channel_id=1, source_target_pairs={{0,24},{8,16},{16,8},{24,0},{32,56},{40,48},{48,40},{56,32},{64,88... | collective-permute-start | bytes 1179656 | tf_op jit(solution)/shard_map/ppermute | solution.py:31
  86.8 18.2 %collective-permute-start.24 = (bf16[2,4,32,768]{3,2,1,0:T(8,128)(2,1)S(1)}, bf16[2,4,32,768]{3,2,1,0:T(8,128)(2,1)S(1)}, u32[]{:S(2)}, u32[]{:S(2)}) collective-permute-start(bf16[2,4,32,768]{3,2,1,0:T(8,128)(2,1)S(1)} %get-tuple-element.81), channel_id=1, source_target_pairs={{0,4},{1,5},{2,6},{3,7},{4,0},{5,1},{6,2},{7,3},{8,12},{9,13},{10,... | collective-permute-start | bytes 1179656 | tf_op jit(solution)/shard_map/ppermute | solution.py:36
  94.4 11.6 %collective-permute-start.25 = (bf16[2,4,32,768]{3,2,1,0:T(8,128)(2,1)S(1)}, bf16[2,4,32,768]{3,2,1,0:T(8,128)(2,1)S(1)}, u32[]{:S(2)}, u32[]{:S(2)}) collective-permute-start(bf16[2,4,32,768]{3,2,1,0:T(8,128)(2,1)S(1)} %get-tuple-element.82), channel_id=1, source_target_pairs={{0,16},{8,24},{16,0},{24,8},{32,48},{40,56},{48,32},{56,40},{64,80... | collective-permute-start | bytes 1179656 | tf_op jit(solution)/shard_map/ppermute | solution.py:31
  106.5 7.0 %collective-permute-start.27 = (bf16[2,2,32,768]{3,2,1,0:T(8,128)(2,1)S(1)}, bf16[2,2,32,768]{3,2,1,0:T(8,128)(2,1)S(1)}, u32[]{:S(2)}, u32[]{:S(2)}) collective-permute-start(bf16[2,2,32,768]{3,2,1,0:T(8,128)(2,1)S(1)} %slice.106), channel_id=1, source_target_pairs={{0,6},{1,7},{2,4},{3,5},{4,2},{5,3},{6,0},{7,1},{8,14},{9,15},{10,... | collective-permute-start | bytes 589832 | tf_op jit(solution)/shard_map/ppermute | solution.py:36
  108.5 6.9 %collective-permute-start.26 = (bf16[2,2,32,768]{3,2,1,0:T(8,128)(2,1)S(1)}, bf16[2,2,32,768]{3,2,1,0:T(8,128)(2,1)S(1)}, u32[]{:S(2)}, u32[]{:S(2)}) collective-permute-start(bf16[2,2,32,768]{3,2,1,0:T(8,128)(2,1)S(1)} %slice.105), channel_id=1, source_target_pairs={{0,24},{8,16},{16,8},{24,0},{32,56},{40,48},{48,40},{56,32},{64,88... | collective-permute-start | bytes 589832 | tf_op jit(solution)/shard_map/ppermute | solution.py:31
  115.5 4.7 %collective-permute-start.29 = (bf16[2,1,32,768]{3,2,1,0:T(8,128)(2,1)S(1)}, bf16[2,1,32,768]{3,2,1,0:T(8,128)(2,1)S(1)}, u32[]{:S(2)}, u32[]{:S(2)}) collective-permute-start(bf16[2,1,32,768]{3,2,1,0:T(8,128)(2,1)S(1)} %slice.110), channel_id=1, source_target_pairs={{0,2},{1,3},{2,0},{3,1},{4,6},{5,7},{6,4},{7,5},{8,10},{9,11},{10,... | collective-permute-start | bytes 294920 | tf_op jit(solution)/shard_map/ppermute | solution.py:36
  115.8 4.6 %collective-permute-start.28 = (bf16[2,1,32,768]{3,2,1,0:T(8,128)(2,1)S(1)}, bf16[2,1,32,768]{3,2,1,0:T(8,128)(2,1)S(1)}, u32[]{:S(2)}, u32[]{:S(2)}) collective-permute-start(bf16[2,1,32,768]{3,2,1,0:T(8,128)(2,1)S(1)} %slice.109), channel_id=1, source_target_pairs={{0,8},{8,0},{16,24},{24,16},{32,40},{40,32},{48,56},{56,48},{64,72... | collective-permute-start | bytes 294920 | tf_op jit(solution)/shard_map/ppermute | solution.py:31

commit v2 on v1

v2 whole, which is shorter than its diff:
```python
import itertools

import jax
import jax.numpy as jnp
from jax import lax
from jax.experimental import pallas as pl
from jax.experimental.pallas import tpu as pltpu
from jax.sharding import PartitionSpec as P

E = 8
NY = 4
NX = 4
CAP = 8
BF = jnp.bfloat16
F32 = jnp.float32
NT = (((1,), (1,)), ((), ()))
VMEM_LIMIT = {"own": 20, "other": 24, "last": 16}


def swap_z(v):
    groups = [[z * NY + y for z in range(E)] for y in range(NY)]
    return lax.all_to_all(v, "dp", 0, 0, axis_index_groups=groups, tiled=True)


def partner(i, q):
    if q == 1:
        return i ^ 1
    return (i + (1 if i % 2 else 3)) % 4 if q == 2 else i ^ 2


def swap(v, q, along_y):
    def place(z, y, x, c):
        return (z * NY + y) * 2 * NX + x * 2 + c

    perm = []
    for z, y, x, c in itertools.product(range(E), range(NY), range(NX), range(2)):
        if c == along_y:
            to = place(z, partner(y, q), x, c)
        else:
            to = place(z, y, partner(x, q), c)
        perm.append((place(z, y, x, c), to))
    return lax.ppermute(v, ("dp", "cuts"), perm)


def to_core(v):
    return lax.ppermute(v, "cuts", [(i, i ^ 1) for i in range(2 * NX)])


def slots_of(routing, gate_values):
    hit = routing[:, :, None] == jnp.arange(E, dtype=jnp.int32)
    chosen = jnp.any(hit, axis=1)
    gates = jnp.sum(jnp.where(hit, gate_values[:, :, None], 0.0), axis=1)
    rows = routing.shape[0]
    below = jnp.arange(rows)[:, None] > jnp.arange(rows)[None, :]
    position = jnp.sum(
        jnp.where(below[:, :, None] & chosen[None, :, :], 1, 0), axis=1
    )
    slot = position[:, :, None] == jnp.arange(CAP, dtype=jnp.int32)
    select = chosen[:, :, None] & slot
    weight = jnp.where(select, gates[:, :, None], 0.0)
    return select.reshape(rows, E * CAP), weight.reshape(rows, E * CAP)


def gather(v, along_y):
    far, near, next_ = lax.optimization_barrier(
        tuple(swap(v, q, along_y) for q in (3, 1, 2))
    )
    return [v, near, next_, far]


def add(*parts):
    total = parts[0].astype(F32)
    for p in parts[1:]:
        total = total + p.astype(F32)
    return total.astype(BF)


def scatter(parts, along_y):
    parts = lax.optimization_barrier(tuple(parts))
    got = lax.optimization_barrier(
        tuple(swap(parts[q], q, along_y) for q in (3, 1, 2))
    )
    return add(parts[0], *got)


def fetch_weights(info, weights, buf, sem):
    hidden, width = weights[0].shape[0], buf.shape[-1]

    def copy(i, k, at):
        rows = pl.ds(i * hidden, hidden)
        return pltpu.make_async_copy(
            weights[i].at[:, pl.ds(at, width)], buf.at[k, rows], sem.at[k, i]
        )

    for k in range(NX):
        for i in range(3):
            copy(i, k, pl.multiple_of(info[k] * width, 128)).start()

    def wait(k):
        for i in range(3):
            copy(i, k, 0).wait()

    return wait


def order(info, b, a):
    first = info[NX] == 0
    return jnp.where(first, b, a), jnp.where(first, a, b)


def load_rows(info, pieces, rows):
    step = rows.shape[2] // NY
    for b in range(4):
        for a in range(4):
            k, j = order(info, b, a)
            at = pl.ds(pl.multiple_of(j * step, step), step)
            for i in range(2):
                rows[k, i, at] = pieces[b][a, i]


def contract(wait, rows, buf, acc):
    two = acc.shape[0] // 3 * 2

    @pl.loop(0, NX)
    def _(k):
        wait(k)
        acc[:two] += lax.dot_general(
            buf[k, :two], rows[k, 0], NT, preferred_element_type=F32
        )
        acc[two:] += lax.dot_general(
            buf[k, two:], rows[k, 1], NT, preferred_element_type=F32
        )


def expand(info, wait, hidden, grads, buf, out):
    step = hidden.shape[0] // NY
    two = grads.shape[1]

    def put(k, i, value):
        for j in range(NY):
            b, a = order(info, k, j)
            out[b, a, i] = value[j * step : (j + 1) * step]

    @pl.loop(0, NX)
    def _(k):
        if wait is not None:
            wait(k)
        o = jnp.dot(hidden[...], buf[k, two:], preferred_element_type=F32)
        put(k, 0, o.astype(BF))
        o = jnp.dot(grads[...], buf[k, :two], preferred_element_type=F32)
        put(k, 1, o.astype(BF))


def own_kernel(info, *refs):
    pieces, weights, (acc, rows, buf, sem) = refs[:4], refs[4:7], refs[7:]
    wait = fetch_weights(info, weights, buf, sem)
    load_rows(info, pieces, rows)
    acc[...] = jnp.zeros_like(acc)
    contract(wait, rows, buf, acc)


def other_kernel(info, *refs):
    pieces, weights, partial, rest = refs[:4], refs[4:7], refs[7], refs[8:]
    out, hidden, grads, rows, acc, buf, sem = rest
    wait = fetch_weights(info, weights, buf, sem)
    load_rows(info, pieces, rows)
    acc[...] = partial[...]
    contract(wait, rows, buf, acc)
    one = acc.shape[0] // 3
    g, u, h = acc[:one], acc[one : 2 * one], acc[2 * one :]
    sigma = jax.nn.sigmoid(g)
    hidden[...] = (g * sigma * u).T.astype(BF)
    gate_grad = h * u * sigma * (1.0 + g * (1.0 - sigma))
    grads[...] = jnp.concatenate([gate_grad, h * g * sigma], axis=0).T.astype(BF)
    expand(info, None, hidden, grads, buf, out)


def last_kernel(info, *refs):
    (hidden, grads), weights, (out, buf, sem) = refs[:2], refs[2:5], refs[5:]
    wait = fetch_weights(info, weights, buf, sem)
    expand(info, wait, hidden, grads, buf, out)


def call(body, name, info, arrays, weights, partial, out, scratch, products):
    hidden, width = weights[0].shape[0], weights[0].shape[1] // (2 * NX)
    rows = E * CAP * NY
    return pl.pallas_call(
        body,
        name=name,
        out_shape=out,
        in_specs=[pl.BlockSpec(memory_space=pltpu.SMEM)]
        + [pl.BlockSpec(memory_space=pltpu.VMEM)] * len(arrays)
        + [pl.BlockSpec(memory_space=pltpu.HBM)] * 3
        + [pl.BlockSpec(memory_space=pltpu.VMEM)] * len(partial),
        out_specs=[pl.BlockSpec(memory_space=pltpu.VMEM)] * len(out),
        scratch_shapes=scratch
        + [
            pltpu.VMEM((NX, 3 * hidden, width), BF),
            pltpu.SemaphoreType.DMA((NX, 3)),
        ],
        compiler_params=pltpu.CompilerParams(vmem_limit_bytes=VMEM_LIMIT[name] << 20),
        cost_estimate=pl.CostEstimate(
            flops=2 * products * rows * width * NX * hidden,
            bytes_accessed=7 << 20,
            transcendentals=0,
        ),
    )(info, *arrays, *weights, *partial)


def on_device(tokens, out_grad, gate_values, routing, gate_weight, up_weight, down_weight):
    width = tokens.shape[1]
    cut = lax.axis_index("cuts")
    x, c = cut // 2, cut % 2
    wg = jnp.swapaxes(gate_weight[0], 0, 1)
    wu = jnp.swapaxes(up_weight[0], 0, 1)
    w2 = down_weight[0]
    hidden = w2.shape[0]
    steps = jnp.arange(NX + 1)
    there = jnp.where(steps == 2, (x + 3 + 2 * (x % 2)) % NX, x ^ steps)
    there = jnp.where(steps == 3, x ^ 2, there)
    own_info = jnp.where(steps < NX, there * 2 + c, c)
    other_info = own_info ^ 1
    rows = NY * E * CAP

    select, weight = slots_of(routing, gate_values)
    pick = select.astype(BF).T
    send_x = jnp.dot(pick, tokens, preferred_element_type=F32).astype(BF)
    slot_gate = jnp.sum(weight, axis=0)
    send_dy = jnp.dot(pick, out_grad, preferred_element_type=F32)
    send_dy = (slot_gate[:, None] * send_dy).astype(BF)
    send = jnp.concatenate(
        [send_x.reshape(E, CAP, width), send_dy.reshape(E, CAP, width)], axis=1
    )
    got = swap_z(send).reshape(E, 2, CAP, width)
    got = jnp.swapaxes(got, 0, 1).reshape(2, E * CAP, width)

    own = gather(jnp.stack(gather(got, 0)), 1)
    own = list(lax.optimization_barrier(tuple(own)))
    other = [to_core(v) for v in own]

    weights = [pltpu.with_memory_space_constraint(w, pltpu.HBM) for w in (wg, wu, w2)]
    pre = jax.ShapeDtypeStruct((3 * hidden, rows), F32)
    act = [
        jax.ShapeDtypeStruct((rows, hidden), BF),
        jax.ShapeDtypeStruct((rows, 2 * hidden), BF),
    ]
    pieces = [jax.ShapeDtypeStruct((4, 4, 2, rows // 4, width), BF)]
    row_buf = [pltpu.VMEM((NX, 2, rows, width), BF)]
    acc_buf = [pltpu.VMEM(pre.shape, F32)]
    partial = call(own_kernel, "own", own_info, own, weights, [], [pre], row_buf, 3)
    far, *act = call(
        other_kernel, "other", other_info, other, weights, partial,
        pieces + act, row_buf + acc_buf, 6,
    )
    (near,) = call(last_kernel, "last", own_info, act, weights, [], pieces, [], 3)
    got = to_core(far)
    sums = scatter([add(near[b], got[b]) for b in range(4)], 1)
    back = scatter([sums[a] for a in range(4)], 0)
    back = back.reshape(2, E, CAP, width)
    back = jnp.swapaxes(back, 0, 1).reshape(E, 2 * CAP, width)
    back = swap_z(back)
    back_y = back[:, :CAP].reshape(E * CAP, width)
    back_dx = back[:, CAP:].reshape(E * CAP, width)
    mixed = jnp.dot(weight, back_y.astype(F32), precision=lax.Precision.HIGHEST)
    grad = jnp.dot(select.astype(BF), back_dx, preferred_element_type=F32)
    return mixed.astype(BF), grad.astype(BF)


def solution(mesh):
    return jax.shard_map(
        on_device,
        mesh=mesh,
        in_specs=(
            P("dp", "cuts"),
            P("dp", "cuts"),
            P("dp", None),
            P("dp", None),
            P("dp", None, "cuts"),
            P("dp", None, "cuts"),
            P("dp", "cuts", None),
        ),
        out_specs=(P("dp", "cuts"), P("dp", "cuts")),
        check_vma=False,
    )
```

time: 136 us -> 132 us (0.971)
  starting transfers between devices: 30.1 us -> 18.1 us
  waiting for transfers between devices: 45.3 us -> 56.6 us
  local copies, waits for them, and re-layouts: 2.59 us -> 0.32 us
    ppermute x20 -> x12, waiting for transfers between devices: 44.1 us -> 55.8 us  [swap(): return lax.ppermute(v, ('dp', 'cuts'), perm)]
    ppermute x20 -> x12, starting transfers between devices: 28.1 us -> 16.9 us  [swap(): return lax.ppermute(v, ('dp', 'cuts'), perm)]
    unnamed x14 -> x2, local copies, waits for them, and re-layouts: 2.27 us -> 0.01 us
  transfers between devices with their start and end apart: 30 -> 17, of which waited for: 17 -> 13; matrix products, arithmetic and copies ran while one was open for 1% -> 0% of each run, Pallas kernels for 7% -> 7%
where the time goes in v2:
time: 132 us; the launch traced here: 131 us
  waiting for transfers between devices  56.6 us (43%)
  blocking collectives  30.9 us (23%)
  Pallas kernels  18.2 us (14%)
  starting transfers between devices  18.1 us (14%)
  other arithmetic  3.6 us (3%)
  matrix products  2.83 us (2%)
    ppermute x12, waiting for transfers between devices, swap(): return lax.ppermute(v, ('dp', 'cuts'), perm)  55.8 us
    all_to_all x2, blocking collectives, swap_z(): return lax.all_to_all(v, 'dp', 0, 0, axis_index_groups=groups, tiled=True)  30.9 us
    pallas_call x3, Pallas kernels, call(): pl.pallas_call(body, name=name, out_shape=out, in_specs=[pl.BlockSpec(mem...  18.2 us
    ppermute x12, starting transfers between devices, swap(): return lax.ppermute(v, ('dp', 'cuts'), perm)  16.9 us
  transfers between devices with their start and end apart: 17, of which 13 were waited for; matrix products, arithmetic and copies ran while one was open for 0% of the time, Pallas kernels for 7%

profile of v2, /device:TPU:6, one launch (start us, length us, event | category | flops | bytes accessed | tf_op | source)
XLA Modules:
  0.0 131.4 jit_solution(6699029886378506838)
XLA Ops:
  0.7 0.7 fusion.31
  1.3 0.7 select_reduce_fusion.2
  2.0 0.3 select_reduce_fusion
  2.4 0.1 copy.19
  2.5 0.1 select_reduce_fusion.1
  2.6 0.1 mul.18
  2.7 0.1 eq.59
  2.7 0.2 fusion.2
  3.0 1.0 fusion.1
  3.9 18.7 %all_to_all.10 = bf16[8,16,768]{2,1,0:T(8,128)(2,1)S(1)} all-to-all(bf16[8,16,768]{2,1,0:T(8,128)(2,1)S(1)} %pad_maximum_fusion.1), channel_id=1, replica_groups={{0,32,64,96,128,160,192,224},{8,40,72,104,136,168,200,232},{16,48,80,11..., dimensions={0} | all-to-all | bytes 393216 | tf_op jit(solution)/shard_map/all_to_all | solution.py:22
  22.7 3.3 %collective-permute-start = (bf16[2,64,768]{2,1,0:T(8,128)(2,1)S(1)}, bf16[2,64,768]{2,1,0:T(8,128)(2,1)S(1)}, u32[]{:S(2)}, u32[]{:S(2)}) collective-permute-start(bf16[2,64,768]{2,1,0:T(8,128)(2,1)S(1)} %get-tuple-element.67), channel_id=1, source_target_pairs={{0,16},{1,5},{2,18},{3,7},{4,20},{5,1},{6,22},{7,3},{8,24},{9,13},... | collective-permute-start | bytes 589832 | tf_op jit(solution)/shard_map/ppermute | solution.py:42
  26.0 0.7 collective-permute-start.1
  26.7 0.4 collective-permute-start.2
  27.1 2.9 %collective-permute-done = bf16[2,64,768]{2,1,0:T(8,128)(2,1)S(1)} collective-permute-done((bf16[2,64,768]{2,1,0:T(8,128)(2,1)S(1)}, bf16[2,64,768]{2,1,0:T(8,128)(2,1)S(1)}, u32[]{:S(2)}, u32[]{:S(2)}) %collective-permute-start) | collective-permute-done | bytes 196640 | tf_op jit(solution)/shard_map/ppermute | solution.py:42
  30.0 2.4 %collective-permute-done.1 = bf16[2,64,768]{2,1,0:T(8,128)(2,1)S(1)} collective-permute-done((bf16[2,64,768]{2,1,0:T(8,128)(2,1)S(1)}, bf16[2,64,768]{2,1,0:T(8,128)(2,1)S(1)}, u32[]{:S(2)}, u32[]{:S(2)}) %collective-permute-start.1) | collective-permute-done | bytes 196640 | tf_op jit(solution)/shard_map/ppermute | solution.py:42
  32.4 9.6 %collective-permute-done.2 = bf16[2,64,768]{2,1,0:T(8,128)(2,1)S(1)} collective-permute-done((bf16[2,64,768]{2,1,0:T(8,128)(2,1)S(1)}, bf16[2,64,768]{2,1,0:T(8,128)(2,1)S(1)}, u32[]{:S(2)}, u32[]{:S(2)}) %collective-permute-start.2) | collective-permute-done | bytes 196640 | tf_op jit(solution)/shard_map/ppermute | solution.py:42
  42.0 0.1 pad_maximum_fusion.refs_0_
  42.1 0.1 collective-permute-start.3
  42.2 0.9 collective-permute-start.4
  43.1 3.2 %collective-permute-start.5 = (bf16[4,2,64,768]{3,2,1,0:T(8,128)(2,1)S(1)}, bf16[4,2,64,768]{3,2,1,0:T(8,128)(2,1)S(1)}, u32[]{:S(2)}, u32[]{:S(2)}) collective-permute-start(bf16[4,2,64,768]{3,2,1,0:T(8,128)(2,1)S(1)} %pad_maximum_fusion.refs_0_), channel_id=1, source_target_pairs={{0,6},{1,25},{2,4},{3,27},{4,2},{5,29},{6,0},{7,31},{8,14},{9,17},... | collective-permute-start | bytes 2359304 | tf_op jit(solution)/shard_map/ppermute | solution.py:42
  46.3 9.5 %collective-permute-done.3.refs_3_ = bf16[4,2,64,768]{3,2,1,0:T(8,128)(2,1)S(1)} collective-permute-done((bf16[4,2,64,768]{3,2,1,0:T(8,128)(2,1)S(1)}, bf16[4,2,64,768]{3,2,1,0:T(8,128)(2,1)S(1)}, u32[]{:S(2)}, u32[]{:S(2)}) %collective-permute-start.3) | collective-permute-done | bytes 786464 | tf_op jit(solution)/shard_map/ppermute | solution.py:42
  55.8 5.7 %collective-permute-done.4.refs_1_ = bf16[4,2,64,768]{3,2,1,0:T(8,128)(2,1)S(1)} collective-permute-done((bf16[4,2,64,768]{3,2,1,0:T(8,128)(2,1)S(1)}, bf16[4,2,64,768]{3,2,1,0:T(8,128)(2,1)S(1)}, u32[]{:S(2)}, u32[]{:S(2)}) %collective-permute-start.4) | collective-permute-done | bytes 786464 | tf_op jit(solution)/shard_map/ppermute | solution.py:42
  61.4 2.6 %collective-permute-done.5.refs_2_ = bf16[4,2,64,768]{3,2,1,0:T(8,128)(2,1)S(1)} collective-permute-done((bf16[4,2,64,768]{3,2,1,0:T(8,128)(2,1)S(1)}, bf16[4,2,64,768]{3,2,1,0:T(8,128)(2,1)S(1)}, u32[]{:S(2)}, u32[]{:S(2)}) %collective-permute-start.5) | collective-permute-done | bytes 786464 | tf_op jit(solution)/shard_map/ppermute | solution.py:42
  64.1 0.5 collective-permute-start.7
  64.6 0.5 collective-permute-start.9
  65.1 4.6 %own.1.refs_7_ = f32[1056,256]{1,0:T(8,128)S(1)} custom-call(s32[5]{0:T(128)S(1)} %get-tuple-element.57.info, bf16[4,2,64,768]{3,2,1,0:T(8,128)(2,1)S(1)} %pad_maximum_fusion.refs_0_, bf16[4,2,64,768]{3,2,1,0:T(8,128)(2,1)S(1)} %collective-permute-done.4.refs_1_, bf16[4,2,64,768]{3,2,1,0:T(8,128)(2,1)S(1)} %collective-permute-done.5.refs_2_, ...), custom_call_target="tpu_custom_call" | custom-call | flops 1660944384 | bytes 7340032 | tf_op jit(solution)/shard_map/own/pallas_call | solution.py:187
  69.7 0.2 collective-permute-done.9.refs_3_
  69.9 8.9 %other.1 = (bf16[4,4,2,64,768]{4,3,2,1,0:T(8,128)(2,1)S(1)}, bf16[256,352]{1,0:T(8,128)(2,1)S(1)}, bf16[256,704]{1,0:T(8,128)(2,1)S(1)}) custom-call(s32[5]{0:T(128)S(1)} %get-tuple-element.56.info, bf16[4,2,64,768]{3,2,1,0:T(8,128)(2,1)} %collective-permute-done.6.refs_0_, bf16[4,2,64,768]{3,2,1,0:T(8,128)(2,1)} %collective-permute-done.7.refs_1_, ...), custom_call_target="tpu_custom_call" | custom-call | flops 3321888768 | bytes 7340032 | tf_op jit(solution)/shard_map/other/pallas_call | solution.py:187
  78.8 0.2 collective-permute-start.10
  79.0 4.8 %last.1 = bf16[4,4,2,64,768]{4,3,2,1,0:T(8,128)(2,1)S(1)} custom-call(s32[5]{0:T(128)S(1)} %get-tuple-element.57.info, bf16[256,352]{1,0:T(8,128)(2,1)S(1)} %get-tuple-element.39.refs_0_, bf16[256,704]{1,0:T(8,128)(2,1)S(1)} %get-tuple-element.40.refs_1_, bf16[352,6144]{1,0:T(8,128)(2,1)} %bitcast.68, bf16[352,6144]{1,0:T(8,128)(2,1)} %bitcast.71, ...), custom_call_target="tpu_custom_call" | custom-call | flops 1660944384 | bytes 7340032 | tf_op jit(solution)/shard_map/last/pallas_call | solution.py:187
  83.8 0.7 collective-permute-done.10
  84.5 1.1 fusion.8
  85.7 1.6 %collective-permute-start.11 = (bf16[4,2,64,768]{3,2,1,0:T(8,128)(2,1)S(1)}, bf16[4,2,64,768]{3,2,1,0:T(8,128)(2,1)S(1)}, u32[]{:S(2)}, u32[]{:S(2)}) collective-permute-start(bf16[4,2,64,768]{3,2,1,0:T(8,128)(2,1)S(1)} %get-tuple-element.43), channel_id=1, source_target_pairs={{0,4},{1,17},{2,6},{3,19},{4,0},{5,21},{6,2},{7,23},{8,12},{9,25},... | collective-permute-start | bytes 2359304 | tf_op jit(solution)/shard_map/ppermute | solution.py:42
  87.2 2.6 %collective-permute-start.13 = (bf16[4,2,64,768]{3,2,1,0:T(8,128)(2,1)S(1)}, bf16[4,2,64,768]{3,2,1,0:T(8,128)(2,1)S(1)}, u32[]{:S(2)}, u32[]{:S(2)}) collective-permute-start(bf16[4,2,64,768]{3,2,1,0:T(8,128)(2,1)S(1)} %get-tuple-element.45), channel_id=1, source_target_pairs={{0,6},{1,25},{2,4},{3,27},{4,2},{5,29},{6,0},{7,31},{8,14},{9,17},... | collective-permute-start | bytes 2359304 | tf_op jit(solution)/shard_map/ppermute | solution.py:42
  89.8 9.5 %collective-permute-done.11 = bf16[4,2,64,768]{3,2,1,0:T(8,128)(2,1)S(1)} collective-permute-done((bf16[4,2,64,768]{3,2,1,0:T(8,128)(2,1)S(1)}, bf16[4,2,64,768]{3,2,1,0:T(8,128)(2,1)S(1)}, u32[]{:S(2)}, u32[]{:S(2)}) %collective-permute-start.11) | collective-permute-done | bytes 786464 | tf_op jit(solution)/shard_map/ppermute | solution.py:42
  99.3 6.3 %collective-permute-done.12 = bf16[4,2,64,768]{3,2,1,0:T(8,128)(2,1)S(1)} collective-permute-done((bf16[4,2,64,768]{3,2,1,0:T(8,128)(2,1)S(1)}, bf16[4,2,64,768]{3,2,1,0:T(8,128)(2,1)S(1)}, u32[]{:S(2)}, u32[]{:S(2)}) %collective-permute-start.12) | collective-permute-done | bytes 786464 | tf_op jit(solution)/shard_map/ppermute | solution.py:42
  105.6 2.0 %collective-permute-done.13 = bf16[4,2,64,768]{3,2,1,0:T(8,128)(2,1)S(1)} collective-permute-done((bf16[4,2,64,768]{3,2,1,0:T(8,128)(2,1)S(1)}, bf16[4,2,64,768]{3,2,1,0:T(8,128)(2,1)S(1)}, u32[]{:S(2)}, u32[]{:S(2)}) %collective-permute-start.13) | collective-permute-done | bytes 786464 | tf_op jit(solution)/shard_map/ppermute | solution.py:42
  107.7 0.4 add_convert_fusion
  108.1 0.1 slice_bitcast_fusion
  108.2 0.1 collective-permute-start.14
  108.3 0.1 collective-permute-start.15
  108.4 4.0 %collective-permute-start.16 = (bf16[2,64,768]{2,1,0:T(8,128)(2,1)S(1)}, bf16[2,64,768]{2,1,0:T(8,128)(2,1)S(1)}, u32[]{:S(2)}, u32[]{:S(2)}) collective-permute-start(bf16[2,64,768]{2,1,0:T(8,128)(2,1)S(1)} %get-tuple-element.52), channel_id=1, source_target_pairs={{0,24},{1,7},{2,26},{3,5},{4,28},{5,3},{6,30},{7,1},{8,16},{9,15},... | collective-permute-start | bytes 589832 | tf_op jit(solution)/shard_map/ppermute | solution.py:42
  112.3 3.2 %collective-permute-done.14 = bf16[2,64,768]{2,1,0:T(8,128)(2,1)S(1)} collective-permute-done((bf16[2,64,768]{2,1,0:T(8,128)(2,1)S(1)}, bf16[2,64,768]{2,1,0:T(8,128)(2,1)S(1)}, u32[]{:S(2)}, u32[]{:S(2)}) %collective-permute-start.14) | collective-permute-done | bytes 196640 | tf_op jit(solution)/shard_map/ppermute | solution.py:42
  115.5 2.0 %collective-permute-done.16 = bf16[2,64,768]{2,1,0:T(8,128)(2,1)S(1)} collective-permute-done((bf16[2,64,768]{2,1,0:T(8,128)(2,1)S(1)}, bf16[2,64,768]{2,1,0:T(8,128)(2,1)S(1)}, u32[]{:S(2)}, u32[]{:S(2)}) %collective-permute-start.16) | collective-permute-done | bytes 196640 | tf_op jit(solution)/shard_map/ppermute | solution.py:42
  117.5 0.1 copy_bitcast_fusion
  117.6 12.2 %all_to_all.11 = bf16[8,16,768]{2,1,0:T(8,128)(2,1)S(1)} all-to-all(bf16[8,16,768]{2,1,0:T(8,128)(2,1)S(1)} %copy_bitcast_fusion), channel_id=1, replica_groups={{0,32,64,96,128,160,192,224},{8,40,72,104,136,168,200,232},{16,48,80,11..., dimensions={0} | all-to-all | bytes 393216 | tf_op jit(solution)/shard_map/all_to_all | solution.py:22
  129.8 0.8 fusion.3
  130.6 0.8 fusion.4
  (14 shorter events, 0.1 us)
Async XLA Ops:
  0.6 2.1 %copy-start = (bf16[16,768]{1,0:T(8,128)(2,1)S(1)}, bf16[16,768]{1,0:T(8,128)(2,1)}, u32[]{:S(2)}) copy-start(bf16[16,768]{1,0:T(8,128)(2,1)} %param.7) | copy-start | bytes 73732
  22.7 7.3 %collective-permute-start = (bf16[2,64,768]{2,1,0:T(8,128)(2,1)S(1)}, bf16[2,64,768]{2,1,0:T(8,128)(2,1)S(1)}, u32[]{:S(2)}, u32[]{:S(2)}) collective-permute-start(bf16[2,64,768]{2,1,0:T(8,128)(2,1)S(1)} %get-tuple-element.67), channel_id=1, source_target_pairs={{0,16},{1,5},{2,18},{3,7},{4,20},{5,1},{6,22},{7,3},{8,24},{9,13},... | collective-permute-start | bytes 589832 | tf_op jit(solution)/shard_map/ppermute | solution.py:42
  26.0 6.4 %collective-permute-start.1 = (bf16[2,64,768]{2,1,0:T(8,128)(2,1)S(1)}, bf16[2,64,768]{2,1,0:T(8,128)(2,1)S(1)}, u32[]{:S(2)}, u32[]{:S(2)}) collective-permute-start(bf16[2,64,768]{2,1,0:T(8,128)(2,1)S(1)} %get-tuple-element.67), channel_id=1, source_target_pairs={{0,8},{1,3},{2,10},{3,1},{4,12},{5,7},{6,14},{7,5},{8,0},{9,11},{1... | collective-permute-start | bytes 589832 | tf_op jit(solution)/shard_map/ppermute | solution.py:42
  26.7 15.3 %collective-permute-start.2 = (bf16[2,64,768]{2,1,0:T(8,128)(2,1)S(1)}, bf16[2,64,768]{2,1,0:T(8,128)(2,1)S(1)}, u32[]{:S(2)}, u32[]{:S(2)}) collective-permute-start(bf16[2,64,768]{2,1,0:T(8,128)(2,1)S(1)} %get-tuple-element.67), channel_id=1, source_target_pairs={{0,24},{1,7},{2,26},{3,5},{4,28},{5,3},{6,30},{7,1},{8,16},{9,15},... | collective-permute-start | bytes 589832 | tf_op jit(solution)/shard_map/ppermute | solution.py:42
  42.1 13.7 %collective-permute-start.3 = (bf16[4,2,64,768]{3,2,1,0:T(8,128)(2,1)S(1)}, bf16[4,2,64,768]{3,2,1,0:T(8,128)(2,1)S(1)}, u32[]{:S(2)}, u32[]{:S(2)}) collective-permute-start(bf16[4,2,64,768]{3,2,1,0:T(8,128)(2,1)S(1)} %pad_maximum_fusion.refs_0_), channel_id=1, source_target_pairs={{0,4},{1,17},{2,6},{3,19},{4,0},{5,21},{6,2},{7,23},{8,12},{9,25},... | collective-permute-start | bytes 2359304 | tf_op jit(solution)/shard_map/ppermute | solution.py:42
  42.2 19.3 %collective-permute-start.4 = (bf16[4,2,64,768]{3,2,1,0:T(8,128)(2,1)S(1)}, bf16[4,2,64,768]{3,2,1,0:T(8,128)(2,1)S(1)}, u32[]{:S(2)}, u32[]{:S(2)}) collective-permute-start(bf16[4,2,64,768]{3,2,1,0:T(8,128)(2,1)S(1)} %pad_maximum_fusion.refs_0_), channel_id=1, source_target_pairs={{0,2},{1,9},{2,0},{3,11},{4,6},{5,13},{6,4},{7,15},{8,10},{9,1},{1... | collective-permute-start | bytes 2359304 | tf_op jit(solution)/shard_map/ppermute | solution.py:42
  43.1 21.0 %collective-permute-start.5 = (bf16[4,2,64,768]{3,2,1,0:T(8,128)(2,1)S(1)}, bf16[4,2,64,768]{3,2,1,0:T(8,128)(2,1)S(1)}, u32[]{:S(2)}, u32[]{:S(2)}) collective-permute-start(bf16[4,2,64,768]{3,2,1,0:T(8,128)(2,1)S(1)} %pad_maximum_fusion.refs_0_), channel_id=1, source_target_pairs={{0,6},{1,25},{2,4},{3,27},{4,2},{5,29},{6,0},{7,31},{8,14},{9,17},... | collective-permute-start | bytes 2359304 | tf_op jit(solution)/shard_map/ppermute | solution.py:42
  64.1 5.6 %collective-permute-start.6 = (bf16[4,2,64,768]{3,2,1,0:T(8,128)(2,1)S(1)}, bf16[4,2,64,768]{3,2,1,0:T(8,128)(2,1)}, u32[]{:S(2)}, u32[]{:S(2)}) collective-permute-start(bf16[4,2,64,768]{3,2,1,0:T(8,128)(2,1)S(1)} %pad_maximum_fusion.refs_0_), channel_id=1, source_target_pairs={{0,1},{1,0},{2,3},{3,2},{4,5},{5,4},{6,7},{7,6},{8,9},{9,8},{10,11... | collective-permute-start | bytes 2359304 | tf_op jit(solution)/shard_map/ppermute | solution.py:46
  64.1 5.6 %collective-permute-start.7 = (bf16[4,2,64,768]{3,2,1,0:T(8,128)(2,1)S(1)}, bf16[4,2,64,768]{3,2,1,0:T(8,128)(2,1)}, u32[]{:S(2)}, u32[]{:S(2)}) collective-permute-start(bf16[4,2,64,768]{3,2,1,0:T(8,128)(2,1)S(1)} %collective-permute-done.4.refs_1_), channel_id=1, source_target_pairs={{0,1},{1,0},{2,3},{3,2},{4,5},{5,4},{6,7},{7,6},{8,9},{9,8},{10,11... | collective-permute-start | bytes 2359304 | tf_op jit(solution)/shard_map/ppermute | solution.py:46
  64.6 5.1 %collective-permute-start.8 = (bf16[4,2,64,768]{3,2,1,0:T(8,128)(2,1)S(1)}, bf16[4,2,64,768]{3,2,1,0:T(8,128)(2,1)}, u32[]{:S(2)}, u32[]{:S(2)}) collective-permute-start(bf16[4,2,64,768]{3,2,1,0:T(8,128)(2,1)S(1)} %collective-permute-done.5.refs_2_), channel_id=1, source_target_pairs={{0,1},{1,0},{2,3},{3,2},{4,5},{5,4},{6,7},{7,6},{8,9},{9,8},{10,11... | collective-permute-start | bytes 2359304 | tf_op jit(solution)/shard_map/ppermute | solution.py:46
  64.6 5.3 %collective-permute-start.9 = (bf16[4,2,64,768]{3,2,1,0:T(8,128)(2,1)S(1)}, bf16[4,2,64,768]{3,2,1,0:T(8,128)(2,1)}, u32[]{:S(2)}, u32[]{:S(2)}) collective-permute-start(bf16[4,2,64,768]{3,2,1,0:T(8,128)(2,1)S(1)} %collective-permute-done.3.refs_3_), channel_id=1, source_target_pairs={{0,1},{1,0},{2,3},{3,2},{4,5},{5,4},{6,7},{7,6},{8,9},{9,8},{10,11... | collective-permute-start | bytes 2359304 | tf_op jit(solution)/shard_map/ppermute | solution.py:46
  78.8 5.7 %collective-permute-start.10 = (bf16[4,4,2,64,768]{4,3,2,1,0:T(8,128)(2,1)S(1)}, bf16[4,4,2,64,768]{4,3,2,1,0:T(8,128)(2,1)S(1)}, u32[]{:S(2)}, u32[]{:S(2)}) collective-permute-start(bf16[4,4,2,64,768]{4,3,2,1,0:T(8,128)(2,1)S(1)} %get-tuple-element.41), channel_id=1, source_target_pairs={{0,1},{1,0},{2,3},{3,2},{4,5},{5,4},{6,7},{7,6},{8,9},{9,8},{10,11... | collective-permute-start | bytes 9437192 | tf_op jit(solution)/shard_map/ppermute | solution.py:46
  85.7 13.7 %collective-permute-start.11 = (bf16[4,2,64,768]{3,2,1,0:T(8,128)(2,1)S(1)}, bf16[4,2,64,768]{3,2,1,0:T(8,128)(2,1)S(1)}, u32[]{:S(2)}, u32[]{:S(2)}) collective-permute-start(bf16[4,2,64,768]{3,2,1,0:T(8,128)(2,1)S(1)} %get-tuple-element.43), channel_id=1, source_target_pairs={{0,4},{1,17},{2,6},{3,19},{4,0},{5,21},{6,2},{7,23},{8,12},{9,25},... | collective-permute-start | bytes 2359304 | tf_op jit(solution)/shard_map/ppermute | solution.py:42
  87.2 18.4 %collective-permute-start.12 = (bf16[4,2,64,768]{3,2,1,0:T(8,128)(2,1)S(1)}, bf16[4,2,64,768]{3,2,1,0:T(8,128)(2,1)S(1)}, u32[]{:S(2)}, u32[]{:S(2)}) collective-permute-start(bf16[4,2,64,768]{3,2,1,0:T(8,128)(2,1)S(1)} %get-tuple-element.44), channel_id=1, source_target_pairs={{0,2},{1,9},{2,0},{3,11},{4,6},{5,13},{6,4},{7,15},{8,10},{9,1},{1... | collective-permute-start | bytes 2359304 | tf_op jit(solution)/shard_map/ppermute | solution.py:42
  87.2 20.4 %collective-permute-start.13 = (bf16[4,2,64,768]{3,2,1,0:T(8,128)(2,1)S(1)}, bf16[4,2,64,768]{3,2,1,0:T(8,128)(2,1)S(1)}, u32[]{:S(2)}, u32[]{:S(2)}) collective-permute-start(bf16[4,2,64,768]{3,2,1,0:T(8,128)(2,1)S(1)} %get-tuple-element.45), channel_id=1, source_target_pairs={{0,6},{1,25},{2,4},{3,27},{4,2},{5,29},{6,0},{7,31},{8,14},{9,17},... | collective-permute-start | bytes 2359304 | tf_op jit(solution)/shard_map/ppermute | solution.py:42
  108.2 7.4 %collective-permute-start.14 = (bf16[2,64,768]{2,1,0:T(8,128)(2,1)S(1)}, bf16[2,64,768]{2,1,0:T(8,128)(2,1)S(1)}, u32[]{:S(2)}, u32[]{:S(2)}) collective-permute-start(bf16[2,64,768]{2,1,0:T(8,128)(2,1)S(1)} %get-tuple-element.50), channel_id=1, source_target_pairs={{0,16},{1,5},{2,18},{3,7},{4,20},{5,1},{6,22},{7,3},{8,24},{9,13},... | collective-permute-start | bytes 589832 | tf_op jit(solution)/shard_map/ppermute | solution.py:42
  108.3 7.3 %collective-permute-start.15 = (bf16[2,64,768]{2,1,0:T(8,128)(2,1)S(1)}, bf16[2,64,768]{2,1,0:T(8,128)(2,1)S(1)}, u32[]{:S(2)}, u32[]{:S(2)}) collective-permute-start(bf16[2,64,768]{2,1,0:T(8,128)(2,1)S(1)} %get-tuple-element.51), channel_id=1, source_target_pairs={{0,8},{1,3},{2,10},{3,1},{4,12},{5,7},{6,14},{7,5},{8,0},{9,11},{1... | collective-permute-start | bytes 589832 | tf_op jit(solution)/shard_map/ppermute | solution.py:42
  108.4 9.2 %collective-permute-start.16 = (bf16[2,64,768]{2,1,0:T(8,128)(2,1)S(1)}, bf16[2,64,768]{2,1,0:T(8,128)(2,1)S(1)}, u32[]{:S(2)}, u32[]{:S(2)}) collective-permute-start(bf16[2,64,768]{2,1,0:T(8,128)(2,1)S(1)} %get-tuple-element.52), channel_id=1, source_target_pairs={{0,24},{1,7},{2,26},{3,5},{4,28},{5,3},{6,30},{7,1},{8,16},{9,15},... | collective-permute-start | bytes 589832 | tf_op jit(solution)/shard_map/ppermute | solution.py:42

commit v3 on v2

--- a/solution.py
+++ b/solution.py
@@ -14,7 +14,7 @@
 BF = jnp.bfloat16
 F32 = jnp.float32
 NT = (((1,), (1,)), ((), ()))
-VMEM_LIMIT = {"own": 20, "other": 24, "last": 16}
+VMEM_LIMIT = {"own": 8, "other": 12, "last": 4}
 
 
 def swap_z(v):
@@ -83,24 +83,41 @@
     return add(parts[0], *got)
 
 
-def fetch_weights(info, weights, buf, sem):
-    hidden, width = weights[0].shape[0], buf.shape[-1]
-
-    def copy(i, k, at):
-        rows = pl.ds(i * hidden, hidden)
-        return pltpu.make_async_copy(
-            weights[i].at[:, pl.ds(at, width)], buf.at[k, rows], sem.at[k, i]
-        )
-
-    for k in range(NX):
-        for i in range(3):
-            copy(i, k, pl.multiple_of(info[k] * width, 128)).start()
-
-    def wait(k):
-        for i in range(3):
-            copy(i, k, 0).wait()
-
-    return wait
+def weights_kernel(infos, *refs):
+    weights, bufs, sem = refs[:3], refs[3:5], refs[5]
+    hidden, width = weights[0].shape[0], bufs[0].shape[-1]
+    copies = []
+    for core in range(2):
+        for k in range(NX):
+            at = pl.ds(pl.multiple_of(infos[core, k] * width, 128), width)
+            for i in range(3):
+                to = bufs[core].at[k, pl.ds(i * hidden, hidden)]
+                copies.append(
+                    pltpu.make_async_copy(
+                        weights[i].at[:, at], to, sem.at[core, k, i]
+                    )
+                )
+    for copy in copies:
+        copy.start()
+    for copy in copies:
+        copy.wait()
+
+
+def load_weights(infos, weights, width):
+    hidden = weights[0].shape[0]
+    return pl.pallas_call(
+        weights_kernel,
+        name="weights",
+        out_shape=[jax.ShapeDtypeStruct((NX, 3 * hidden, width), BF)] * 2,
+        in_specs=[pl.BlockSpec(memory_space=pltpu.SMEM)]
+        + [pl.BlockSpec(memory_space=pltpu.HBM)] * 3,
+        out_specs=[pl.BlockSpec(memory_space=pltpu.VMEM)] * 2,
+        scratch_shapes=[pltpu.SemaphoreType.DMA((2, NX, 3))],
+        compiler_params=pltpu.CompilerParams(vmem_limit_bytes=4 << 20),
+        cost_estimate=pl.CostEstimate(
+            flops=0, bytes_accessed=26 << 20, transcendentals=0
+        ),
+    )(infos, *weights)
 
 
 def order(info, b, a):
@@ -118,12 +135,11 @@
                 rows[k, i, at] = pieces[b][a, i]
 
 
-def contract(wait, rows, buf, acc):
+def contract(rows, buf, acc):
     two = acc.shape[0] // 3 * 2
 
     @pl.loop(0, NX)
     def _(k):
-        wait(k)
         acc[:two] += lax.dot_general(
             buf[k, :two], rows[k, 0], NT, preferred_element_type=F32
         )
@@ -132,7 +148,7 @@
         )
 
 
-def expand(info, wait, hidden, grads, buf, out):
+def expand(info, hidden, grads, buf, out):
     step = hidden.shape[0] // NY
     two = grads.shape[1]
 
@@ -143,8 +159,6 @@
 
     @pl.loop(0, NX)
     def _(k):
-        if wait is not None:
-            wait(k)
         o = jnp.dot(hidden[...], buf[k, two:], preferred_element_type=F32)
         put(k, 0, o.astype(BF))
         o = jnp.dot(grads[...], buf[k, :two], preferred_element_type=F32)
@@ -152,59 +166,47 @@
 
 
 def own_kernel(info, *refs):
-    pieces, weights, (acc, rows, buf, sem) = refs[:4], refs[4:7], refs[7:]
-    wait = fetch_weights(info, weights, buf, sem)
+    pieces, (buf, acc, rows) = refs[:4], refs[4:]
     load_rows(info, pieces, rows)
     acc[...] = jnp.zeros_like(acc)
-    contract(wait, rows, buf, acc)
+    contract(rows, buf, acc)
 
 
 def other_kernel(info, *refs):
-    pieces, weights, partial, rest = refs[:4], refs[4:7], refs[7], refs[8:]
-    out, hidden, grads, rows, acc, buf, sem = rest
-    wait = fetch_weights(info, weights, buf, sem)
+    pieces, (buf, partial, out, hidden, grads, rows, acc) = refs[:4], refs[4:]
     load_rows(info, pieces, rows)
     acc[...] = partial[...]
-    contract(wait, rows, buf, acc)
+    contract(rows, buf, acc)
     one = acc.shape[0] // 3
     g, u, h = acc[:one], acc[one : 2 * one], acc[2 * one :]
     sigma = jax.nn.sigmoid(g)
     hidden[...] = (g * sigma * u).T.astype(BF)
     gate_grad = h * u * sigma * (1.0 + g * (1.0 - sigma))
     grads[...] = jnp.concatenate([gate_grad, h * g * sigma], axis=0).T.astype(BF)
-    expand(info, None, hidden, grads, buf, out)
-
-
-def last_kernel(info, *refs):
-    (hidden, grads), weights, (out, buf, sem) = refs[:2], refs[2:5], refs[5:]
-    wait = fetch_weights(info, weights, buf, sem)
-    expand(info, wait, hidden, grads, buf, out)
-
-
-def call(body, name, info, arrays, weights, partial, out, scratch, products):
-    hidden, width = weights[0].shape[0], weights[0].shape[1] // (2 * NX)
-    rows = E * CAP * NY
+    expand(info, hidden, grads, buf, out)
+
+
+def last_kernel(info, hidden, grads, buf, out):
+    expand(info, hidden, grads, buf, out)
+
+
+def call(body, name, info, arrays, out, scratch, products, shape):
+    rows, hidden, width = shape
     return pl.pallas_call(
         body,
         name=name,
         out_shape=out,
         in_specs=[pl.BlockSpec(memory_space=pltpu.SMEM)]
-        + [pl.BlockSpec(memory_space=pltpu.VMEM)] * len(arrays)
-        + [pl.BlockSpec(memory_space=pltpu.HBM)] * 3
-        + [pl.BlockSpec(memory_space=pltpu.VMEM)] * len(partial),
+        + [pl.BlockSpec(memory_space=pltpu.VMEM)] * len(arrays),
         out_specs=[pl.BlockSpec(memory_space=pltpu.VMEM)] * len(out),
-        scratch_shapes=scratch
-        + [
-            pltpu.VMEM((NX, 3 * hidden, width), BF),
-            pltpu.SemaphoreType.DMA((NX, 3)),
-        ],
+        scratch_shapes=scratch,
         compiler_params=pltpu.CompilerParams(vmem_limit_bytes=VMEM_LIMIT[name] << 20),
         cost_estimate=pl.CostEstimate(
             flops=2 * products * rows * width * NX * hidden,
             bytes_accessed=7 << 20,
             transcendentals=0,
         ),
-    )(info, *arrays, *weights, *partial)
+    )(info, *arrays)
 
 
 def on_device(tokens, out_grad, gate_values, routing, gate_weight, up_weight, down_weight):
@@ -234,11 +236,15 @@
     got = swap_z(send).reshape(E, 2, CAP, width)
     got = jnp.swapaxes(got, 0, 1).reshape(2, E * CAP, width)
 
-    own = gather(jnp.stack(gather(got, 0)), 1)
-    own = list(lax.optimization_barrier(tuple(own)))
+    parts = gather(got, 0)
+    token = to_core(parts[3][0, :8, :128])[0, 0]
+    near = jnp.where(token == token, jnp.stack(parts), jnp.zeros((), BF))
+    weights = [pltpu.with_memory_space_constraint(w, pltpu.HBM) for w in (wg, wu, w2)]
+    infos, near = lax.optimization_barrier((jnp.stack([own_info, other_info]), near))
+    bufs = load_weights(infos, weights, width)
+    own, bufs = lax.optimization_barrier((tuple(gather(near, 1)), tuple(bufs)))
     other = [to_core(v) for v in own]
 
-    weights = [pltpu.with_memory_space_constraint(w, pltpu.HBM) for w in (wg, wu, w2)]
     pre = jax.ShapeDtypeStruct((3 * hidden, rows), F32)
     act = [
         jax.ShapeDtypeStruct((rows, hidden), BF),
@@ -247,12 +253,17 @@
     pieces = [jax.ShapeDtypeStruct((4, 4, 2, rows // 4, width), BF)]
     row_buf = [pltpu.VMEM((NX, 2, rows, width), BF)]
     acc_buf = [pltpu.VMEM(pre.shape, F32)]
-    partial = call(own_kernel, "own", own_info, own, weights, [], [pre], row_buf, 3)
+    shape = rows, hidden, width
+    (partial,) = call(
+        own_kernel, "own", own_info, [*own, bufs[0]], [pre], row_buf, 3, shape
+    )
     far, *act = call(
-        other_kernel, "other", other_info, other, weights, partial,
-        pieces + act, row_buf + acc_buf, 6,
-    )
-    (near,) = call(last_kernel, "last", own_info, act, weights, [], pieces, [], 3)
+        other_kernel, "other", other_info, [*other, bufs[1], partial],
+        pieces + act, row_buf + acc_buf, 6, shape,
+    )
+    (near,) = call(
+        last_kernel, "last", own_info, [*act, bufs[0]], pieces, [], 3, shape
+    )
     got = to_core(far)
     sums = scatter([add(near[b], got[b]) for b in range(4)], 1)
     back = scatter([sums[a] for a in range(4)], 0)

time: 132 us -> 126 us (0.955)
  waiting for transfers between devices: 56.6 us -> 47.4 us
  starting transfers between devices: 18.1 us -> 19.7 us
    ppermute x12, waiting for transfers between devices: 55.8 us -> 42.7 us  [swap(): return lax.ppermute(v, ('dp', 'cuts'), perm)]
    pallas_call x0 -> x1, Pallas kernels: none -> 5.52 us  [load_weights(): pl.pallas_call(weights_kernel, name='weights', out_shape=[jax.ShapeDtypeS...]
    pallas_call x3, Pallas kernels: 18.2 us -> 13 us  [call(): pl.pallas_call(body, name=name, out_shape=out, in_specs=[pl.BlockSpec(mem...]
    ppermute x5 -> x6, waiting for transfers between devices: 0.88 us -> 4.65 us  [to_core(): return lax.ppermute(v, 'cuts', [(i, i ^ 1) for i in range(2 * NX)])]
    ppermute x12, starting transfers between devices: 16.9 us -> 18.5 us  [swap(): return lax.ppermute(v, ('dp', 'cuts'), perm)]
  transfers between devices with their start and end apart: 17 -> 18, of which waited for: 13 -> 15; matrix products, arithmetic and copies ran while one was open for 0% -> 0% of each run, Pallas kernels for 7% -> 10%
where the time goes in v3:
time: 126 us
  waiting for transfers between devices  47.4 us (38%)
  blocking collectives  30.9 us (25%)
  starting transfers between devices  19.7 us (16%)
  Pallas kernels  18.5 us (15%)
  other arithmetic  3.7 us (3%)
  matrix products  2.83 us (2%)
  between operations  2.07 us (2%)
    ppermute x12, waiting for transfers between devices, swap(): return lax.ppermute(v, ('dp', 'cuts'), perm)  42.7 us
    all_to_all x2, blocking collectives, swap_z(): return lax.all_to_all(v, 'dp', 0, 0, axis_index_groups=groups, tiled=True)  30.9 us
    ppermute x12, starting transfers between devices, swap(): return lax.ppermute(v, ('dp', 'cuts'), perm)  18.5 us
    pallas_call x3, Pallas kernels, call(): pl.pallas_call(body, name=name, out_shape=out, in_specs=[pl.BlockSpec(mem...  13 us
    pallas_call x1, Pallas kernels, load_weights(): pl.pallas_call(weights_kernel, name='weights', out_shape=[jax.ShapeDtypeS...  5.52 us
    ppermute x6, waiting for transfers between devices, to_core(): return lax.ppermute(v, 'cuts', [(i, i ^ 1) for i in range(2 * NX)])  4.65 us
  transfers between devices with their start and end apart: 18, of which 15 were waited for; matrix products, arithmetic and copies ran while one was open for 0% of the time, Pallas kernels for 10%

profile of v3, /device:TPU:6, one launch (start us, length us, event | category | flops | bytes accessed | tf_op | source)
XLA Modules:
  0.0 125.9 jit_solution(15780467819831150188)
XLA Ops:
  0.7 0.7 fusion.31
  1.3 0.7 select_reduce_fusion.2
  2.1 0.4 select_reduce_fusion
  2.7 0.2 fusion.2
  3.0 1.0 fusion.1
  3.9 18.7 %all_to_all.10 = bf16[8,16,768]{2,1,0:T(8,128)(2,1)S(1)} all-to-all(bf16[8,16,768]{2,1,0:T(8,128)(2,1)S(1)} %pad_maximum_fusion), channel_id=1, replica_groups={{0,32,64,96,128,160,192,224},{8,40,72,104,136,168,200,232},{16,48,80,11..., dimensions={0} | all-to-all | bytes 393216 | tf_op jit(solution)/shard_map/all_to_all | solution.py:22
  22.7 3.1 %collective-permute-start.2 = (bf16[2,64,768]{2,1,0:T(8,128)(2,1)S(1)}, bf16[2,64,768]{2,1,0:T(8,128)(2,1)S(1)}, u32[]{:S(2)}, u32[]{:S(2)}) collective-permute-start(bf16[2,64,768]{2,1,0:T(8,128)(2,1)S(1)} %get-tuple-element.81), channel_id=1, source_target_pairs={{0,24},{1,7},{2,26},{3,5},{4,28},{5,3},{6,30},{7,1},{8,16},{9,15},... | collective-permute-start | bytes 589832 | tf_op jit(solution)/shard_map/ppermute | solution.py:42
  25.8 0.1 collective-permute-start.1
  26.0 1.5 %collective-permute-start = (bf16[2,64,768]{2,1,0:T(8,128)(2,1)S(1)}, bf16[2,64,768]{2,1,0:T(8,128)(2,1)S(1)}, u32[]{:S(2)}, u32[]{:S(2)}) collective-permute-start(bf16[2,64,768]{2,1,0:T(8,128)(2,1)S(1)} %get-tuple-element.81), channel_id=1, source_target_pairs={{0,16},{1,5},{2,18},{3,7},{4,20},{5,1},{6,22},{7,3},{8,24},{9,13},... | collective-permute-start | bytes 589832 | tf_op jit(solution)/shard_map/ppermute | solution.py:42
  27.5 2.2 %collective-permute-done.2 = bf16[2,64,768]{2,1,0:T(8,128)(2,1)S(1)} collective-permute-done((bf16[2,64,768]{2,1,0:T(8,128)(2,1)S(1)}, bf16[2,64,768]{2,1,0:T(8,128)(2,1)S(1)}, u32[]{:S(2)}, u32[]{:S(2)}) %collective-permute-start.2) | collective-permute-done | bytes 196640 | tf_op jit(solution)/shard_map/ppermute | solution.py:42
  29.7 1.8 %collective-permute-done.1 = bf16[2,64,768]{2,1,0:T(8,128)(2,1)S(1)} collective-permute-done((bf16[2,64,768]{2,1,0:T(8,128)(2,1)S(1)}, bf16[2,64,768]{2,1,0:T(8,128)(2,1)S(1)}, u32[]{:S(2)}, u32[]{:S(2)}) %collective-permute-start.1) | collective-permute-done | bytes 196640 | tf_op jit(solution)/shard_map/ppermute | solution.py:42
  31.5 1.8 %collective-permute-done = bf16[2,64,768]{2,1,0:T(8,128)(2,1)S(1)} collective-permute-done((bf16[2,64,768]{2,1,0:T(8,128)(2,1)S(1)}, bf16[2,64,768]{2,1,0:T(8,128)(2,1)S(1)}, u32[]{:S(2)}, u32[]{:S(2)}) %collective-permute-start) | collective-permute-done | bytes 196640 | tf_op jit(solution)/shard_map/ppermute | solution.py:42
  33.3 1.1 collective-permute-done.3
  34.4 0.5 slice.49
  36.2 0.1 maximum_select_fusion.refs_0_
  36.3 0.6 collective-permute-start.6
  36.9 0.9 collective-permute-start.5
  37.8 3.3 %collective-permute-start.4 = (bf16[4,2,64,768]{3,2,1,0:T(8,128)(2,1)S(1)}, bf16[4,2,64,768]{3,2,1,0:T(8,128)(2,1)S(1)}, u32[]{:S(2)}, u32[]{:S(2)}) collective-permute-start(bf16[4,2,64,768]{3,2,1,0:T(8,128)(2,1)S(1)} %maximum_select_fusion.refs_0_), channel_id=1, source_target_pairs={{0,4},{1,17},{2,6},{3,19},{4,0},{5,21},{6,2},{7,23},{8,12},{9,25},... | collective-permute-start | bytes 2359304 | tf_op jit(solution)/shard_map/ppermute | solution.py:42
  41.1 5.5 %weights.1 = (bf16[4,1056,768]{2,1,0:T(8,128)(2,1)S(1)}, bf16[4,1056,768]{2,1,0:T(8,128)(2,1)S(1)}) custom-call(s32[2,5]{1,0:T(2,128)S(1)} %pad_add_fusion.infos, bf16[352,6144]{1,0:T(8,128)(2,1)} %bitcast.69, bf16[352,6144]{1,0:T(8,128)(2,1)} %bitcast.70, bf16[352,6144]{1,0:T(8,128)(2,1)} %bitcast.71), custom_call_target="tpu_custom_call" | custom-call | bytes 27262976 | tf_op jit(solution)/shard_map/weights/pallas_call | solution.py:108
  46.7 3.0 %collective-permute-done.6.refs_2_ = bf16[4,2,64,768]{3,2,1,0:T(8,128)(2,1)S(1)} collective-permute-done((bf16[4,2,64,768]{3,2,1,0:T(8,128)(2,1)S(1)}, bf16[4,2,64,768]{3,2,1,0:T(8,128)(2,1)S(1)}, u32[]{:S(2)}, u32[]{:S(2)}) %collective-permute-start.6) | collective-permute-done | bytes 786464 | tf_op jit(solution)/shard_map/ppermute | solution.py:42
  49.6 9.9 %collective-permute-done.4.refs_3_ = bf16[4,2,64,768]{3,2,1,0:T(8,128)(2,1)S(1)} collective-permute-done((bf16[4,2,64,768]{3,2,1,0:T(8,128)(2,1)S(1)}, bf16[4,2,64,768]{3,2,1,0:T(8,128)(2,1)S(1)}, u32[]{:S(2)}, u32[]{:S(2)}) %collective-permute-start.4) | collective-permute-done | bytes 786464 | tf_op jit(solution)/shard_map/ppermute | solution.py:42
  59.5 0.5 collective-permute-start.8
  60.0 0.5 collective-permute-start.10
  60.6 3.3 %own.1.refs_5_ = f32[1056,256]{1,0:T(8,128)S(1)} custom-call(s32[5]{0:T(128)S(1)} %get-tuple-element.71.info, bf16[4,2,64,768]{3,2,1,0:T(8,128)(2,1)S(1)} %maximum_select_fusion.refs_0_, bf16[4,2,64,768]{3,2,1,0:T(8,128)(2,1)S(1)} %collective-permute-done.5.refs_1_, bf16[4,2,64,768]{3,2,1,0:T(8,128)(2,1)S(1)} %collective-permute-done.6.refs_2_, ...), custom_call_target="tpu_custom_call" | custom-call | flops 1660944384 | bytes 7340032 | tf_op jit(solution)/shard_map/own/pallas_call | solution.py:195
  63.9 0.1 collective-permute-done.9.refs_2_
  64.1 1.1 collective-permute-done.10.refs_3_
  65.2 6.4 %other.1 = (bf16[4,4,2,64,768]{4,3,2,1,0:T(8,128)(2,1)S(1)}, bf16[256,352]{1,0:T(8,128)(2,1)S(1)}, bf16[256,704]{1,0:T(8,128)(2,1)S(1)}) custom-call(s32[5]{0:T(128)S(1)} %get-tuple-element.70.info, bf16[4,2,64,768]{3,2,1,0:T(8,128)(2,1)S(1)} %collective-permute-done.7.refs_0_, bf16[4,2,64,768]{3,2,1,0:T(8,128)(2,1)S(1)} %collective-permute-done.8.refs_1_, ...), custom_call_target="tpu_custom_call" | custom-call | flops 3321888768 | bytes 7340032 | tf_op jit(solution)/shard_map/other/pallas_call | solution.py:195
  71.6 0.2 collective-permute-start.11
  71.8 3.3 %last.1 = bf16[4,4,2,64,768]{4,3,2,1,0:T(8,128)(2,1)S(1)} custom-call(s32[5]{0:T(128)S(1)} %get-tuple-element.71.info, bf16[256,352]{1,0:T(8,128)(2,1)S(1)} %get-tuple-element.51.hidden, bf16[256,704]{1,0:T(8,128)(2,1)S(1)} %get-tuple-element.52.grads, bf16[4,1056,768]{2,1,0:T(8,128)(2,1)S(1)} %get-tuple-element.50.refs_4_.buf), custom_call_target="tpu_custom_call" | custom-call | flops 1660944384 | bytes 7340032 | tf_op jit(solution)/shard_map/last/pallas_call | solution.py:195
  75.1 2.2 %collective-permute-done.11 = bf16[4,4,2,64,768]{4,3,2,1,0:T(8,128)(2,1)S(1)} collective-permute-done((bf16[4,4,2,64,768]{4,3,2,1,0:T(8,128)(2,1)S(1)}, bf16[4,4,2,64,768]{4,3,2,1,0:T(8,128)(2,1)S(1)}, u32[]{:S(2)}, u32[]{:S(2)}) %collective-permute-start.11) | collective-permute-done | bytes 3145760 | tf_op jit(solution)/shard_map/ppermute | solution.py:46
  77.3 1.2 fusion.8
  78.5 0.5 collective-permute-start.12
  79.0 1.2 collective-permute-start.13
  80.1 2.7 %collective-permute-start.14 = (bf16[4,2,64,768]{3,2,1,0:T(8,128)(2,1)S(1)}, bf16[4,2,64,768]{3,2,1,0:T(8,128)(2,1)S(1)}, u32[]{:S(2)}, u32[]{:S(2)}) collective-permute-start(bf16[4,2,64,768]{3,2,1,0:T(8,128)(2,1)S(1)} %get-tuple-element.57), channel_id=1, source_target_pairs={{0,6},{1,25},{2,4},{3,27},{4,2},{5,29},{6,0},{7,31},{8,14},{9,17},... | collective-permute-start | bytes 2359304 | tf_op jit(solution)/shard_map/ppermute | solution.py:42
  82.9 9.5 %collective-permute-done.12 = bf16[4,2,64,768]{3,2,1,0:T(8,128)(2,1)S(1)} collective-permute-done((bf16[4,2,64,768]{3,2,1,0:T(8,128)(2,1)S(1)}, bf16[4,2,64,768]{3,2,1,0:T(8,128)(2,1)S(1)}, u32[]{:S(2)}, u32[]{:S(2)}) %collective-permute-start.12) | collective-permute-done | bytes 786464 | tf_op jit(solution)/shard_map/ppermute | solution.py:42
  92.4 6.2 %collective-permute-done.13 = bf16[4,2,64,768]{3,2,1,0:T(8,128)(2,1)S(1)} collective-permute-done((bf16[4,2,64,768]{3,2,1,0:T(8,128)(2,1)S(1)}, bf16[4,2,64,768]{3,2,1,0:T(8,128)(2,1)S(1)}, u32[]{:S(2)}, u32[]{:S(2)}) %collective-permute-start.13) | collective-permute-done | bytes 786464 | tf_op jit(solution)/shard_map/ppermute | solution.py:42
  98.5 2.1 %collective-permute-done.14 = bf16[4,2,64,768]{3,2,1,0:T(8,128)(2,1)S(1)} collective-permute-done((bf16[4,2,64,768]{3,2,1,0:T(8,128)(2,1)S(1)}, bf16[4,2,64,768]{3,2,1,0:T(8,128)(2,1)S(1)}, u32[]{:S(2)}, u32[]{:S(2)}) %collective-permute-start.14) | collective-permute-done | bytes 786464 | tf_op jit(solution)/shard_map/ppermute | solution.py:42
  100.7 0.4 add_convert_fusion
  101.2 2.1 %collective-permute-start.15 = (bf16[2,64,768]{2,1,0:T(8,128)(2,1)S(1)}, bf16[2,64,768]{2,1,0:T(8,128)(2,1)S(1)}, u32[]{:S(2)}, u32[]{:S(2)}) collective-permute-start(bf16[2,64,768]{2,1,0:T(8,128)(2,1)S(1)} %get-tuple-element.62), channel_id=1, source_target_pairs={{0,16},{1,5},{2,18},{3,7},{4,20},{5,1},{6,22},{7,3},{8,24},{9,13},... | collective-permute-start | bytes 589832 | tf_op jit(solution)/shard_map/ppermute | solution.py:42
  103.3 1.9 %collective-permute-start.16 = (bf16[2,64,768]{2,1,0:T(8,128)(2,1)S(1)}, bf16[2,64,768]{2,1,0:T(8,128)(2,1)S(1)}, u32[]{:S(2)}, u32[]{:S(2)}) collective-permute-start(bf16[2,64,768]{2,1,0:T(8,128)(2,1)S(1)} %get-tuple-element.63), channel_id=1, source_target_pairs={{0,8},{1,3},{2,10},{3,1},{4,12},{5,7},{6,14},{7,5},{8,0},{9,11},{1... | collective-permute-start | bytes 589832 | tf_op jit(solution)/shard_map/ppermute | solution.py:42
  105.1 0.6 collective-permute-start.17
  105.7 2.7 %collective-permute-done.15 = bf16[2,64,768]{2,1,0:T(8,128)(2,1)S(1)} collective-permute-done((bf16[2,64,768]{2,1,0:T(8,128)(2,1)S(1)}, bf16[2,64,768]{2,1,0:T(8,128)(2,1)S(1)}, u32[]{:S(2)}, u32[]{:S(2)}) %collective-permute-start.15) | collective-permute-done | bytes 196640 | tf_op jit(solution)/shard_map/ppermute | solution.py:42
  108.4 2.5 %collective-permute-done.16 = bf16[2,64,768]{2,1,0:T(8,128)(2,1)S(1)} collective-permute-done((bf16[2,64,768]{2,1,0:T(8,128)(2,1)S(1)}, bf16[2,64,768]{2,1,0:T(8,128)(2,1)S(1)}, u32[]{:S(2)}, u32[]{:S(2)}) %collective-permute-start.16) | collective-permute-done | bytes 196640 | tf_op jit(solution)/shard_map/ppermute | solution.py:42
  110.9 1.1 collective-permute-done.17
  112.0 0.1 copy_bitcast_fusion
  112.1 12.2 %all_to_all.11 = bf16[8,16,768]{2,1,0:T(8,128)(2,1)S(1)} all-to-all(bf16[8,16,768]{2,1,0:T(8,128)(2,1)S(1)} %copy_bitcast_fusion), channel_id=1, replica_groups={{0,32,64,96,128,160,192,224},{8,40,72,104,136,168,200,232},{16,48,80,11..., dimensions={0} | all-to-all | bytes 393216 | tf_op jit(solution)/shard_map/all_to_all | solution.py:22
  124.3 0.8 fusion.3
  125.1 0.8 fusion.4
  (21 shorter events, 0.5 us)
Async XLA Ops:
  0.6 2.1 %copy-start = (bf16[16,768]{1,0:T(8,128)(2,1)S(1)}, bf16[16,768]{1,0:T(8,128)(2,1)}, u32[]{:S(2)}) copy-start(bf16[16,768]{1,0:T(8,128)(2,1)} %param.7) | copy-start | bytes 73732
  22.7 7.0 %collective-permute-start.2 = (bf16[2,64,768]{2,1,0:T(8,128)(2,1)S(1)}, bf16[2,64,768]{2,1,0:T(8,128)(2,1)S(1)}, u32[]{:S(2)}, u32[]{:S(2)}) collective-permute-start(bf16[2,64,768]{2,1,0:T(8,128)(2,1)S(1)} %get-tuple-element.81), channel_id=1, source_target_pairs={{0,24},{1,7},{2,26},{3,5},{4,28},{5,3},{6,30},{7,1},{8,16},{9,15},... | collective-permute-start | bytes 589832 | tf_op jit(solution)/shard_map/ppermute | solution.py:42
  25.8 5.7 %collective-permute-start.1 = (bf16[2,64,768]{2,1,0:T(8,128)(2,1)S(1)}, bf16[2,64,768]{2,1,0:T(8,128)(2,1)S(1)}, u32[]{:S(2)}, u32[]{:S(2)}) collective-permute-start(bf16[2,64,768]{2,1,0:T(8,128)(2,1)S(1)} %get-tuple-element.81), channel_id=1, source_target_pairs={{0,8},{1,3},{2,10},{3,1},{4,12},{5,7},{6,14},{7,5},{8,0},{9,11},{1... | collective-permute-start | bytes 589832 | tf_op jit(solution)/shard_map/ppermute | solution.py:42
  26.0 7.3 %collective-permute-start = (bf16[2,64,768]{2,1,0:T(8,128)(2,1)S(1)}, bf16[2,64,768]{2,1,0:T(8,128)(2,1)S(1)}, u32[]{:S(2)}, u32[]{:S(2)}) collective-permute-start(bf16[2,64,768]{2,1,0:T(8,128)(2,1)S(1)} %get-tuple-element.81), channel_id=1, source_target_pairs={{0,16},{1,5},{2,18},{3,7},{4,20},{5,1},{6,22},{7,3},{8,24},{9,13},... | collective-permute-start | bytes 589832 | tf_op jit(solution)/shard_map/ppermute | solution.py:42
  33.3 1.2 collective-permute-start.3
  36.3 13.3 %collective-permute-start.6 = (bf16[4,2,64,768]{3,2,1,0:T(8,128)(2,1)S(1)}, bf16[4,2,64,768]{3,2,1,0:T(8,128)(2,1)S(1)}, u32[]{:S(2)}, u32[]{:S(2)}) collective-permute-start(bf16[4,2,64,768]{3,2,1,0:T(8,128)(2,1)S(1)} %maximum_select_fusion.refs_0_), channel_id=1, source_target_pairs={{0,6},{1,25},{2,4},{3,27},{4,2},{5,29},{6,0},{7,31},{8,14},{9,17},... | collective-permute-start | bytes 2359304 | tf_op jit(solution)/shard_map/ppermute | solution.py:42
  36.9 12.7 %collective-permute-start.5 = (bf16[4,2,64,768]{3,2,1,0:T(8,128)(2,1)S(1)}, bf16[4,2,64,768]{3,2,1,0:T(8,128)(2,1)S(1)}, u32[]{:S(2)}, u32[]{:S(2)}) collective-permute-start(bf16[4,2,64,768]{3,2,1,0:T(8,128)(2,1)S(1)} %maximum_select_fusion.refs_0_), channel_id=1, source_target_pairs={{0,2},{1,9},{2,0},{3,11},{4,6},{5,13},{6,4},{7,15},{8,10},{9,1},{1... | collective-permute-start | bytes 2359304 | tf_op jit(solution)/shard_map/ppermute | solution.py:42
  37.8 21.7 %collective-permute-start.4 = (bf16[4,2,64,768]{3,2,1,0:T(8,128)(2,1)S(1)}, bf16[4,2,64,768]{3,2,1,0:T(8,128)(2,1)S(1)}, u32[]{:S(2)}, u32[]{:S(2)}) collective-permute-start(bf16[4,2,64,768]{3,2,1,0:T(8,128)(2,1)S(1)} %maximum_select_fusion.refs_0_), channel_id=1, source_target_pairs={{0,4},{1,17},{2,6},{3,19},{4,0},{5,21},{6,2},{7,23},{8,12},{9,25},... | collective-permute-start | bytes 2359304 | tf_op jit(solution)/shard_map/ppermute | solution.py:42
  59.5 4.4 %collective-permute-start.7 = (bf16[4,2,64,768]{3,2,1,0:T(8,128)(2,1)S(1)}, bf16[4,2,64,768]{3,2,1,0:T(8,128)(2,1)S(1)}, u32[]{:S(2)}, u32[]{:S(2)}) collective-permute-start(bf16[4,2,64,768]{3,2,1,0:T(8,128)(2,1)S(1)} %maximum_select_fusion.refs_0_), channel_id=1, source_target_pairs={{0,1},{1,0},{2,3},{3,2},{4,5},{5,4},{6,7},{7,6},{8,9},{9,8},{10,11... | collective-permute-start | bytes 2359304 | tf_op jit(solution)/shard_map/ppermute | solution.py:46
  59.5 4.4 %collective-permute-start.8 = (bf16[4,2,64,768]{3,2,1,0:T(8,128)(2,1)S(1)}, bf16[4,2,64,768]{3,2,1,0:T(8,128)(2,1)S(1)}, u32[]{:S(2)}, u32[]{:S(2)}) collective-permute-start(bf16[4,2,64,768]{3,2,1,0:T(8,128)(2,1)S(1)} %collective-permute-done.5.refs_1_), channel_id=1, source_target_pairs={{0,1},{1,0},{2,3},{3,2},{4,5},{5,4},{6,7},{7,6},{8,9},{9,8},{10,11... | collective-permute-start | bytes 2359304 | tf_op jit(solution)/shard_map/ppermute | solution.py:46
  60.0 4.0 %collective-permute-start.9 = (bf16[4,2,64,768]{3,2,1,0:T(8,128)(2,1)S(1)}, bf16[4,2,64,768]{3,2,1,0:T(8,128)(2,1)S(1)}, u32[]{:S(2)}, u32[]{:S(2)}) collective-permute-start(bf16[4,2,64,768]{3,2,1,0:T(8,128)(2,1)S(1)} %collective-permute-done.6.refs_2_), channel_id=1, source_target_pairs={{0,1},{1,0},{2,3},{3,2},{4,5},{5,4},{6,7},{7,6},{8,9},{9,8},{10,11... | collective-permute-start | bytes 2359304 | tf_op jit(solution)/shard_map/ppermute | solution.py:46
  60.0 5.1 %collective-permute-start.10 = (bf16[4,2,64,768]{3,2,1,0:T(8,128)(2,1)S(1)}, bf16[4,2,64,768]{3,2,1,0:T(8,128)(2,1)S(1)}, u32[]{:S(2)}, u32[]{:S(2)}) collective-permute-start(bf16[4,2,64,768]{3,2,1,0:T(8,128)(2,1)S(1)} %collective-permute-done.4.refs_3_), channel_id=1, source_target_pairs={{0,1},{1,0},{2,3},{3,2},{4,5},{5,4},{6,7},{7,6},{8,9},{9,8},{10,11... | collective-permute-start | bytes 2359304 | tf_op jit(solution)/shard_map/ppermute | solution.py:46
  71.6 5.7 %collective-permute-start.11 = (bf16[4,4,2,64,768]{4,3,2,1,0:T(8,128)(2,1)S(1)}, bf16[4,4,2,64,768]{4,3,2,1,0:T(8,128)(2,1)S(1)}, u32[]{:S(2)}, u32[]{:S(2)}) collective-permute-start(bf16[4,4,2,64,768]{4,3,2,1,0:T(8,128)(2,1)S(1)} %get-tuple-element.53), channel_id=1, source_target_pairs={{0,1},{1,0},{2,3},{3,2},{4,5},{5,4},{6,7},{7,6},{8,9},{9,8},{10,11... | collective-permute-start | bytes 9437192 | tf_op jit(solution)/shard_map/ppermute | solution.py:46
  78.5 13.9 %collective-permute-start.12 = (bf16[4,2,64,768]{3,2,1,0:T(8,128)(2,1)S(1)}, bf16[4,2,64,768]{3,2,1,0:T(8,128)(2,1)S(1)}, u32[]{:S(2)}, u32[]{:S(2)}) collective-permute-start(bf16[4,2,64,768]{3,2,1,0:T(8,128)(2,1)S(1)} %get-tuple-element.55), channel_id=1, source_target_pairs={{0,4},{1,17},{2,6},{3,19},{4,0},{5,21},{6,2},{7,23},{8,12},{9,25},... | collective-permute-start | bytes 2359304 | tf_op jit(solution)/shard_map/ppermute | solution.py:42
  79.0 19.6 %collective-permute-start.13 = (bf16[4,2,64,768]{3,2,1,0:T(8,128)(2,1)S(1)}, bf16[4,2,64,768]{3,2,1,0:T(8,128)(2,1)S(1)}, u32[]{:S(2)}, u32[]{:S(2)}) collective-permute-start(bf16[4,2,64,768]{3,2,1,0:T(8,128)(2,1)S(1)} %get-tuple-element.56), channel_id=1, source_target_pairs={{0,2},{1,9},{2,0},{3,11},{4,6},{5,13},{6,4},{7,15},{8,10},{9,1},{1... | collective-permute-start | bytes 2359304 | tf_op jit(solution)/shard_map/ppermute | solution.py:42
  80.1 20.6 %collective-permute-start.14 = (bf16[4,2,64,768]{3,2,1,0:T(8,128)(2,1)S(1)}, bf16[4,2,64,768]{3,2,1,0:T(8,128)(2,1)S(1)}, u32[]{:S(2)}, u32[]{:S(2)}) collective-permute-start(bf16[4,2,64,768]{3,2,1,0:T(8,128)(2,1)S(1)} %get-tuple-element.57), channel_id=1, source_target_pairs={{0,6},{1,25},{2,4},{3,27},{4,2},{5,29},{6,0},{7,31},{8,14},{9,17},... | collective-permute-start | bytes 2359304 | tf_op jit(solution)/shard_map/ppermute | solution.py:42
  101.2 7.3 %collective-permute-start.15 = (bf16[2,64,768]{2,1,0:T(8,128)(2,1)S(1)}, bf16[2,64,768]{2,1,0:T(8,128)(2,1)S(1)}, u32[]{:S(2)}, u32[]{:S(2)}) collective-permute-start(bf16[2,64,768]{2,1,0:T(8,128)(2,1)S(1)} %get-tuple-element.62), channel_id=1, source_target_pairs={{0,16},{1,5},{2,18},{3,7},{4,20},{5,1},{6,22},{7,3},{8,24},{9,13},... | collective-permute-start | bytes 589832 | tf_op jit(solution)/shard_map/ppermute | solution.py:42
  103.3 7.6 %collective-permute-start.16 = (bf16[2,64,768]{2,1,0:T(8,128)(2,1)S(1)}, bf16[2,64,768]{2,1,0:T(8,128)(2,1)S(1)}, u32[]{:S(2)}, u32[]{:S(2)}) collective-permute-start(bf16[2,64,768]{2,1,0:T(8,128)(2,1)S(1)} %get-tuple-element.63), channel_id=1, source_target_pairs={{0,8},{1,3},{2,10},{3,1},{4,12},{5,7},{6,14},{7,5},{8,0},{9,11},{1... | collective-permute-start | bytes 589832 | tf_op jit(solution)/shard_map/ppermute | solution.py:42
  105.1 6.9 %collective-permute-start.17 = (bf16[2,64,768]{2,1,0:T(8,128)(2,1)S(1)}, bf16[2,64,768]{2,1,0:T(8,128)(2,1)S(1)}, u32[]{:S(2)}, u32[]{:S(2)}) collective-permute-start(bf16[2,64,768]{2,1,0:T(8,128)(2,1)S(1)} %get-tuple-element.64), channel_id=1, source_target_pairs={{0,24},{1,7},{2,26},{3,5},{4,28},{5,3},{6,30},{7,1},{8,16},{9,15},... | collective-permute-start | bytes 589832 | tf_op jit(solution)/shard_map/ppermute | solution.py:42

commit v4 on v3

--- a/solution.py
+++ b/solution.py
@@ -11,15 +11,22 @@
 NY = 4
 NX = 4
 CAP = 8
+TOPK = 2
 BF = jnp.bfloat16
 F32 = jnp.float32
 NT = (((1,), (1,)), ((), ()))
 VMEM_LIMIT = {"own": 8, "other": 12, "last": 4}
 
 
+Z_GROUPS = [[z * NY + y for z in range(E)] for y in range(NY)]
+
+
+def gather_z(v):
+    return lax.all_gather(v, "dp", axis_index_groups=Z_GROUPS)
+
+
 def swap_z(v):
-    groups = [[z * NY + y for z in range(E)] for y in range(NY)]
-    return lax.all_to_all(v, "dp", 0, 0, axis_index_groups=groups, tiled=True)
+    return lax.all_to_all(v, "dp", 0, 0, axis_index_groups=Z_GROUPS, tiled=True)
 
 
 def partner(i, q):
@@ -46,19 +53,113 @@
     return lax.ppermute(v, "cuts", [(i, i ^ 1) for i in range(2 * NX)])
 
 
-def slots_of(routing, gate_values):
-    hit = routing[:, :, None] == jnp.arange(E, dtype=jnp.int32)
-    chosen = jnp.any(hit, axis=1)
-    gates = jnp.sum(jnp.where(hit, gate_values[:, :, None], 0.0), axis=1)
-    rows = routing.shape[0]
-    below = jnp.arange(rows)[:, None] > jnp.arange(rows)[None, :]
-    position = jnp.sum(
-        jnp.where(below[:, :, None] & chosen[None, :, :], 1, 0), axis=1
-    )
-    slot = position[:, :, None] == jnp.arange(CAP, dtype=jnp.int32)
-    select = chosen[:, :, None] & slot
-    weight = jnp.where(select, gates[:, :, None], 0.0)
-    return select.reshape(rows, E * CAP), weight.reshape(rows, E * CAP)
+def thirds(v):
+    first = v.astype(BF)
+    rest = v - first.astype(F32)
+    second = rest.astype(BF)
+    return first, second, (rest - second.astype(F32)).astype(BF)
+
+
+def later(n):
+    i = lax.broadcasted_iota(jnp.int32, (n, n), 0)
+    j = lax.broadcasted_iota(jnp.int32, (n, n), 1)
+    return jnp.where(i < j, 1.0, 0.0).astype(BF)
+
+
+def pack_kernel(tokens, out_grad, routing_in, gates_in, out, routing, gates, sem):
+    rows = tokens.shape[0]
+    copies = [
+        pltpu.make_async_copy(tokens, out.at[:rows], sem.at[0]),
+        pltpu.make_async_copy(out_grad, out.at[rows : 2 * rows], sem.at[1]),
+        pltpu.make_async_copy(routing_in, routing, sem.at[2]),
+        pltpu.make_async_copy(gates_in, gates, sem.at[3]),
+    ]
+    for copy in copies:
+        copy.start()
+    out[2 * rows :] = jnp.zeros_like(out[2 * rows :])
+    copies[2].wait()
+    copies[3].wait()
+    info = [routing[k : k + 1, :].astype(F32) for k in range(TOPK)]
+    for k in range(TOPK):
+        info += [p.astype(F32) for p in thirds(gates[k : k + 1, :])]
+    out[2 * rows :, :rows] = jnp.concatenate(info, axis=0).astype(BF)
+    copies[0].wait()
+    copies[1].wait()
+
+
+def slot_kernel(expert, got, out):
+    rows = (got.shape[1] - 8) // 2
+    e = expert[0].astype(F32)
+    lanes = 128
+    lane = lax.broadcasted_iota(jnp.int32, (CAP, lanes), 1)
+    slot = lax.broadcasted_iota(jnp.int32, (CAP, lanes), 0).astype(F32)
+    before = later(lanes)
+    xs, dys = [], []
+    for z in range(E):
+        info = got[z, 2 * rows :, :lanes].astype(F32)
+        is0 = info[0:1] == e
+        chosen = (is0 | (info[1:2] == e)) & (lane < rows)
+        flags = jnp.where(chosen, 1.0, 0.0).astype(BF)
+        position = jnp.dot(flags, before, preferred_element_type=F32)
+        select = chosen & (position == slot)
+        gate0 = info[2:3] + info[3:4] + info[4:5]
+        gate1 = info[5:6] + info[6:7] + info[7:8]
+        gate = jnp.where(is0, gate0, gate1)
+        gate = jnp.sum(jnp.where(select, gate, 0.0), axis=1, keepdims=True)
+        pick = jnp.where(select, 1.0, 0.0)[:, :rows].astype(BF)
+        xs.append(jnp.dot(pick, got[z, :rows], preferred_element_type=F32))
+        dy = jnp.dot(pick, got[z, rows : 2 * rows], preferred_element_type=F32)
+        dys.append(gate * dy)
+    out[0] = jnp.concatenate(xs, axis=0).astype(BF)
+    out[1] = jnp.concatenate(dys, axis=0).astype(BF)
+
+
+def own_slots(routing, gates, mix, select_ref):
+    rows = routing.shape[1]
+    shape = E * CAP, rows
+    index = lax.broadcasted_iota(jnp.int32, shape, 0)
+    expert = index // CAP
+    is0 = routing[0:1, :] == expert
+    chosen = is0 | (routing[1:2, :] == expert)
+    flags = jnp.where(chosen, 1.0, 0.0).astype(BF)
+    position = jnp.dot(flags, later(rows), preferred_element_type=F32)
+    select = chosen & (position == (index % CAP).astype(F32))
+    gate = jnp.where(is0, gates[0:1, :], gates[1:2, :])
+    i = lax.broadcasted_iota(jnp.int32, (rows, rows), 0)
+    j = lax.broadcasted_iota(jnp.int32, (rows, rows), 1)
+    eye = jnp.where(i == j, 1.0, 0.0).astype(BF)
+
+    def turned(v):
+        return lax.dot_general(eye, v, NT, preferred_element_type=F32).astype(BF)
+
+    select_ref[...] = turned(jnp.where(select, 1.0, 0.0).astype(BF))
+    for n, part in enumerate(thirds(jnp.where(select, gate, 0.0))):
+        mix[n] = turned(part)
+
+
+def combine_kernel(back, mix, select, mixed, grad):
+    def rows(at):
+        parts = [back[e, at : at + CAP].astype(F32) for e in range(E)]
+        return jnp.concatenate(parts, axis=0).astype(BF)
+
+    y, dx = rows(0), rows(CAP)
+    total = jnp.dot(mix[0], y, preferred_element_type=F32)
+    for n in (1, 2):
+        total = total + jnp.dot(mix[n], y, preferred_element_type=F32)
+    mixed[...] = total.astype(BF)
+    grad[...] = jnp.dot(select[...], dx, preferred_element_type=F32).astype(BF)
+
+
+def small(body, name, out, arrays, scalars=0):
+    return pl.pallas_call(
+        body,
+        name=name,
+        out_shape=out,
+        in_specs=[pl.BlockSpec(memory_space=pltpu.SMEM)] * scalars
+        + [pl.BlockSpec(memory_space=pltpu.VMEM)] * (len(arrays) - scalars),
+        out_specs=jax.tree.map(lambda _: pl.BlockSpec(memory_space=pltpu.VMEM), out),
+        compiler_params=pltpu.CompilerParams(vmem_limit_bytes=4 << 20),
+    )(*arrays)
 
 
 def gather(v, along_y):
@@ -83,8 +184,8 @@
     return add(parts[0], *got)
 
 
-def weights_kernel(infos, *refs):
-    weights, bufs, sem = refs[:3], refs[3:5], refs[5]
+def weights_kernel(infos, routing, gates, *refs):
+    weights, bufs, mix, select, sem = refs[:3], refs[3:5], refs[5], refs[6], refs[7]
     hidden, width = weights[0].shape[0], bufs[0].shape[-1]
     copies = []
     for core in range(2):
@@ -99,25 +200,31 @@
                 )
     for copy in copies:
         copy.start()
+    own_slots(routing, gates, mix, select)
     for copy in copies:
         copy.wait()
 
 
-def load_weights(infos, weights, width):
+def load_weights(infos, routing, gates, weights, width):
     hidden = weights[0].shape[0]
     return pl.pallas_call(
         weights_kernel,
         name="weights",
-        out_shape=[jax.ShapeDtypeStruct((NX, 3 * hidden, width), BF)] * 2,
+        out_shape=[jax.ShapeDtypeStruct((NX, 3 * hidden, width), BF)] * 2
+        + [
+            jax.ShapeDtypeStruct((3, routing.shape[1], E * CAP), BF),
+            jax.ShapeDtypeStruct((routing.shape[1], E * CAP), BF),
+        ],
         in_specs=[pl.BlockSpec(memory_space=pltpu.SMEM)]
+        + [pl.BlockSpec(memory_space=pltpu.VMEM)] * 2
         + [pl.BlockSpec(memory_space=pltpu.HBM)] * 3,
-        out_specs=[pl.BlockSpec(memory_space=pltpu.VMEM)] * 2,
+        out_specs=[pl.BlockSpec(memory_space=pltpu.VMEM)] * 4,
         scratch_shapes=[pltpu.SemaphoreType.DMA((2, NX, 3))],
         compiler_params=pltpu.CompilerParams(vmem_limit_bytes=4 << 20),
         cost_estimate=pl.CostEstimate(
             flops=0, bytes_accessed=26 << 20, transcendentals=0
         ),
-    )(infos, *weights)
+    )(infos, routing, gates, *weights)
 
 
 def order(info, b, a):
@@ -224,24 +331,35 @@
     other_info = own_info ^ 1
     rows = NY * E * CAP
 
-    select, weight = slots_of(routing, gate_values)
-    pick = select.astype(BF).T
-    send_x = jnp.dot(pick, tokens, preferred_element_type=F32).astype(BF)
-    slot_gate = jnp.sum(weight, axis=0)
-    send_dy = jnp.dot(pick, out_grad, preferred_element_type=F32)
-    send_dy = (slot_gate[:, None] * send_dy).astype(BF)
-    send = jnp.concatenate(
-        [send_x.reshape(E, CAP, width), send_dy.reshape(E, CAP, width)], axis=1
-    )
-    got = swap_z(send).reshape(E, 2, CAP, width)
-    got = jnp.swapaxes(got, 0, 1).reshape(2, E * CAP, width)
+    turned = jnp.swapaxes(routing, 0, 1), jnp.swapaxes(gate_values, 0, 1)
+    packed = jax.ShapeDtypeStruct((2 * tokens.shape[0] + 8, width), BF)
+    packed = pl.pallas_call(
+        pack_kernel,
+        name="pack",
+        out_shape=packed,
+        in_specs=[pl.BlockSpec(memory_space=pl.ANY)] * 4,
+        out_specs=pl.BlockSpec(memory_space=pltpu.VMEM),
+        scratch_shapes=[
+            pltpu.VMEM(turned[0].shape, jnp.int32),
+            pltpu.VMEM(turned[1].shape, F32),
+            pltpu.SemaphoreType.DMA((4,)),
+        ],
+    )(
+        *[
+            pltpu.with_memory_space_constraint(v, pltpu.HBM)
+            for v in (tokens, out_grad, *turned)
+        ]
+    )
+    plane = (lax.axis_index("dp") // NY).reshape(1)
+    got = jax.ShapeDtypeStruct((2, E * CAP, width), BF)
+    got = small(slot_kernel, "slots", got, [plane, gather_z(packed)], 1)
 
     parts = gather(got, 0)
-    token = to_core(parts[3][0, :8, :128])[0, 0]
+    token = to_core(parts[3][0, :8])[0]
     near = jnp.where(token == token, jnp.stack(parts), jnp.zeros((), BF))
     weights = [pltpu.with_memory_space_constraint(w, pltpu.HBM) for w in (wg, wu, w2)]
     infos, near = lax.optimization_barrier((jnp.stack([own_info, other_info]), near))
-    bufs = load_weights(infos, weights, width)
+    bufs = load_weights(infos, *turned, weights, width)
     own, bufs = lax.optimization_barrier((tuple(gather(near, 1)), tuple(bufs)))
     other = [to_core(v) for v in own]
 
@@ -270,11 +388,8 @@
     back = back.reshape(2, E, CAP, width)
     back = jnp.swapaxes(back, 0, 1).reshape(E, 2 * CAP, width)
     back = swap_z(back)
-    back_y = back[:, :CAP].reshape(E * CAP, width)
-    back_dx = back[:, CAP:].reshape(E * CAP, width)
-    mixed = jnp.dot(weight, back_y.astype(F32), precision=lax.Precision.HIGHEST)
-    grad = jnp.dot(select.astype(BF), back_dx, preferred_element_type=F32)
-    return mixed.astype(BF), grad.astype(BF)
+    result = [jax.ShapeDtypeStruct(tokens.shape, BF)] * 2
+    return tuple(small(combine_kernel, "combine", result, [back, bufs[2], bufs[3]]))
 
 
 def solution(mesh):

time: 126 us -> 135 us (1.071)
  blocking collectives: 30.9 us -> 43.5 us
  Pallas kernels: 18.5 us -> 22 us
  matrix products: 2.83 us -> 0 us
  other arithmetic: 3.7 us -> 1.94 us
    all_gather x0 -> x1, blocking collectives: none -> 29.3 us  [gather_z(): return lax.all_gather(v, 'dp', axis_index_groups=Z_GROUPS)]
    all_to_all x2 -> x1, blocking collectives: 30.9 us -> 14.2 us  [swap_z(): return lax.all_to_all(v, 'dp', 0, 0, axis_index_groups=Z_GROUPS, tiled=True)]
    pallas_call x0 -> x3, Pallas kernels: none -> 3.46 us  [the longest x2 2.06 us: small(): pl.pallas_call(body, name=name, out_shape=out, in_specs=[pl.BlockSpec(mem...]
    dot_general x4 -> x0, matrix products: 2.83 us -> none  [the longest x1 0.96 us: on_device(): send_dy = jnp.dot(pick, out_grad, preferred_element_type=F32)]
  transfers between devices with their start and end apart: 18 -> 18, of which waited for: 15 -> 15; matrix products, arithmetic and copies ran while one was open for 0% -> 0% of each run, Pallas kernels for 10% -> 9%
where the time goes in v4:
time: 135 us
  waiting for transfers between devices  47.4 us (35%)
  blocking collectives  43.5 us (32%)
  Pallas kernels  22 us (16%)
  starting transfers between devices  19.5 us (14%)
  other arithmetic  1.94 us (1%)
    ppermute x12, waiting for transfers between devices, swap(): return lax.ppermute(v, ('dp', 'cuts'), perm)  42.7 us
    all_gather x1, blocking collectives, gather_z(): return lax.all_gather(v, 'dp', axis_index_groups=Z_GROUPS)  29.3 us
    ppermute x12, starting transfers between devices, swap(): return lax.ppermute(v, ('dp', 'cuts'), perm)  18.3 us
    all_to_all x1, blocking collectives, swap_z(): return lax.all_to_all(v, 'dp', 0, 0, axis_index_groups=Z_GROUPS, tiled=True)  14.2 us
    pallas_call x3, Pallas kernels, call(): pl.pallas_call(body, name=name, out_shape=out, in_specs=[pl.BlockSpec(mem...  13 us
    pallas_call x1, Pallas kernels, load_weights(): pl.pallas_call(weights_kernel, name='weights', out_shape=[jax.ShapeDtypeS...  5.52 us
    ppermute x6, waiting for transfers between devices, to_core(): return lax.ppermute(v, 'cuts', [(i, i ^ 1) for i in range(2 * NX)])  4.62 us
  transfers between devices with their start and end apart: 18, of which 15 were waited for; matrix products, arithmetic and copies ran while one was open for 0% of the time, Pallas kernels for 9%

profile of v4, /device:TPU:6, one launch (start us, length us, event | category | flops | bytes accessed | tf_op | source)
XLA Modules:
  0.0 135.2 jit_solution(13266829623314239580)
XLA Ops:
  0.7 1.4 %pack.1 = bf16[40,768]{1,0:T(8,128)(2,1)} custom-call(bf16[16,768]{1,0:T(8,128)(2,1)} %tokens.1, bf16[16,768]{1,0:T(8,128)(2,1)} %out_grad.1, s32[2,16]{1,0:T(2,128)} %bitcast.42, f32[2,16]{1,0:T(2,128)} %bitcast.44), custom_call_target="tpu_custom_call" | custom-call | tf_op jit(solution)/shard_map/pack/pallas_call | solution.py:336
  2.1 29.3 %all-gather = bf16[320,768]{1,0:T(8,128)(2,1)S(1)} all-gather(bf16[40,768]{1,0:T(8,128)(2,1)} %pack.1), channel_id=2, replica_groups={{0,32,64,96,128,160,192,224},{8,40,72,104,136,168,200,232},{16,48,80,11..., dimensions={0}, use_global_device_ids=true | all-gather | bytes 552960 | tf_op jit(solution)/shard_map/all_gather | solution.py:25
  31.4 1.3 slots.1
  32.7 3.1 %collective-permute-start.2 = (bf16[2,64,768]{2,1,0:T(8,128)(2,1)S(1)}, bf16[2,64,768]{2,1,0:T(8,128)(2,1)S(1)}, u32[]{:S(2)}, u32[]{:S(2)}) collective-permute-start(bf16[2,64,768]{2,1,0:T(8,128)(2,1)S(1)} %slots.1), channel_id=1, source_target_pairs={{0,24},{1,7},{2,26},{3,5},{4,28},{5,3},{6,30},{7,1},{8,16},{9,15},... | collective-permute-start | bytes 589832 | tf_op jit(solution)/shard_map/ppermute | solution.py:49
  35.8 0.1 collective-permute-start.1
  35.9 1.5 %collective-permute-start = (bf16[2,64,768]{2,1,0:T(8,128)(2,1)S(1)}, bf16[2,64,768]{2,1,0:T(8,128)(2,1)S(1)}, u32[]{:S(2)}, u32[]{:S(2)}) collective-permute-start(bf16[2,64,768]{2,1,0:T(8,128)(2,1)S(1)} %slots.1), channel_id=1, source_target_pairs={{0,16},{1,5},{2,18},{3,7},{4,20},{5,1},{6,22},{7,3},{8,24},{9,13},... | collective-permute-start | bytes 589832 | tf_op jit(solution)/shard_map/ppermute | solution.py:49
  37.5 2.2 %collective-permute-done.2 = bf16[2,64,768]{2,1,0:T(8,128)(2,1)S(1)} collective-permute-done((bf16[2,64,768]{2,1,0:T(8,128)(2,1)S(1)}, bf16[2,64,768]{2,1,0:T(8,128)(2,1)S(1)}, u32[]{:S(2)}, u32[]{:S(2)}) %collective-permute-start.2) | collective-permute-done | bytes 196640 | tf_op jit(solution)/shard_map/ppermute | solution.py:49
  39.6 1.8 %collective-permute-done.1 = bf16[2,64,768]{2,1,0:T(8,128)(2,1)S(1)} collective-permute-done((bf16[2,64,768]{2,1,0:T(8,128)(2,1)S(1)}, bf16[2,64,768]{2,1,0:T(8,128)(2,1)S(1)}, u32[]{:S(2)}, u32[]{:S(2)}) %collective-permute-start.1) | collective-permute-done | bytes 196640 | tf_op jit(solution)/shard_map/ppermute | solution.py:49
  41.4 1.8 %collective-permute-done = bf16[2,64,768]{2,1,0:T(8,128)(2,1)S(1)} collective-permute-done((bf16[2,64,768]{2,1,0:T(8,128)(2,1)S(1)}, bf16[2,64,768]{2,1,0:T(8,128)(2,1)S(1)}, u32[]{:S(2)}, u32[]{:S(2)}) %collective-permute-start) | collective-permute-done | bytes 196640 | tf_op jit(solution)/shard_map/ppermute | solution.py:49
  43.2 0.0 collective-permute-start.3
  43.2 1.2 collective-permute-done.3
  44.4 0.1 maximum_select_fusion.refs_0_
  44.5 0.6 collective-permute-start.6
  45.1 0.9 collective-permute-start.5
  46.0 3.3 %collective-permute-start.4 = (bf16[4,2,64,768]{3,2,1,0:T(8,128)(2,1)S(1)}, bf16[4,2,64,768]{3,2,1,0:T(8,128)(2,1)S(1)}, u32[]{:S(2)}, u32[]{:S(2)}) collective-permute-start(bf16[4,2,64,768]{3,2,1,0:T(8,128)(2,1)S(1)} %maximum_select_fusion.refs_0_), channel_id=1, source_target_pairs={{0,4},{1,17},{2,6},{3,19},{4,0},{5,21},{6,2},{7,23},{8,12},{9,25},... | collective-permute-start | bytes 2359304 | tf_op jit(solution)/shard_map/ppermute | solution.py:49
  49.3 5.5 %weights.1 = (bf16[4,1056,768]{2,1,0:T(8,128)(2,1)S(1)}, bf16[4,1056,768]{2,1,0:T(8,128)(2,1)S(1)}, bf16[3,16,64]{2,1,0:T(8,128)(2,1)S(1)}, bf16[16,64]{1,0:T(8,128)(2,1)S(1)}) custom-call(s32[2,5]{1,0:T(2,128)S(1)} %pad_add_fusion.infos, s32[2,16]{1,0:T(2,128)S(1)} %bitcast.43, f32[2,16]{1,0:T(2,128)S(1)} %bitcast.45, bf16[352,6144]{1,0:T(8,128)(2,1)} %bitcast.46, ...), custom_call_target="tpu_custom_call" | custom-call | bytes 27262976 | tf_op jit(solution)/shard_map/weights/pallas_call | solution.py:210
  54.8 3.0 %collective-permute-done.6.refs_2_ = bf16[4,2,64,768]{3,2,1,0:T(8,128)(2,1)S(1)} collective-permute-done((bf16[4,2,64,768]{3,2,1,0:T(8,128)(2,1)S(1)}, bf16[4,2,64,768]{3,2,1,0:T(8,128)(2,1)S(1)}, u32[]{:S(2)}, u32[]{:S(2)}) %collective-permute-start.6) | collective-permute-done | bytes 786464 | tf_op jit(solution)/shard_map/ppermute | solution.py:49
  57.8 9.9 %collective-permute-done.4.refs_3_ = bf16[4,2,64,768]{3,2,1,0:T(8,128)(2,1)S(1)} collective-permute-done((bf16[4,2,64,768]{3,2,1,0:T(8,128)(2,1)S(1)}, bf16[4,2,64,768]{3,2,1,0:T(8,128)(2,1)S(1)}, u32[]{:S(2)}, u32[]{:S(2)}) %collective-permute-start.4) | collective-permute-done | bytes 786464 | tf_op jit(solution)/shard_map/ppermute | solution.py:49
  67.7 0.0 collective-permute-start.7
  67.7 0.5 collective-permute-start.8
  68.2 0.0 collective-permute-start.9
  68.2 0.5 collective-permute-start.10
  68.7 3.4 %own.1.refs_5_ = f32[1056,256]{1,0:T(8,128)S(1)} custom-call(s32[5]{0:T(128)S(1)} %get-tuple-element.79.info, bf16[4,2,64,768]{3,2,1,0:T(8,128)(2,1)S(1)} %maximum_select_fusion.refs_0_, bf16[4,2,64,768]{3,2,1,0:T(8,128)(2,1)S(1)} %collective-permute-done.5.refs_1_, bf16[4,2,64,768]{3,2,1,0:T(8,128)(2,1)S(1)} %collective-permute-done.6.refs_2_, ...), custom_call_target="tpu_custom_call" | custom-call | flops 1660944384 | bytes 7340032 | tf_op jit(solution)/shard_map/own/pallas_call | solution.py:302
  72.2 0.0 collective-permute-done.8.refs_1_
  72.2 0.1 collective-permute-done.9.refs_2_
  72.2 1.1 collective-permute-done.10.refs_3_
  73.4 6.4 %other.1 = (bf16[4,4,2,64,768]{4,3,2,1,0:T(8,128)(2,1)S(1)}, bf16[256,352]{1,0:T(8,128)(2,1)S(1)}, bf16[256,704]{1,0:T(8,128)(2,1)S(1)}) custom-call(s32[5]{0:T(128)S(1)} %get-tuple-element.78.info, bf16[4,2,64,768]{3,2,1,0:T(8,128)(2,1)S(1)} %collective-permute-done.7.refs_0_, bf16[4,2,64,768]{3,2,1,0:T(8,128)(2,1)S(1)} %collective-permute-done.8.refs_1_, ...), custom_call_target="tpu_custom_call" | custom-call | flops 3321888768 | bytes 7340032 | tf_op jit(solution)/shard_map/other/pallas_call | solution.py:302
  79.8 0.2 collective-permute-start.11
  80.0 3.3 %last.1 = bf16[4,4,2,64,768]{4,3,2,1,0:T(8,128)(2,1)S(1)} custom-call(s32[5]{0:T(128)S(1)} %get-tuple-element.79.info, bf16[256,352]{1,0:T(8,128)(2,1)S(1)} %get-tuple-element.57.hidden, bf16[256,704]{1,0:T(8,128)(2,1)S(1)} %get-tuple-element.58.grads, bf16[4,1056,768]{2,1,0:T(8,128)(2,1)S(1)} %get-tuple-element.56.refs_4_.buf), custom_call_target="tpu_custom_call" | custom-call | flops 1660944384 | bytes 7340032 | tf_op jit(solution)/shard_map/last/pallas_call | solution.py:302
  83.3 2.3 %collective-permute-done.11 = bf16[4,4,2,64,768]{4,3,2,1,0:T(8,128)(2,1)S(1)} collective-permute-done((bf16[4,4,2,64,768]{4,3,2,1,0:T(8,128)(2,1)S(1)}, bf16[4,4,2,64,768]{4,3,2,1,0:T(8,128)(2,1)S(1)}, u32[]{:S(2)}, u32[]{:S(2)}) %collective-permute-start.11) | collective-permute-done | bytes 3145760 | tf_op jit(solution)/shard_map/ppermute | solution.py:53
  85.5 1.2 fusion.3
  86.8 0.3 collective-permute-start.12
  87.0 1.2 collective-permute-start.13
  88.2 2.8 %collective-permute-start.14 = (bf16[4,2,64,768]{3,2,1,0:T(8,128)(2,1)S(1)}, bf16[4,2,64,768]{3,2,1,0:T(8,128)(2,1)S(1)}, u32[]{:S(2)}, u32[]{:S(2)}) collective-permute-start(bf16[4,2,64,768]{3,2,1,0:T(8,128)(2,1)S(1)} %get-tuple-element.63), channel_id=1, source_target_pairs={{0,6},{1,25},{2,4},{3,27},{4,2},{5,29},{6,0},{7,31},{8,14},{9,17},... | collective-permute-start | bytes 2359304 | tf_op jit(solution)/shard_map/ppermute | solution.py:49
  90.9 9.5 %collective-permute-done.12 = bf16[4,2,64,768]{3,2,1,0:T(8,128)(2,1)S(1)} collective-permute-done((bf16[4,2,64,768]{3,2,1,0:T(8,128)(2,1)S(1)}, bf16[4,2,64,768]{3,2,1,0:T(8,128)(2,1)S(1)}, u32[]{:S(2)}, u32[]{:S(2)}) %collective-permute-start.12) | collective-permute-done | bytes 786464 | tf_op jit(solution)/shard_map/ppermute | solution.py:49
  100.4 6.2 %collective-permute-done.13 = bf16[4,2,64,768]{3,2,1,0:T(8,128)(2,1)S(1)} collective-permute-done((bf16[4,2,64,768]{3,2,1,0:T(8,128)(2,1)S(1)}, bf16[4,2,64,768]{3,2,1,0:T(8,128)(2,1)S(1)}, u32[]{:S(2)}, u32[]{:S(2)}) %collective-permute-start.13) | collective-permute-done | bytes 786464 | tf_op jit(solution)/shard_map/ppermute | solution.py:49
  106.6 2.1 %collective-permute-done.14 = bf16[4,2,64,768]{3,2,1,0:T(8,128)(2,1)S(1)} collective-permute-done((bf16[4,2,64,768]{3,2,1,0:T(8,128)(2,1)S(1)}, bf16[4,2,64,768]{3,2,1,0:T(8,128)(2,1)S(1)}, u32[]{:S(2)}, u32[]{:S(2)}) %collective-permute-start.14) | collective-permute-done | bytes 786464 | tf_op jit(solution)/shard_map/ppermute | solution.py:49
  108.8 0.4 add_convert_fusion
  109.2 0.1 slice_bitcast_fusion
  109.3 2.1 %collective-permute-start.15 = (bf16[2,64,768]{2,1,0:T(8,128)(2,1)S(1)}, bf16[2,64,768]{2,1,0:T(8,128)(2,1)S(1)}, u32[]{:S(2)}, u32[]{:S(2)}) collective-permute-start(bf16[2,64,768]{2,1,0:T(8,128)(2,1)S(1)} %get-tuple-element.68), channel_id=1, source_target_pairs={{0,16},{1,5},{2,18},{3,7},{4,20},{5,1},{6,22},{7,3},{8,24},{9,13},... | collective-permute-start | bytes 589832 | tf_op jit(solution)/shard_map/ppermute | solution.py:49
  111.3 1.9 %collective-permute-start.16 = (bf16[2,64,768]{2,1,0:T(8,128)(2,1)S(1)}, bf16[2,64,768]{2,1,0:T(8,128)(2,1)S(1)}, u32[]{:S(2)}, u32[]{:S(2)}) collective-permute-start(bf16[2,64,768]{2,1,0:T(8,128)(2,1)S(1)} %get-tuple-element.69), channel_id=1, source_target_pairs={{0,8},{1,3},{2,10},{3,1},{4,12},{5,7},{6,14},{7,5},{8,0},{9,11},{1... | collective-permute-start | bytes 589832 | tf_op jit(solution)/shard_map/ppermute | solution.py:49
  113.2 0.6 collective-permute-start.17
  113.8 2.7 %collective-permute-done.15 = bf16[2,64,768]{2,1,0:T(8,128)(2,1)S(1)} collective-permute-done((bf16[2,64,768]{2,1,0:T(8,128)(2,1)S(1)}, bf16[2,64,768]{2,1,0:T(8,128)(2,1)S(1)}, u32[]{:S(2)}, u32[]{:S(2)}) %collective-permute-start.15) | collective-permute-done | bytes 196640 | tf_op jit(solution)/shard_map/ppermute | solution.py:49
  116.5 2.5 %collective-permute-done.16 = bf16[2,64,768]{2,1,0:T(8,128)(2,1)S(1)} collective-permute-done((bf16[2,64,768]{2,1,0:T(8,128)(2,1)S(1)}, bf16[2,64,768]{2,1,0:T(8,128)(2,1)S(1)}, u32[]{:S(2)}, u32[]{:S(2)}) %collective-permute-start.16) | collective-permute-done | bytes 196640 | tf_op jit(solution)/shard_map/ppermute | solution.py:49
  119.0 1.1 collective-permute-done.17
  120.1 0.1 copy_bitcast_fusion
  120.2 14.2 %all_to_all.5.back = bf16[8,16,768]{2,1,0:T(8,128)(2,1)S(1)} all-to-all(bf16[8,16,768]{2,1,0:T(8,128)(2,1)S(1)} %copy_bitcast_fusion), channel_id=1, replica_groups={{0,32,64,96,128,160,192,224},{8,40,72,104,136,168,200,232},{16,48,80,11..., dimensions={0} | all-to-all | bytes 393216 | tf_op jit(solution)/shard_map/all_to_all | solution.py:29
  134.4 0.8 combine.1
  (11 shorter events, 0.1 us)
Async XLA Ops:
  0.6 48.7 %copy-start = (s32[16,2]{0,1:T(2,128)S(1)}, s32[16,2]{0,1:T(2,128)}, u32[]{:S(2)}) copy-start(s32[16,2]{0,1:T(2,128)} %param.10) | copy-start | bytes 388
  0.6 48.7 %copy-start.1 = (f32[16,2]{0,1:T(2,128)S(1)}, f32[16,2]{0,1:T(2,128)}, u32[]{:S(2)}) copy-start(f32[16,2]{0,1:T(2,128)} %param.9) | copy-start | bytes 388
  32.7 7.0 %collective-permute-start.2 = (bf16[2,64,768]{2,1,0:T(8,128)(2,1)S(1)}, bf16[2,64,768]{2,1,0:T(8,128)(2,1)S(1)}, u32[]{:S(2)}, u32[]{:S(2)}) collective-permute-start(bf16[2,64,768]{2,1,0:T(8,128)(2,1)S(1)} %slots.1), channel_id=1, source_target_pairs={{0,24},{1,7},{2,26},{3,5},{4,28},{5,3},{6,30},{7,1},{8,16},{9,15},... | collective-permute-start | bytes 589832 | tf_op jit(solution)/shard_map/ppermute | solution.py:49
  35.8 5.7 %collective-permute-start.1 = (bf16[2,64,768]{2,1,0:T(8,128)(2,1)S(1)}, bf16[2,64,768]{2,1,0:T(8,128)(2,1)S(1)}, u32[]{:S(2)}, u32[]{:S(2)}) collective-permute-start(bf16[2,64,768]{2,1,0:T(8,128)(2,1)S(1)} %slots.1), channel_id=1, source_target_pairs={{0,8},{1,3},{2,10},{3,1},{4,12},{5,7},{6,14},{7,5},{8,0},{9,11},{1... | collective-permute-start | bytes 589832 | tf_op jit(solution)/shard_map/ppermute | solution.py:49
  35.9 7.3 %collective-permute-start = (bf16[2,64,768]{2,1,0:T(8,128)(2,1)S(1)}, bf16[2,64,768]{2,1,0:T(8,128)(2,1)S(1)}, u32[]{:S(2)}, u32[]{:S(2)}) collective-permute-start(bf16[2,64,768]{2,1,0:T(8,128)(2,1)S(1)} %slots.1), channel_id=1, source_target_pairs={{0,16},{1,5},{2,18},{3,7},{4,20},{5,1},{6,22},{7,3},{8,24},{9,13},... | collective-permute-start | bytes 589832 | tf_op jit(solution)/shard_map/ppermute | solution.py:49
  43.2 1.2 collective-permute-start.3
  44.5 13.3 %collective-permute-start.6 = (bf16[4,2,64,768]{3,2,1,0:T(8,128)(2,1)S(1)}, bf16[4,2,64,768]{3,2,1,0:T(8,128)(2,1)S(1)}, u32[]{:S(2)}, u32[]{:S(2)}) collective-permute-start(bf16[4,2,64,768]{3,2,1,0:T(8,128)(2,1)S(1)} %maximum_select_fusion.refs_0_), channel_id=1, source_target_pairs={{0,6},{1,25},{2,4},{3,27},{4,2},{5,29},{6,0},{7,31},{8,14},{9,17},... | collective-permute-start | bytes 2359304 | tf_op jit(solution)/shard_map/ppermute | solution.py:49
  45.1 12.7 %collective-permute-start.5 = (bf16[4,2,64,768]{3,2,1,0:T(8,128)(2,1)S(1)}, bf16[4,2,64,768]{3,2,1,0:T(8,128)(2,1)S(1)}, u32[]{:S(2)}, u32[]{:S(2)}) collective-permute-start(bf16[4,2,64,768]{3,2,1,0:T(8,128)(2,1)S(1)} %maximum_select_fusion.refs_0_), channel_id=1, source_target_pairs={{0,2},{1,9},{2,0},{3,11},{4,6},{5,13},{6,4},{7,15},{8,10},{9,1},{1... | collective-permute-start | bytes 2359304 | tf_op jit(solution)/shard_map/ppermute | solution.py:49
  46.0 21.7 %collective-permute-start.4 = (bf16[4,2,64,768]{3,2,1,0:T(8,128)(2,1)S(1)}, bf16[4,2,64,768]{3,2,1,0:T(8,128)(2,1)S(1)}, u32[]{:S(2)}, u32[]{:S(2)}) collective-permute-start(bf16[4,2,64,768]{3,2,1,0:T(8,128)(2,1)S(1)} %maximum_select_fusion.refs_0_), channel_id=1, source_target_pairs={{0,4},{1,17},{2,6},{3,19},{4,0},{5,21},{6,2},{7,23},{8,12},{9,25},... | collective-permute-start | bytes 2359304 | tf_op jit(solution)/shard_map/ppermute | solution.py:49
  67.7 4.4 %collective-permute-start.7 = (bf16[4,2,64,768]{3,2,1,0:T(8,128)(2,1)S(1)}, bf16[4,2,64,768]{3,2,1,0:T(8,128)(2,1)S(1)}, u32[]{:S(2)}, u32[]{:S(2)}) collective-permute-start(bf16[4,2,64,768]{3,2,1,0:T(8,128)(2,1)S(1)} %maximum_select_fusion.refs_0_), channel_id=1, source_target_pairs={{0,1},{1,0},{2,3},{3,2},{4,5},{5,4},{6,7},{7,6},{8,9},{9,8},{10,11... | collective-permute-start | bytes 2359304 | tf_op jit(solution)/shard_map/ppermute | solution.py:53
  67.7 4.4 %collective-permute-start.8 = (bf16[4,2,64,768]{3,2,1,0:T(8,128)(2,1)S(1)}, bf16[4,2,64,768]{3,2,1,0:T(8,128)(2,1)S(1)}, u32[]{:S(2)}, u32[]{:S(2)}) collective-permute-start(bf16[4,2,64,768]{3,2,1,0:T(8,128)(2,1)S(1)} %collective-permute-done.5.refs_1_), channel_id=1, source_target_pairs={{0,1},{1,0},{2,3},{3,2},{4,5},{5,4},{6,7},{7,6},{8,9},{9,8},{10,11... | collective-permute-start | bytes 2359304 | tf_op jit(solution)/shard_map/ppermute | solution.py:53
  68.2 4.0 %collective-permute-start.9 = (bf16[4,2,64,768]{3,2,1,0:T(8,128)(2,1)S(1)}, bf16[4,2,64,768]{3,2,1,0:T(8,128)(2,1)S(1)}, u32[]{:S(2)}, u32[]{:S(2)}) collective-permute-start(bf16[4,2,64,768]{3,2,1,0:T(8,128)(2,1)S(1)} %collective-permute-done.6.refs_2_), channel_id=1, source_target_pairs={{0,1},{1,0},{2,3},{3,2},{4,5},{5,4},{6,7},{7,6},{8,9},{9,8},{10,11... | collective-permute-start | bytes 2359304 | tf_op jit(solution)/shard_map/ppermute | solution.py:53
  68.2 5.1 %collective-permute-start.10 = (bf16[4,2,64,768]{3,2,1,0:T(8,128)(2,1)S(1)}, bf16[4,2,64,768]{3,2,1,0:T(8,128)(2,1)S(1)}, u32[]{:S(2)}, u32[]{:S(2)}) collective-permute-start(bf16[4,2,64,768]{3,2,1,0:T(8,128)(2,1)S(1)} %collective-permute-done.4.refs_3_), channel_id=1, source_target_pairs={{0,1},{1,0},{2,3},{3,2},{4,5},{5,4},{6,7},{7,6},{8,9},{9,8},{10,11... | collective-permute-start | bytes 2359304 | tf_op jit(solution)/shard_map/ppermute | solution.py:53
  79.8 5.7 %collective-permute-start.11 = (bf16[4,4,2,64,768]{4,3,2,1,0:T(8,128)(2,1)S(1)}, bf16[4,4,2,64,768]{4,3,2,1,0:T(8,128)(2,1)S(1)}, u32[]{:S(2)}, u32[]{:S(2)}) collective-permute-start(bf16[4,4,2,64,768]{4,3,2,1,0:T(8,128)(2,1)S(1)} %get-tuple-element.59), channel_id=1, source_target_pairs={{0,1},{1,0},{2,3},{3,2},{4,5},{5,4},{6,7},{7,6},{8,9},{9,8},{10,11... | collective-permute-start | bytes 9437192 | tf_op jit(solution)/shard_map/ppermute | solution.py:53
  86.8 13.7 %collective-permute-start.12 = (bf16[4,2,64,768]{3,2,1,0:T(8,128)(2,1)S(1)}, bf16[4,2,64,768]{3,2,1,0:T(8,128)(2,1)S(1)}, u32[]{:S(2)}, u32[]{:S(2)}) collective-permute-start(bf16[4,2,64,768]{3,2,1,0:T(8,128)(2,1)S(1)} %get-tuple-element.61), channel_id=1, source_target_pairs={{0,4},{1,17},{2,6},{3,19},{4,0},{5,21},{6,2},{7,23},{8,12},{9,25},... | collective-permute-start | bytes 2359304 | tf_op jit(solution)/shard_map/ppermute | solution.py:49
  87.0 19.6 %collective-permute-start.13 = (bf16[4,2,64,768]{3,2,1,0:T(8,128)(2,1)S(1)}, bf16[4,2,64,768]{3,2,1,0:T(8,128)(2,1)S(1)}, u32[]{:S(2)}, u32[]{:S(2)}) collective-permute-start(bf16[4,2,64,768]{3,2,1,0:T(8,128)(2,1)S(1)} %get-tuple-element.62), channel_id=1, source_target_pairs={{0,2},{1,9},{2,0},{3,11},{4,6},{5,13},{6,4},{7,15},{8,10},{9,1},{1... | collective-permute-start | bytes 2359304 | tf_op jit(solution)/shard_map/ppermute | solution.py:49
  88.2 20.6 %collective-permute-start.14 = (bf16[4,2,64,768]{3,2,1,0:T(8,128)(2,1)S(1)}, bf16[4,2,64,768]{3,2,1,0:T(8,128)(2,1)S(1)}, u32[]{:S(2)}, u32[]{:S(2)}) collective-permute-start(bf16[4,2,64,768]{3,2,1,0:T(8,128)(2,1)S(1)} %get-tuple-element.63), channel_id=1, source_target_pairs={{0,6},{1,25},{2,4},{3,27},{4,2},{5,29},{6,0},{7,31},{8,14},{9,17},... | collective-permute-start | bytes 2359304 | tf_op jit(solution)/shard_map/ppermute | solution.py:49
  109.3 7.3 %collective-permute-start.15 = (bf16[2,64,768]{2,1,0:T(8,128)(2,1)S(1)}, bf16[2,64,768]{2,1,0:T(8,128)(2,1)S(1)}, u32[]{:S(2)}, u32[]{:S(2)}) collective-permute-start(bf16[2,64,768]{2,1,0:T(8,128)(2,1)S(1)} %get-tuple-element.68), channel_id=1, source_target_pairs={{0,16},{1,5},{2,18},{3,7},{4,20},{5,1},{6,22},{7,3},{8,24},{9,13},... | collective-permute-start | bytes 589832 | tf_op jit(solution)/shard_map/ppermute | solution.py:49
  111.3 7.6 %collective-permute-start.16 = (bf16[2,64,768]{2,1,0:T(8,128)(2,1)S(1)}, bf16[2,64,768]{2,1,0:T(8,128)(2,1)S(1)}, u32[]{:S(2)}, u32[]{:S(2)}) collective-permute-start(bf16[2,64,768]{2,1,0:T(8,128)(2,1)S(1)} %get-tuple-element.69), channel_id=1, source_target_pairs={{0,8},{1,3},{2,10},{3,1},{4,12},{5,7},{6,14},{7,5},{8,0},{9,11},{1... | collective-permute-start | bytes 589832 | tf_op jit(solution)/shard_map/ppermute | solution.py:49
  113.2 6.9 %collective-permute-start.17 = (bf16[2,64,768]{2,1,0:T(8,128)(2,1)S(1)}, bf16[2,64,768]{2,1,0:T(8,128)(2,1)S(1)}, u32[]{:S(2)}, u32[]{:S(2)}) collective-permute-start(bf16[2,64,768]{2,1,0:T(8,128)(2,1)S(1)} %get-tuple-element.70), channel_id=1, source_target_pairs={{0,24},{1,7},{2,26},{3,5},{4,28},{5,3},{6,30},{7,1},{8,16},{9,15},... | collective-permute-start | bytes 589832 | tf_op jit(solution)/shard_map/ppermute | solution.py:49

commit v5 on v4

--- a/solution.py
+++ b/solution.py
@@ -21,10 +21,6 @@
 Z_GROUPS = [[z * NY + y for z in range(E)] for y in range(NY)]
 
 
-def gather_z(v):
-    return lax.all_gather(v, "dp", axis_index_groups=Z_GROUPS)
-
-
 def swap_z(v):
     return lax.all_to_all(v, "dp", 0, 0, axis_index_groups=Z_GROUPS, tiled=True)
 
@@ -66,65 +62,42 @@
     return jnp.where(i < j, 1.0, 0.0).astype(BF)
 
 
-def pack_kernel(tokens, out_grad, routing_in, gates_in, out, routing, gates, sem):
-    rows = tokens.shape[0]
-    copies = [
-        pltpu.make_async_copy(tokens, out.at[:rows], sem.at[0]),
-        pltpu.make_async_copy(out_grad, out.at[rows : 2 * rows], sem.at[1]),
-        pltpu.make_async_copy(routing_in, routing, sem.at[2]),
-        pltpu.make_async_copy(gates_in, gates, sem.at[3]),
-    ]
-    for copy in copies:
-        copy.start()
-    out[2 * rows :] = jnp.zeros_like(out[2 * rows :])
-    copies[2].wait()
-    copies[3].wait()
-    info = [routing[k : k + 1, :].astype(F32) for k in range(TOPK)]
-    for k in range(TOPK):
-        info += [p.astype(F32) for p in thirds(gates[k : k + 1, :])]
-    out[2 * rows :, :rows] = jnp.concatenate(info, axis=0).astype(BF)
-    copies[0].wait()
-    copies[1].wait()
-
-
-def slot_kernel(expert, got, out):
-    rows = (got.shape[1] - 8) // 2
-    e = expert[0].astype(F32)
-    lanes = 128
-    lane = lax.broadcasted_iota(jnp.int32, (CAP, lanes), 1)
-    slot = lax.broadcasted_iota(jnp.int32, (CAP, lanes), 0).astype(F32)
-    before = later(lanes)
-    xs, dys = [], []
-    for z in range(E):
-        info = got[z, 2 * rows :, :lanes].astype(F32)
-        is0 = info[0:1] == e
-        chosen = (is0 | (info[1:2] == e)) & (lane < rows)
-        flags = jnp.where(chosen, 1.0, 0.0).astype(BF)
-        position = jnp.dot(flags, before, preferred_element_type=F32)
-        select = chosen & (position == slot)
-        gate0 = info[2:3] + info[3:4] + info[4:5]
-        gate1 = info[5:6] + info[6:7] + info[7:8]
-        gate = jnp.where(is0, gate0, gate1)
-        gate = jnp.sum(jnp.where(select, gate, 0.0), axis=1, keepdims=True)
-        pick = jnp.where(select, 1.0, 0.0)[:, :rows].astype(BF)
-        xs.append(jnp.dot(pick, got[z, :rows], preferred_element_type=F32))
-        dy = jnp.dot(pick, got[z, rows : 2 * rows], preferred_element_type=F32)
-        dys.append(gate * dy)
-    out[0] = jnp.concatenate(xs, axis=0).astype(BF)
-    out[1] = jnp.concatenate(dys, axis=0).astype(BF)
-
-
-def own_slots(routing, gates, mix, select_ref):
-    rows = routing.shape[1]
-    shape = E * CAP, rows
+def choose(routing, gates):
+    shape = E * CAP, routing.shape[1]
     index = lax.broadcasted_iota(jnp.int32, shape, 0)
     expert = index // CAP
     is0 = routing[0:1, :] == expert
     chosen = is0 | (routing[1:2, :] == expert)
     flags = jnp.where(chosen, 1.0, 0.0).astype(BF)
-    position = jnp.dot(flags, later(rows), preferred_element_type=F32)
+    position = jnp.dot(flags, later(shape[1]), preferred_element_type=F32)
     select = chosen & (position == (index % CAP).astype(F32))
-    gate = jnp.where(is0, gates[0:1, :], gates[1:2, :])
+    return select, jnp.where(is0, gates[0:1, :], gates[1:2, :])
+
+
+def send_kernel(tokens_in, dy_in, routing_in, gates_in, out, tokens, dy, routing, gates, sem):
+    pairs = (routing_in, routing), (gates_in, gates), (tokens_in, tokens), (dy_in, dy)
+    copies = [
+        pltpu.make_async_copy(a, b, sem.at[n]) for n, (a, b) in enumerate(pairs)
+    ]
+    for copy in copies:
+        copy.start()
+    copies[0].wait()
+    copies[1].wait()
+    select, gate = choose(routing, gates)
+    gate = jnp.sum(jnp.where(select, gate, 0.0), axis=1, keepdims=True)
+    pick = jnp.where(select, 1.0, 0.0).astype(BF)
+    copies[2].wait()
+    copies[3].wait()
+    x = jnp.dot(pick, tokens[...], preferred_element_type=F32)
+    grad = gate * jnp.dot(pick, dy[...], preferred_element_type=F32)
+    for e in range(E):
+        at = slice(e * CAP, (e + 1) * CAP)
+        out[e] = jnp.concatenate([x[at], grad[at]], axis=0).astype(BF)
+
+
+def own_slots(routing, gates, mix, select_ref):
+    rows = routing.shape[1]
+    select, gate = choose(routing, gates)
     i = lax.broadcasted_iota(jnp.int32, (rows, rows), 0)
     j = lax.broadcasted_iota(jnp.int32, (rows, rows), 1)
     eye = jnp.where(i == j, 1.0, 0.0).astype(BF)
@@ -332,27 +305,18 @@
     rows = NY * E * CAP
 
     turned = jnp.swapaxes(routing, 0, 1), jnp.swapaxes(gate_values, 0, 1)
-    packed = jax.ShapeDtypeStruct((2 * tokens.shape[0] + 8, width), BF)
-    packed = pl.pallas_call(
-        pack_kernel,
-        name="pack",
-        out_shape=packed,
+    sources = tokens, out_grad, *turned
+    send = pl.pallas_call(
+        send_kernel,
+        name="send",
+        out_shape=jax.ShapeDtypeStruct((E, 2 * CAP, width), BF),
         in_specs=[pl.BlockSpec(memory_space=pl.ANY)] * 4,
         out_specs=pl.BlockSpec(memory_space=pltpu.VMEM),
-        scratch_shapes=[
-            pltpu.VMEM(turned[0].shape, jnp.int32),
-            pltpu.VMEM(turned[1].shape, F32),
-            pltpu.SemaphoreType.DMA((4,)),
-        ],
-    )(
-        *[
-            pltpu.with_memory_space_constraint(v, pltpu.HBM)
-            for v in (tokens, out_grad, *turned)
-        ]
-    )
-    plane = (lax.axis_index("dp") // NY).reshape(1)
-    got = jax.ShapeDtypeStruct((2, E * CAP, width), BF)
-    got = small(slot_kernel, "slots", got, [plane, gather_z(packed)], 1)
+        scratch_shapes=[pltpu.VMEM(v.shape, v.dtype) for v in sources]
+        + [pltpu.SemaphoreType.DMA((4,))],
+    )(*[pltpu.with_memory_space_constraint(v, pltpu.HBM) for v in sources])
+    got = swap_z(send).reshape(E, 2, CAP, width)
+    got = jnp.swapaxes(got, 0, 1).reshape(2, E * CAP, width)
 
     parts = gather(got, 0)
     token = to_core(parts[3][0, :8])[0]
@@ -360,8 +324,11 @@
     weights = [pltpu.with_memory_space_constraint(w, pltpu.HBM) for w in (wg, wu, w2)]
     infos, near = lax.optimization_barrier((jnp.stack([own_info, other_info]), near))
     bufs = load_weights(infos, *turned, weights, width)
-    own, bufs = lax.optimization_barrier((tuple(gather(near, 1)), tuple(bufs)))
-    other = [to_core(v) for v in own]
+    third, first, second = (swap(near, q, 1) for q in (3, 1, 2))
+    other = tuple(to_core(v) for v in (near, first, second))
+    third, other, bufs = lax.optimization_barrier((third, other, tuple(bufs)))
+    other = [*other, to_core(third)]
+    own = [near, first, second, third]
 
     pre = jax.ShapeDtypeStruct((3 * hidden, rows), F32)
     act = [

time: 135 us -> 120 us (0.89)
  blocking collectives: 43.5 us -> 31.1 us
  waiting for transfers between devices: 47.4 us -> 45.4 us
    all_gather x1 -> x0, blocking collectives: 29.3 us -> none  [gather_z(): return lax.all_gather(v, 'dp', axis_index_groups=Z_GROUPS)]
    all_to_all x1 -> x2, blocking collectives: 14.2 us -> 31.1 us  [swap_z(): return lax.all_to_all(v, 'dp', 0, 0, axis_index_groups=Z_GROUPS, tiled=True)]
    ppermute x12, starting transfers between devices: 18.3 us -> 16.7 us  [swap(): return lax.ppermute(v, ('dp', 'cuts'), perm)]
    ppermute x6, waiting for transfers between devices: 4.62 us -> 3.19 us  [to_core(): return lax.ppermute(v, 'cuts', [(i, i ^ 1) for i in range(2 * NX)])]
    ppermute x6, starting transfers between devices: 1.24 us -> 2.65 us  [to_core(): return lax.ppermute(v, 'cuts', [(i, i ^ 1) for i in range(2 * NX)])]
  transfers between devices with their start and end apart: 18 -> 18, of which waited for: 15 -> 13; matrix products, arithmetic and copies ran while one was open for 0% -> 0% of each run, Pallas kernels for 9% -> 10%
where the time goes in v5:
time: 120 us
  waiting for transfers between devices  45.4 us (38%)
  blocking collectives  31.1 us (26%)
  Pallas kernels  21.2 us (18%)
  starting transfers between devices  19.4 us (16%)
  other arithmetic  1.94 us (2%)
    ppermute x12, waiting for transfers between devices, swap(): return lax.ppermute(v, ('dp', 'cuts'), perm)  42.2 us
    all_to_all x2, blocking collectives, swap_z(): return lax.all_to_all(v, 'dp', 0, 0, axis_index_groups=Z_GROUPS, tiled=True)  31.1 us
    ppermute x12, starting transfers between devices, swap(): return lax.ppermute(v, ('dp', 'cuts'), perm)  16.7 us
    pallas_call x3, Pallas kernels, call(): pl.pallas_call(body, name=name, out_shape=out, in_specs=[pl.BlockSpec(mem...  13 us
    pallas_call x1, Pallas kernels, load_weights(): pl.pallas_call(weights_kernel, name='weights', out_shape=[jax.ShapeDtypeS...  5.52 us
    ppermute x6, waiting for transfers between devices, to_core(): return lax.ppermute(v, 'cuts', [(i, i ^ 1) for i in range(2 * NX)])  3.19 us
    ppermute x6, starting transfers between devices, to_core(): return lax.ppermute(v, 'cuts', [(i, i ^ 1) for i in range(2 * NX)])  2.65 us
  transfers between devices with their start and end apart: 18, of which 13 were waited for; matrix products, arithmetic and copies ran while one was open for 0% of the time, Pallas kernels for 10%

profile of v5, /device:TPU:6, one launch (start us, length us, event | category | flops | bytes accessed | tf_op | source)
XLA Modules:
  0.0 119.9 jit_solution(1659369624932161178)
XLA Ops:
  0.7 1.8 %send.1 = bf16[8,16,768]{2,1,0:T(8,128)(2,1)} custom-call(bf16[16,768]{1,0:T(8,128)(2,1)} %tokens_in.1, bf16[16,768]{1,0:T(8,128)(2,1)} %dy_in.1, s32[2,16]{1,0:T(2,128)} %bitcast.47, f32[2,16]{1,0:T(2,128)} %bitcast.49), custom_call_target="tpu_custom_call" | custom-call | tf_op jit(solution)/shard_map/send/pallas_call | solution.py:309
  2.5 18.9 %all_to_all.10 = bf16[8,16,768]{2,1,0:T(8,128)(2,1)S(1)} all-to-all(bf16[8,16,768]{2,1,0:T(8,128)(2,1)} %send.1), channel_id=1, replica_groups={{0,32,64,96,128,160,192,224},{8,40,72,104,136,168,200,232},{16,48,80,11..., dimensions={0} | all-to-all | bytes 393216 | tf_op jit(solution)/shard_map/all_to_all | solution.py:25
  21.5 3.1 %collective-permute-start.2 = (bf16[2,64,768]{2,1,0:T(8,128)(2,1)S(1)}, bf16[2,64,768]{2,1,0:T(8,128)(2,1)S(1)}, u32[]{:S(2)}, u32[]{:S(2)}) collective-permute-start(bf16[2,64,768]{2,1,0:T(8,128)(2,1)S(1)} %get-tuple-element.83), channel_id=1, source_target_pairs={{0,24},{1,7},{2,26},{3,5},{4,28},{5,3},{6,30},{7,1},{8,16},{9,15},... | collective-permute-start | bytes 589832 | tf_op jit(solution)/shard_map/ppermute | solution.py:45
  24.6 0.1 collective-permute-start.1
  24.7 1.6 %collective-permute-start = (bf16[2,64,768]{2,1,0:T(8,128)(2,1)S(1)}, bf16[2,64,768]{2,1,0:T(8,128)(2,1)S(1)}, u32[]{:S(2)}, u32[]{:S(2)}) collective-permute-start(bf16[2,64,768]{2,1,0:T(8,128)(2,1)S(1)} %get-tuple-element.83), channel_id=1, source_target_pairs={{0,16},{1,5},{2,18},{3,7},{4,20},{5,1},{6,22},{7,3},{8,24},{9,13},... | collective-permute-start | bytes 589832 | tf_op jit(solution)/shard_map/ppermute | solution.py:45
  26.3 2.2 %collective-permute-done.2 = bf16[2,64,768]{2,1,0:T(8,128)(2,1)S(1)} collective-permute-done((bf16[2,64,768]{2,1,0:T(8,128)(2,1)S(1)}, bf16[2,64,768]{2,1,0:T(8,128)(2,1)S(1)}, u32[]{:S(2)}, u32[]{:S(2)}) %collective-permute-start.2) | collective-permute-done | bytes 196640 | tf_op jit(solution)/shard_map/ppermute | solution.py:45
  28.5 1.8 %collective-permute-done.1 = bf16[2,64,768]{2,1,0:T(8,128)(2,1)S(1)} collective-permute-done((bf16[2,64,768]{2,1,0:T(8,128)(2,1)S(1)}, bf16[2,64,768]{2,1,0:T(8,128)(2,1)S(1)}, u32[]{:S(2)}, u32[]{:S(2)}) %collective-permute-start.1) | collective-permute-done | bytes 196640 | tf_op jit(solution)/shard_map/ppermute | solution.py:45
  30.3 1.8 %collective-permute-done = bf16[2,64,768]{2,1,0:T(8,128)(2,1)S(1)} collective-permute-done((bf16[2,64,768]{2,1,0:T(8,128)(2,1)S(1)}, bf16[2,64,768]{2,1,0:T(8,128)(2,1)S(1)}, u32[]{:S(2)}, u32[]{:S(2)}) %collective-permute-start) | collective-permute-done | bytes 196640 | tf_op jit(solution)/shard_map/ppermute | solution.py:45
  32.0 0.0 collective-permute-start.3
  32.0 1.2 collective-permute-done.3
  33.2 0.1 maximum_select_fusion.refs_0_
  33.3 0.6 collective-permute-start.8
  33.9 0.9 collective-permute-start.6
  34.8 1.5 %collective-permute-start.5 = (bf16[4,2,64,768]{3,2,1,0:T(8,128)(2,1)S(1)}, bf16[4,2,64,768]{3,2,1,0:T(8,128)(2,1)S(1)}, u32[]{:S(2)}, u32[]{:S(2)}) collective-permute-start(bf16[4,2,64,768]{3,2,1,0:T(8,128)(2,1)S(1)} %maximum_select_fusion.refs_0_), channel_id=1, source_target_pairs={{0,1},{1,0},{2,3},{3,2},{4,5},{5,4},{6,7},{7,6},{8,9},{9,8},{10,11... | collective-permute-start | bytes 2359304 | tf_op jit(solution)/shard_map/ppermute | solution.py:49
  36.3 1.8 %collective-permute-start.4 = (bf16[4,2,64,768]{3,2,1,0:T(8,128)(2,1)S(1)}, bf16[4,2,64,768]{3,2,1,0:T(8,128)(2,1)S(1)}, u32[]{:S(2)}, u32[]{:S(2)}) collective-permute-start(bf16[4,2,64,768]{3,2,1,0:T(8,128)(2,1)S(1)} %maximum_select_fusion.refs_0_), channel_id=1, source_target_pairs={{0,4},{1,17},{2,6},{3,19},{4,0},{5,21},{6,2},{7,23},{8,12},{9,25},... | collective-permute-start | bytes 2359304 | tf_op jit(solution)/shard_map/ppermute | solution.py:45
  38.1 8.5 %collective-permute-done.8.refs_2_ = bf16[4,2,64,768]{3,2,1,0:T(8,128)(2,1)S(1)} collective-permute-done((bf16[4,2,64,768]{3,2,1,0:T(8,128)(2,1)S(1)}, bf16[4,2,64,768]{3,2,1,0:T(8,128)(2,1)S(1)}, u32[]{:S(2)}, u32[]{:S(2)}) %collective-permute-start.8) | collective-permute-done | bytes 786464 | tf_op jit(solution)/shard_map/ppermute | solution.py:45
  46.6 0.0 collective-permute-start.9
  46.6 0.0 collective-permute-done.6.refs_1_
  46.6 0.5 collective-permute-start.7
  47.2 5.5 %weights.1 = (bf16[4,1056,768]{2,1,0:T(8,128)(2,1)S(1)}, bf16[4,1056,768]{2,1,0:T(8,128)(2,1)S(1)}, bf16[3,16,64]{2,1,0:T(8,128)(2,1)S(1)}, bf16[16,64]{1,0:T(8,128)(2,1)S(1)}) custom-call(s32[2,5]{1,0:T(2,128)S(1)} %pad_add_fusion.infos, s32[2,16]{1,0:T(2,128)S(1)} %bitcast.48, f32[2,16]{1,0:T(2,128)S(1)} %bitcast.50, bf16[352,6144]{1,0:T(8,128)(2,1)} %bitcast.51, ...), custom_call_target="tpu_custom_call" | custom-call | bytes 27262976 | tf_op jit(solution)/shard_map/weights/pallas_call | solution.py:183
  52.7 0.0 collective-permute-done.5.refs_0_
  52.7 3.8 %collective-permute-done.4.refs_3_ = bf16[4,2,64,768]{3,2,1,0:T(8,128)(2,1)S(1)} collective-permute-done((bf16[4,2,64,768]{3,2,1,0:T(8,128)(2,1)S(1)}, bf16[4,2,64,768]{3,2,1,0:T(8,128)(2,1)S(1)}, u32[]{:S(2)}, u32[]{:S(2)}) %collective-permute-start.4) | collective-permute-done | bytes 786464 | tf_op jit(solution)/shard_map/ppermute | solution.py:45
  56.5 0.0 collective-permute-done.9.refs_2_
  56.5 0.0 collective-permute-done.7.refs_1_
  56.5 0.0 collective-permute-start.10
  56.6 3.4 %own.1.refs_5_ = f32[1056,256]{1,0:T(8,128)S(1)} custom-call(s32[5]{0:T(128)S(1)} %get-tuple-element.73.info, bf16[4,2,64,768]{3,2,1,0:T(8,128)(2,1)S(1)} %maximum_select_fusion.refs_0_, bf16[4,2,64,768]{3,2,1,0:T(8,128)(2,1)S(1)} %collective-permute-done.6.refs_1_, bf16[4,2,64,768]{3,2,1,0:T(8,128)(2,1)S(1)} %collective-permute-done.8.refs_2_, ...), custom_call_target="tpu_custom_call" | custom-call | flops 1660944384 | bytes 7340032 | tf_op jit(solution)/shard_map/own/pallas_call | solution.py:275
  59.9 6.4 %other.1 = (bf16[4,4,2,64,768]{4,3,2,1,0:T(8,128)(2,1)S(1)}, bf16[256,352]{1,0:T(8,128)(2,1)S(1)}, bf16[256,704]{1,0:T(8,128)(2,1)S(1)}) custom-call(s32[5]{0:T(128)S(1)} %get-tuple-element.72.info, bf16[4,2,64,768]{3,2,1,0:T(8,128)(2,1)S(1)} %collective-permute-done.5.refs_0_, bf16[4,2,64,768]{3,2,1,0:T(8,128)(2,1)S(1)} %collective-permute-done.7.refs_1_, ...), custom_call_target="tpu_custom_call" | custom-call | flops 3321888768 | bytes 7340032 | tf_op jit(solution)/shard_map/other/pallas_call | solution.py:275
  66.3 0.6 collective-permute-start.11
  66.9 3.3 %last.1 = bf16[4,4,2,64,768]{4,3,2,1,0:T(8,128)(2,1)S(1)} custom-call(s32[5]{0:T(128)S(1)} %get-tuple-element.73.info, bf16[256,352]{1,0:T(8,128)(2,1)S(1)} %get-tuple-element.51.hidden, bf16[256,704]{1,0:T(8,128)(2,1)S(1)} %get-tuple-element.52.grads, bf16[4,1056,768]{2,1,0:T(8,128)(2,1)S(1)} %get-tuple-element.50.refs_4_.buf), custom_call_target="tpu_custom_call" | custom-call | flops 1660944384 | bytes 7340032 | tf_op jit(solution)/shard_map/last/pallas_call | solution.py:275
  70.2 2.0 %collective-permute-done.11 = bf16[4,4,2,64,768]{4,3,2,1,0:T(8,128)(2,1)S(1)} collective-permute-done((bf16[4,4,2,64,768]{4,3,2,1,0:T(8,128)(2,1)S(1)}, bf16[4,4,2,64,768]{4,3,2,1,0:T(8,128)(2,1)S(1)}, u32[]{:S(2)}, u32[]{:S(2)}) %collective-permute-start.11) | collective-permute-done | bytes 3145760 | tf_op jit(solution)/shard_map/ppermute | solution.py:49
  72.2 1.2 %fusion.3 = (bf16[4,2,64,768]{3,2,1,0:T(8,128)(2,1)S(1)}, bf16[4,2,64,768]{3,2,1,0:T(8,128)(2,1)S(1)}, bf16[4,2,64,768]{3,2,1,0:T(8,128)(2,1)S(1)}, bf16[4,2,64,768]{3,2,1,0:T(8,128)(2,1)S(1)}) fusion(bf16[4,4,2,64,768]{4,3,2,1,0:T(8,128)(2,1)S(1)} %collective-permute-done.11, bf16[4,4,2,64,768]{4,3,2,1,0:T(8,128)(2,1)S(1)} %last.1), kind=kLoop, calls=%fused_computation.8 | loop fusion | flops 6291456 | bytes 9437184 | tf_op jit(solution)/shard_map/convert_element_type | solution.py:149
  73.5 0.3 collective-permute-start.12
  73.7 1.2 collective-permute-start.13
  74.9 2.8 %collective-permute-start.14 = (bf16[4,2,64,768]{3,2,1,0:T(8,128)(2,1)S(1)}, bf16[4,2,64,768]{3,2,1,0:T(8,128)(2,1)S(1)}, u32[]{:S(2)}, u32[]{:S(2)}) collective-permute-start(bf16[4,2,64,768]{3,2,1,0:T(8,128)(2,1)S(1)} %get-tuple-element.57), channel_id=1, source_target_pairs={{0,6},{1,25},{2,4},{3,27},{4,2},{5,29},{6,0},{7,31},{8,14},{9,17},... | collective-permute-start | bytes 2359304 | tf_op jit(solution)/shard_map/ppermute | solution.py:45
  77.6 9.5 %collective-permute-done.12 = bf16[4,2,64,768]{3,2,1,0:T(8,128)(2,1)S(1)} collective-permute-done((bf16[4,2,64,768]{3,2,1,0:T(8,128)(2,1)S(1)}, bf16[4,2,64,768]{3,2,1,0:T(8,128)(2,1)S(1)}, u32[]{:S(2)}, u32[]{:S(2)}) %collective-permute-start.12) | collective-permute-done | bytes 786464 | tf_op jit(solution)/shard_map/ppermute | solution.py:45
  87.1 6.2 %collective-permute-done.13 = bf16[4,2,64,768]{3,2,1,0:T(8,128)(2,1)S(1)} collective-permute-done((bf16[4,2,64,768]{3,2,1,0:T(8,128)(2,1)S(1)}, bf16[4,2,64,768]{3,2,1,0:T(8,128)(2,1)S(1)}, u32[]{:S(2)}, u32[]{:S(2)}) %collective-permute-start.13) | collective-permute-done | bytes 786464 | tf_op jit(solution)/shard_map/ppermute | solution.py:45
  93.3 2.2 %collective-permute-done.14 = bf16[4,2,64,768]{3,2,1,0:T(8,128)(2,1)S(1)} collective-permute-done((bf16[4,2,64,768]{3,2,1,0:T(8,128)(2,1)S(1)}, bf16[4,2,64,768]{3,2,1,0:T(8,128)(2,1)S(1)}, u32[]{:S(2)}, u32[]{:S(2)}) %collective-permute-start.14) | collective-permute-done | bytes 786464 | tf_op jit(solution)/shard_map/ppermute | solution.py:45
  95.5 0.4 add_convert_fusion
  95.9 0.1 slice_bitcast_fusion
  96.0 2.0 %collective-permute-start.15 = (bf16[2,64,768]{2,1,0:T(8,128)(2,1)S(1)}, bf16[2,64,768]{2,1,0:T(8,128)(2,1)S(1)}, u32[]{:S(2)}, u32[]{:S(2)}) collective-permute-start(bf16[2,64,768]{2,1,0:T(8,128)(2,1)S(1)} %get-tuple-element.62), channel_id=1, source_target_pairs={{0,16},{1,5},{2,18},{3,7},{4,20},{5,1},{6,22},{7,3},{8,24},{9,13},... | collective-permute-start | bytes 589832 | tf_op jit(solution)/shard_map/ppermute | solution.py:45
  98.0 1.9 %collective-permute-start.16 = (bf16[2,64,768]{2,1,0:T(8,128)(2,1)S(1)}, bf16[2,64,768]{2,1,0:T(8,128)(2,1)S(1)}, u32[]{:S(2)}, u32[]{:S(2)}) collective-permute-start(bf16[2,64,768]{2,1,0:T(8,128)(2,1)S(1)} %get-tuple-element.63), channel_id=1, source_target_pairs={{0,8},{1,3},{2,10},{3,1},{4,12},{5,7},{6,14},{7,5},{8,0},{9,11},{1... | collective-permute-start | bytes 589832 | tf_op jit(solution)/shard_map/ppermute | solution.py:45
  99.9 0.5 collective-permute-start.17
  100.5 2.8 %collective-permute-done.15 = bf16[2,64,768]{2,1,0:T(8,128)(2,1)S(1)} collective-permute-done((bf16[2,64,768]{2,1,0:T(8,128)(2,1)S(1)}, bf16[2,64,768]{2,1,0:T(8,128)(2,1)S(1)}, u32[]{:S(2)}, u32[]{:S(2)}) %collective-permute-start.15) | collective-permute-done | bytes 196640 | tf_op jit(solution)/shard_map/ppermute | solution.py:45
  103.2 2.5 %collective-permute-done.16 = bf16[2,64,768]{2,1,0:T(8,128)(2,1)S(1)} collective-permute-done((bf16[2,64,768]{2,1,0:T(8,128)(2,1)S(1)}, bf16[2,64,768]{2,1,0:T(8,128)(2,1)S(1)}, u32[]{:S(2)}, u32[]{:S(2)}) %collective-permute-start.16) | collective-permute-done | bytes 196640 | tf_op jit(solution)/shard_map/ppermute | solution.py:45
  105.7 1.1 collective-permute-done.17
  106.8 0.1 copy_bitcast_fusion
  106.9 12.2 %all_to_all.11.back = bf16[8,16,768]{2,1,0:T(8,128)(2,1)S(1)} all-to-all(bf16[8,16,768]{2,1,0:T(8,128)(2,1)S(1)} %copy_bitcast_fusion), channel_id=1, replica_groups={{0,32,64,96,128,160,192,224},{8,40,72,104,136,168,200,232},{16,48,80,11..., dimensions={0} | all-to-all | bytes 393216 | tf_op jit(solution)/shard_map/all_to_all | solution.py:25
  119.1 0.8 combine.1
  (11 shorter events, 0.1 us)
Async XLA Ops:
  0.6 46.5 %copy-start = (s32[16,2]{0,1:T(2,128)S(1)}, s32[16,2]{0,1:T(2,128)}, u32[]{:S(2)}) copy-start(s32[16,2]{0,1:T(2,128)} %param.10) | copy-start | bytes 388
  0.6 46.5 %copy-start.1 = (f32[16,2]{0,1:T(2,128)S(1)}, f32[16,2]{0,1:T(2,128)}, u32[]{:S(2)}) copy-start(f32[16,2]{0,1:T(2,128)} %param.9) | copy-start | bytes 388
  21.5 7.0 %collective-permute-start.2 = (bf16[2,64,768]{2,1,0:T(8,128)(2,1)S(1)}, bf16[2,64,768]{2,1,0:T(8,128)(2,1)S(1)}, u32[]{:S(2)}, u32[]{:S(2)}) collective-permute-start(bf16[2,64,768]{2,1,0:T(8,128)(2,1)S(1)} %get-tuple-element.83), channel_id=1, source_target_pairs={{0,24},{1,7},{2,26},{3,5},{4,28},{5,3},{6,30},{7,1},{8,16},{9,15},... | collective-permute-start | bytes 589832 | tf_op jit(solution)/shard_map/ppermute | solution.py:45
  24.6 5.7 %collective-permute-start.1 = (bf16[2,64,768]{2,1,0:T(8,128)(2,1)S(1)}, bf16[2,64,768]{2,1,0:T(8,128)(2,1)S(1)}, u32[]{:S(2)}, u32[]{:S(2)}) collective-permute-start(bf16[2,64,768]{2,1,0:T(8,128)(2,1)S(1)} %get-tuple-element.83), channel_id=1, source_target_pairs={{0,8},{1,3},{2,10},{3,1},{4,12},{5,7},{6,14},{7,5},{8,0},{9,11},{1... | collective-permute-start | bytes 589832 | tf_op jit(solution)/shard_map/ppermute | solution.py:45
  24.7 7.3 %collective-permute-start = (bf16[2,64,768]{2,1,0:T(8,128)(2,1)S(1)}, bf16[2,64,768]{2,1,0:T(8,128)(2,1)S(1)}, u32[]{:S(2)}, u32[]{:S(2)}) collective-permute-start(bf16[2,64,768]{2,1,0:T(8,128)(2,1)S(1)} %get-tuple-element.83), channel_id=1, source_target_pairs={{0,16},{1,5},{2,18},{3,7},{4,20},{5,1},{6,22},{7,3},{8,24},{9,13},... | collective-permute-start | bytes 589832 | tf_op jit(solution)/shard_map/ppermute | solution.py:45
  32.0 1.2 collective-permute-start.3
  33.3 13.3 %collective-permute-start.8 = (bf16[4,2,64,768]{3,2,1,0:T(8,128)(2,1)S(1)}, bf16[4,2,64,768]{3,2,1,0:T(8,128)(2,1)S(1)}, u32[]{:S(2)}, u32[]{:S(2)}) collective-permute-start(bf16[4,2,64,768]{3,2,1,0:T(8,128)(2,1)S(1)} %maximum_select_fusion.refs_0_), channel_id=1, source_target_pairs={{0,6},{1,25},{2,4},{3,27},{4,2},{5,29},{6,0},{7,31},{8,14},{9,17},... | collective-permute-start | bytes 2359304 | tf_op jit(solution)/shard_map/ppermute | solution.py:45
  33.9 12.7 %collective-permute-start.6 = (bf16[4,2,64,768]{3,2,1,0:T(8,128)(2,1)S(1)}, bf16[4,2,64,768]{3,2,1,0:T(8,128)(2,1)S(1)}, u32[]{:S(2)}, u32[]{:S(2)}) collective-permute-start(bf16[4,2,64,768]{3,2,1,0:T(8,128)(2,1)S(1)} %maximum_select_fusion.refs_0_), channel_id=1, source_target_pairs={{0,2},{1,9},{2,0},{3,11},{4,6},{5,13},{6,4},{7,15},{8,10},{9,1},{1... | collective-permute-start | bytes 2359304 | tf_op jit(solution)/shard_map/ppermute | solution.py:45
  34.8 17.9 %collective-permute-start.5 = (bf16[4,2,64,768]{3,2,1,0:T(8,128)(2,1)S(1)}, bf16[4,2,64,768]{3,2,1,0:T(8,128)(2,1)S(1)}, u32[]{:S(2)}, u32[]{:S(2)}) collective-permute-start(bf16[4,2,64,768]{3,2,1,0:T(8,128)(2,1)S(1)} %maximum_select_fusion.refs_0_), channel_id=1, source_target_pairs={{0,1},{1,0},{2,3},{3,2},{4,5},{5,4},{6,7},{7,6},{8,9},{9,8},{10,11... | collective-permute-start | bytes 2359304 | tf_op jit(solution)/shard_map/ppermute | solution.py:49
  36.3 20.2 %collective-permute-start.4 = (bf16[4,2,64,768]{3,2,1,0:T(8,128)(2,1)S(1)}, bf16[4,2,64,768]{3,2,1,0:T(8,128)(2,1)S(1)}, u32[]{:S(2)}, u32[]{:S(2)}) collective-permute-start(bf16[4,2,64,768]{3,2,1,0:T(8,128)(2,1)S(1)} %maximum_select_fusion.refs_0_), channel_id=1, source_target_pairs={{0,4},{1,17},{2,6},{3,19},{4,0},{5,21},{6,2},{7,23},{8,12},{9,25},... | collective-permute-start | bytes 2359304 | tf_op jit(solution)/shard_map/ppermute | solution.py:45
  46.6 9.9 %collective-permute-start.9 = (bf16[4,2,64,768]{3,2,1,0:T(8,128)(2,1)S(1)}, bf16[4,2,64,768]{3,2,1,0:T(8,128)(2,1)S(1)}, u32[]{:S(2)}, u32[]{:S(2)}) collective-permute-start(bf16[4,2,64,768]{3,2,1,0:T(8,128)(2,1)S(1)} %collective-permute-done.8.refs_2_), channel_id=1, source_target_pairs={{0,1},{1,0},{2,3},{3,2},{4,5},{5,4},{6,7},{7,6},{8,9},{9,8},{10,11... | collective-permute-start | bytes 2359304 | tf_op jit(solution)/shard_map/ppermute | solution.py:49
  46.6 9.9 %collective-permute-start.7 = (bf16[4,2,64,768]{3,2,1,0:T(8,128)(2,1)S(1)}, bf16[4,2,64,768]{3,2,1,0:T(8,128)(2,1)S(1)}, u32[]{:S(2)}, u32[]{:S(2)}) collective-permute-start(bf16[4,2,64,768]{3,2,1,0:T(8,128)(2,1)S(1)} %collective-permute-done.6.refs_1_), channel_id=1, source_target_pairs={{0,1},{1,0},{2,3},{3,2},{4,5},{5,4},{6,7},{7,6},{8,9},{9,8},{10,11... | collective-permute-start | bytes 2359304 | tf_op jit(solution)/shard_map/ppermute | solution.py:49
  56.5 3.4 %collective-permute-start.10 = (bf16[4,2,64,768]{3,2,1,0:T(8,128)(2,1)S(1)}, bf16[4,2,64,768]{3,2,1,0:T(8,128)(2,1)S(1)}, u32[]{:S(2)}, u32[]{:S(2)}) collective-permute-start(bf16[4,2,64,768]{3,2,1,0:T(8,128)(2,1)S(1)} %collective-permute-done.4.refs_3_), channel_id=1, source_target_pairs={{0,1},{1,0},{2,3},{3,2},{4,5},{5,4},{6,7},{7,6},{8,9},{9,8},{10,11... | collective-permute-start | bytes 2359304 | tf_op jit(solution)/shard_map/ppermute | solution.py:49
  66.3 5.9 %collective-permute-start.11 = (bf16[4,4,2,64,768]{4,3,2,1,0:T(8,128)(2,1)S(1)}, bf16[4,4,2,64,768]{4,3,2,1,0:T(8,128)(2,1)S(1)}, u32[]{:S(2)}, u32[]{:S(2)}) collective-permute-start(bf16[4,4,2,64,768]{4,3,2,1,0:T(8,128)(2,1)S(1)} %get-tuple-element.53), channel_id=1, source_target_pairs={{0,1},{1,0},{2,3},{3,2},{4,5},{5,4},{6,7},{7,6},{8,9},{9,8},{10,11... | collective-permute-start | bytes 9437192 | tf_op jit(solution)/shard_map/ppermute | solution.py:49
  73.5 13.7 %collective-permute-start.12 = (bf16[4,2,64,768]{3,2,1,0:T(8,128)(2,1)S(1)}, bf16[4,2,64,768]{3,2,1,0:T(8,128)(2,1)S(1)}, u32[]{:S(2)}, u32[]{:S(2)}) collective-permute-start(bf16[4,2,64,768]{3,2,1,0:T(8,128)(2,1)S(1)} %get-tuple-element.55), channel_id=1, source_target_pairs={{0,4},{1,17},{2,6},{3,19},{4,0},{5,21},{6,2},{7,23},{8,12},{9,25},... | collective-permute-start | bytes 2359304 | tf_op jit(solution)/shard_map/ppermute | solution.py:45
  73.7 19.6 %collective-permute-start.13 = (bf16[4,2,64,768]{3,2,1,0:T(8,128)(2,1)S(1)}, bf16[4,2,64,768]{3,2,1,0:T(8,128)(2,1)S(1)}, u32[]{:S(2)}, u32[]{:S(2)}) collective-permute-start(bf16[4,2,64,768]{3,2,1,0:T(8,128)(2,1)S(1)} %get-tuple-element.56), channel_id=1, source_target_pairs={{0,2},{1,9},{2,0},{3,11},{4,6},{5,13},{6,4},{7,15},{8,10},{9,1},{1... | collective-permute-start | bytes 2359304 | tf_op jit(solution)/shard_map/ppermute | solution.py:45
  74.9 20.6 %collective-permute-start.14 = (bf16[4,2,64,768]{3,2,1,0:T(8,128)(2,1)S(1)}, bf16[4,2,64,768]{3,2,1,0:T(8,128)(2,1)S(1)}, u32[]{:S(2)}, u32[]{:S(2)}) collective-permute-start(bf16[4,2,64,768]{3,2,1,0:T(8,128)(2,1)S(1)} %get-tuple-element.57), channel_id=1, source_target_pairs={{0,6},{1,25},{2,4},{3,27},{4,2},{5,29},{6,0},{7,31},{8,14},{9,17},... | collective-permute-start | bytes 2359304 | tf_op jit(solution)/shard_map/ppermute | solution.py:45
  96.0 7.3 %collective-permute-start.15 = (bf16[2,64,768]{2,1,0:T(8,128)(2,1)S(1)}, bf16[2,64,768]{2,1,0:T(8,128)(2,1)S(1)}, u32[]{:S(2)}, u32[]{:S(2)}) collective-permute-start(bf16[2,64,768]{2,1,0:T(8,128)(2,1)S(1)} %get-tuple-element.62), channel_id=1, source_target_pairs={{0,16},{1,5},{2,18},{3,7},{4,20},{5,1},{6,22},{7,3},{8,24},{9,13},... | collective-permute-start | bytes 589832 | tf_op jit(solution)/shard_map/ppermute | solution.py:45
  98.0 7.7 %collective-permute-start.16 = (bf16[2,64,768]{2,1,0:T(8,128)(2,1)S(1)}, bf16[2,64,768]{2,1,0:T(8,128)(2,1)S(1)}, u32[]{:S(2)}, u32[]{:S(2)}) collective-permute-start(bf16[2,64,768]{2,1,0:T(8,128)(2,1)S(1)} %get-tuple-element.63), channel_id=1, source_target_pairs={{0,8},{1,3},{2,10},{3,1},{4,12},{5,7},{6,14},{7,5},{8,0},{9,11},{1... | collective-permute-start | bytes 589832 | tf_op jit(solution)/shard_map/ppermute | solution.py:45
  99.9 6.9 %collective-permute-start.17 = (bf16[2,64,768]{2,1,0:T(8,128)(2,1)S(1)}, bf16[2,64,768]{2,1,0:T(8,128)(2,1)S(1)}, u32[]{:S(2)}, u32[]{:S(2)}) collective-permute-start(bf16[2,64,768]{2,1,0:T(8,128)(2,1)S(1)} %get-tuple-element.64), channel_id=1, source_target_pairs={{0,24},{1,7},{2,26},{3,5},{4,28},{5,3},{6,30},{7,1},{8,16},{9,15},... | collective-permute-start | bytes 589832 | tf_op jit(solution)/shard_map/ppermute | solution.py:45

commit v6 on v5

--- a/solution.py
+++ b/solution.py
@@ -18,7 +18,7 @@
 VMEM_LIMIT = {"own": 8, "other": 12, "last": 4}
 
 
-Z_GROUPS = [[z * NY + y for z in range(E)] for y in range(NY)]
+Z_GROUPS = [[z * NY + y for z in reversed(range(E))] for y in range(NY)]
 
 
 def swap_z(v):
@@ -92,7 +92,7 @@
     grad = gate * jnp.dot(pick, dy[...], preferred_element_type=F32)
     for e in range(E):
         at = slice(e * CAP, (e + 1) * CAP)
-        out[e] = jnp.concatenate([x[at], grad[at]], axis=0).astype(BF)
+        out[E - 1 - e] = jnp.concatenate([x[at], grad[at]], axis=0).astype(BF)
 
 
 def own_slots(routing, gates, mix, select_ref):
@@ -112,7 +112,7 @@
 
 def combine_kernel(back, mix, select, mixed, grad):
     def rows(at):
-        parts = [back[e, at : at + CAP].astype(F32) for e in range(E)]
+        parts = [back[E - 1 - e, at : at + CAP].astype(F32) for e in range(E)]
         return jnp.concatenate(parts, axis=0).astype(BF)
 
     y, dx = rows(0), rows(CAP)

time: 120 us -> 118 us (0.983)
  blocking collectives: 31.1 us -> 28.6 us
    all_to_all x2, blocking collectives: 31.1 us -> 28.6 us  [swap_z(): return lax.all_to_all(v, 'dp', 0, 0, axis_index_groups=Z_GROUPS, tiled=True)]
where the time goes in v6:
time: 118 us; the launch traced here: 117 us
  waiting for transfers between devices  45.4 us (38%)
  blocking collectives  28.6 us (24%)
  Pallas kernels  21.2 us (18%)
  starting transfers between devices  19.4 us (16%)
  other arithmetic  1.94 us (2%)
    ppermute x12, waiting for transfers between devices, swap(): return lax.ppermute(v, ('dp', 'cuts'), perm)  42.2 us
    all_to_all x2, blocking collectives, swap_z(): return lax.all_to_all(v, 'dp', 0, 0, axis_index_groups=Z_GROUPS, tiled=True)  28.6 us
    ppermute x12, starting transfers between devices, swap(): return lax.ppermute(v, ('dp', 'cuts'), perm)  16.8 us
    pallas_call x3, Pallas kernels, call(): pl.pallas_call(body, name=name, out_shape=out, in_specs=[pl.BlockSpec(mem...  13 us
    pallas_call x1, Pallas kernels, load_weights(): pl.pallas_call(weights_kernel, name='weights', out_shape=[jax.ShapeDtypeS...  5.52 us
    ppermute x6, waiting for transfers between devices, to_core(): return lax.ppermute(v, 'cuts', [(i, i ^ 1) for i in range(2 * NX)])  3.19 us
    ppermute x6, starting transfers between devices, to_core(): return lax.ppermute(v, 'cuts', [(i, i ^ 1) for i in range(2 * NX)])  2.63 us
  transfers between devices with their start and end apart: 18, of which 13 were waited for; matrix products, arithmetic and copies ran while one was open for 0% of the time, Pallas kernels for 10%

profile of v6, /device:TPU:6, one launch (start us, length us, event | category | flops | bytes accessed | tf_op | source)
XLA Modules:
  0.0 117.3 jit_solution(8949686215722010261)
XLA Ops:
  0.7 1.8 %send.1 = bf16[8,16,768]{2,1,0:T(8,128)(2,1)} custom-call(bf16[16,768]{1,0:T(8,128)(2,1)} %tokens_in.1, bf16[16,768]{1,0:T(8,128)(2,1)} %dy_in.1, s32[2,16]{1,0:T(2,128)} %bitcast.47, f32[2,16]{1,0:T(2,128)} %bitcast.49), custom_call_target="tpu_custom_call" | custom-call | tf_op jit(solution)/shard_map/send/pallas_call | solution.py:309
  2.5 15.6 %all_to_all.10 = bf16[8,16,768]{2,1,0:T(8,128)(2,1)S(1)} all-to-all(bf16[8,16,768]{2,1,0:T(8,128)(2,1)} %send.1), channel_id=1, replica_groups={{224,192,160,128,96,64,32,0},{232,200,168,136,104,72,40,8},{240,208,176..., dimensions={0} | all-to-all | bytes 393216 | tf_op jit(solution)/shard_map/all_to_all | solution.py:25
  18.2 3.1 %collective-permute-start.2 = (bf16[2,64,768]{2,1,0:T(8,128)(2,1)S(1)}, bf16[2,64,768]{2,1,0:T(8,128)(2,1)S(1)}, u32[]{:S(2)}, u32[]{:S(2)}) collective-permute-start(bf16[2,64,768]{2,1,0:T(8,128)(2,1)S(1)} %get-tuple-element.83), channel_id=1, source_target_pairs={{0,24},{1,7},{2,26},{3,5},{4,28},{5,3},{6,30},{7,1},{8,16},{9,15},... | collective-permute-start | bytes 589832 | tf_op jit(solution)/shard_map/ppermute | solution.py:45
  21.3 0.1 collective-permute-start.1
  21.4 1.6 %collective-permute-start = (bf16[2,64,768]{2,1,0:T(8,128)(2,1)S(1)}, bf16[2,64,768]{2,1,0:T(8,128)(2,1)S(1)}, u32[]{:S(2)}, u32[]{:S(2)}) collective-permute-start(bf16[2,64,768]{2,1,0:T(8,128)(2,1)S(1)} %get-tuple-element.83), channel_id=1, source_target_pairs={{0,16},{1,5},{2,18},{3,7},{4,20},{5,1},{6,22},{7,3},{8,24},{9,13},... | collective-permute-start | bytes 589832 | tf_op jit(solution)/shard_map/ppermute | solution.py:45
  23.0 2.2 %collective-permute-done.2 = bf16[2,64,768]{2,1,0:T(8,128)(2,1)S(1)} collective-permute-done((bf16[2,64,768]{2,1,0:T(8,128)(2,1)S(1)}, bf16[2,64,768]{2,1,0:T(8,128)(2,1)S(1)}, u32[]{:S(2)}, u32[]{:S(2)}) %collective-permute-start.2) | collective-permute-done | bytes 196640 | tf_op jit(solution)/shard_map/ppermute | solution.py:45
  25.1 1.8 %collective-permute-done.1 = bf16[2,64,768]{2,1,0:T(8,128)(2,1)S(1)} collective-permute-done((bf16[2,64,768]{2,1,0:T(8,128)(2,1)S(1)}, bf16[2,64,768]{2,1,0:T(8,128)(2,1)S(1)}, u32[]{:S(2)}, u32[]{:S(2)}) %collective-permute-start.1) | collective-permute-done | bytes 196640 | tf_op jit(solution)/shard_map/ppermute | solution.py:45
  26.9 1.8 %collective-permute-done = bf16[2,64,768]{2,1,0:T(8,128)(2,1)S(1)} collective-permute-done((bf16[2,64,768]{2,1,0:T(8,128)(2,1)S(1)}, bf16[2,64,768]{2,1,0:T(8,128)(2,1)S(1)}, u32[]{:S(2)}, u32[]{:S(2)}) %collective-permute-start) | collective-permute-done | bytes 196640 | tf_op jit(solution)/shard_map/ppermute | solution.py:45
  28.7 0.0 collective-permute-start.3
  28.7 1.2 collective-permute-done.3
  29.9 0.1 maximum_select_fusion.refs_0_
  30.0 0.6 collective-permute-start.8
  30.6 0.9 collective-permute-start.6
  31.5 1.5 %collective-permute-start.5 = (bf16[4,2,64,768]{3,2,1,0:T(8,128)(2,1)S(1)}, bf16[4,2,64,768]{3,2,1,0:T(8,128)(2,1)S(1)}, u32[]{:S(2)}, u32[]{:S(2)}) collective-permute-start(bf16[4,2,64,768]{3,2,1,0:T(8,128)(2,1)S(1)} %maximum_select_fusion.refs_0_), channel_id=1, source_target_pairs={{0,1},{1,0},{2,3},{3,2},{4,5},{5,4},{6,7},{7,6},{8,9},{9,8},{10,11... | collective-permute-start | bytes 2359304 | tf_op jit(solution)/shard_map/ppermute | solution.py:49
  33.0 1.8 %collective-permute-start.4 = (bf16[4,2,64,768]{3,2,1,0:T(8,128)(2,1)S(1)}, bf16[4,2,64,768]{3,2,1,0:T(8,128)(2,1)S(1)}, u32[]{:S(2)}, u32[]{:S(2)}) collective-permute-start(bf16[4,2,64,768]{3,2,1,0:T(8,128)(2,1)S(1)} %maximum_select_fusion.refs_0_), channel_id=1, source_target_pairs={{0,4},{1,17},{2,6},{3,19},{4,0},{5,21},{6,2},{7,23},{8,12},{9,25},... | collective-permute-start | bytes 2359304 | tf_op jit(solution)/shard_map/ppermute | solution.py:45
  34.8 8.5 %collective-permute-done.8.refs_2_ = bf16[4,2,64,768]{3,2,1,0:T(8,128)(2,1)S(1)} collective-permute-done((bf16[4,2,64,768]{3,2,1,0:T(8,128)(2,1)S(1)}, bf16[4,2,64,768]{3,2,1,0:T(8,128)(2,1)S(1)}, u32[]{:S(2)}, u32[]{:S(2)}) %collective-permute-start.8) | collective-permute-done | bytes 786464 | tf_op jit(solution)/shard_map/ppermute | solution.py:45
  43.3 0.0 collective-permute-start.9
  43.3 0.0 collective-permute-done.6.refs_1_
  43.3 0.5 collective-permute-start.7
  43.9 5.5 %weights.1 = (bf16[4,1056,768]{2,1,0:T(8,128)(2,1)S(1)}, bf16[4,1056,768]{2,1,0:T(8,128)(2,1)S(1)}, bf16[3,16,64]{2,1,0:T(8,128)(2,1)S(1)}, bf16[16,64]{1,0:T(8,128)(2,1)S(1)}) custom-call(s32[2,5]{1,0:T(2,128)S(1)} %pad_add_fusion.infos, s32[2,16]{1,0:T(2,128)S(1)} %bitcast.48, f32[2,16]{1,0:T(2,128)S(1)} %bitcast.50, bf16[352,6144]{1,0:T(8,128)(2,1)} %bitcast.51, ...), custom_call_target="tpu_custom_call" | custom-call | bytes 27262976 | tf_op jit(solution)/shard_map/weights/pallas_call | solution.py:183
  49.4 0.0 collective-permute-done.5.refs_0_
  49.4 3.8 %collective-permute-done.4.refs_3_ = bf16[4,2,64,768]{3,2,1,0:T(8,128)(2,1)S(1)} collective-permute-done((bf16[4,2,64,768]{3,2,1,0:T(8,128)(2,1)S(1)}, bf16[4,2,64,768]{3,2,1,0:T(8,128)(2,1)S(1)}, u32[]{:S(2)}, u32[]{:S(2)}) %collective-permute-start.4) | collective-permute-done | bytes 786464 | tf_op jit(solution)/shard_map/ppermute | solution.py:45
  53.2 0.0 collective-permute-done.7.refs_1_
  53.2 0.0 collective-permute-start.10
  53.2 3.4 %own.1.refs_5_ = f32[1056,256]{1,0:T(8,128)S(1)} custom-call(s32[5]{0:T(128)S(1)} %get-tuple-element.73.info, bf16[4,2,64,768]{3,2,1,0:T(8,128)(2,1)S(1)} %maximum_select_fusion.refs_0_, bf16[4,2,64,768]{3,2,1,0:T(8,128)(2,1)S(1)} %collective-permute-done.6.refs_1_, bf16[4,2,64,768]{3,2,1,0:T(8,128)(2,1)S(1)} %collective-permute-done.8.refs_2_, ...), custom_call_target="tpu_custom_call" | custom-call | flops 1660944384 | bytes 7340032 | tf_op jit(solution)/shard_map/own/pallas_call | solution.py:275
  56.6 0.0 collective-permute-done.10.refs_3_
  56.6 6.4 %other.1 = (bf16[4,4,2,64,768]{4,3,2,1,0:T(8,128)(2,1)S(1)}, bf16[256,352]{1,0:T(8,128)(2,1)S(1)}, bf16[256,704]{1,0:T(8,128)(2,1)S(1)}) custom-call(s32[5]{0:T(128)S(1)} %get-tuple-element.72.info, bf16[4,2,64,768]{3,2,1,0:T(8,128)(2,1)S(1)} %collective-permute-done.5.refs_0_, bf16[4,2,64,768]{3,2,1,0:T(8,128)(2,1)S(1)} %collective-permute-done.7.refs_1_, ...), custom_call_target="tpu_custom_call" | custom-call | flops 3321888768 | bytes 7340032 | tf_op jit(solution)/shard_map/other/pallas_call | solution.py:275
  63.0 0.6 collective-permute-start.11
  63.6 3.3 %last.1 = bf16[4,4,2,64,768]{4,3,2,1,0:T(8,128)(2,1)S(1)} custom-call(s32[5]{0:T(128)S(1)} %get-tuple-element.73.info, bf16[256,352]{1,0:T(8,128)(2,1)S(1)} %get-tuple-element.51.hidden, bf16[256,704]{1,0:T(8,128)(2,1)S(1)} %get-tuple-element.52.grads, bf16[4,1056,768]{2,1,0:T(8,128)(2,1)S(1)} %get-tuple-element.50.refs_4_.buf), custom_call_target="tpu_custom_call" | custom-call | flops 1660944384 | bytes 7340032 | tf_op jit(solution)/shard_map/last/pallas_call | solution.py:275
  66.9 2.0 %collective-permute-done.11 = bf16[4,4,2,64,768]{4,3,2,1,0:T(8,128)(2,1)S(1)} collective-permute-done((bf16[4,4,2,64,768]{4,3,2,1,0:T(8,128)(2,1)S(1)}, bf16[4,4,2,64,768]{4,3,2,1,0:T(8,128)(2,1)S(1)}, u32[]{:S(2)}, u32[]{:S(2)}) %collective-permute-start.11) | collective-permute-done | bytes 3145760 | tf_op jit(solution)/shard_map/ppermute | solution.py:49
  68.9 1.2 %fusion.3 = (bf16[4,2,64,768]{3,2,1,0:T(8,128)(2,1)S(1)}, bf16[4,2,64,768]{3,2,1,0:T(8,128)(2,1)S(1)}, bf16[4,2,64,768]{3,2,1,0:T(8,128)(2,1)S(1)}, bf16[4,2,64,768]{3,2,1,0:T(8,128)(2,1)S(1)}) fusion(bf16[4,4,2,64,768]{4,3,2,1,0:T(8,128)(2,1)S(1)} %collective-permute-done.11, bf16[4,4,2,64,768]{4,3,2,1,0:T(8,128)(2,1)S(1)} %last.1), kind=kLoop, calls=%fused_computation.8 | loop fusion | flops 6291456 | bytes 9437184 | tf_op jit(solution)/shard_map/convert_element_type | solution.py:149
  70.1 0.3 collective-permute-start.12
  70.4 1.1 collective-permute-start.13
  71.5 2.8 %collective-permute-start.14 = (bf16[4,2,64,768]{3,2,1,0:T(8,128)(2,1)S(1)}, bf16[4,2,64,768]{3,2,1,0:T(8,128)(2,1)S(1)}, u32[]{:S(2)}, u32[]{:S(2)}) collective-permute-start(bf16[4,2,64,768]{3,2,1,0:T(8,128)(2,1)S(1)} %get-tuple-element.57), channel_id=1, source_target_pairs={{0,6},{1,25},{2,4},{3,27},{4,2},{5,29},{6,0},{7,31},{8,14},{9,17},... | collective-permute-start | bytes 2359304 | tf_op jit(solution)/shard_map/ppermute | solution.py:45
  74.3 9.5 %collective-permute-done.12 = bf16[4,2,64,768]{3,2,1,0:T(8,128)(2,1)S(1)} collective-permute-done((bf16[4,2,64,768]{3,2,1,0:T(8,128)(2,1)S(1)}, bf16[4,2,64,768]{3,2,1,0:T(8,128)(2,1)S(1)}, u32[]{:S(2)}, u32[]{:S(2)}) %collective-permute-start.12) | collective-permute-done | bytes 786464 | tf_op jit(solution)/shard_map/ppermute | solution.py:45
  83.8 6.2 %collective-permute-done.13 = bf16[4,2,64,768]{3,2,1,0:T(8,128)(2,1)S(1)} collective-permute-done((bf16[4,2,64,768]{3,2,1,0:T(8,128)(2,1)S(1)}, bf16[4,2,64,768]{3,2,1,0:T(8,128)(2,1)S(1)}, u32[]{:S(2)}, u32[]{:S(2)}) %collective-permute-start.13) | collective-permute-done | bytes 786464 | tf_op jit(solution)/shard_map/ppermute | solution.py:45
  90.0 2.2 %collective-permute-done.14 = bf16[4,2,64,768]{3,2,1,0:T(8,128)(2,1)S(1)} collective-permute-done((bf16[4,2,64,768]{3,2,1,0:T(8,128)(2,1)S(1)}, bf16[4,2,64,768]{3,2,1,0:T(8,128)(2,1)S(1)}, u32[]{:S(2)}, u32[]{:S(2)}) %collective-permute-start.14) | collective-permute-done | bytes 786464 | tf_op jit(solution)/shard_map/ppermute | solution.py:45
  92.1 0.4 add_convert_fusion
  92.6 0.1 slice_bitcast_fusion
  92.6 2.1 %collective-permute-start.15 = (bf16[2,64,768]{2,1,0:T(8,128)(2,1)S(1)}, bf16[2,64,768]{2,1,0:T(8,128)(2,1)S(1)}, u32[]{:S(2)}, u32[]{:S(2)}) collective-permute-start(bf16[2,64,768]{2,1,0:T(8,128)(2,1)S(1)} %get-tuple-element.62), channel_id=1, source_target_pairs={{0,16},{1,5},{2,18},{3,7},{4,20},{5,1},{6,22},{7,3},{8,24},{9,13},... | collective-permute-start | bytes 589832 | tf_op jit(solution)/shard_map/ppermute | solution.py:45
  94.7 1.9 %collective-permute-start.16 = (bf16[2,64,768]{2,1,0:T(8,128)(2,1)S(1)}, bf16[2,64,768]{2,1,0:T(8,128)(2,1)S(1)}, u32[]{:S(2)}, u32[]{:S(2)}) collective-permute-start(bf16[2,64,768]{2,1,0:T(8,128)(2,1)S(1)} %get-tuple-element.63), channel_id=1, source_target_pairs={{0,8},{1,3},{2,10},{3,1},{4,12},{5,7},{6,14},{7,5},{8,0},{9,11},{1... | collective-permute-start | bytes 589832 | tf_op jit(solution)/shard_map/ppermute | solution.py:45
  96.6 0.6 collective-permute-start.17
  97.2 2.7 %collective-permute-done.15 = bf16[2,64,768]{2,1,0:T(8,128)(2,1)S(1)} collective-permute-done((bf16[2,64,768]{2,1,0:T(8,128)(2,1)S(1)}, bf16[2,64,768]{2,1,0:T(8,128)(2,1)S(1)}, u32[]{:S(2)}, u32[]{:S(2)}) %collective-permute-start.15) | collective-permute-done | bytes 196640 | tf_op jit(solution)/shard_map/ppermute | solution.py:45
  99.9 2.5 %collective-permute-done.16 = bf16[2,64,768]{2,1,0:T(8,128)(2,1)S(1)} collective-permute-done((bf16[2,64,768]{2,1,0:T(8,128)(2,1)S(1)}, bf16[2,64,768]{2,1,0:T(8,128)(2,1)S(1)}, u32[]{:S(2)}, u32[]{:S(2)}) %collective-permute-start.16) | collective-permute-done | bytes 196640 | tf_op jit(solution)/shard_map/ppermute | solution.py:45
  102.3 1.1 collective-permute-done.17
  103.5 0.1 copy_bitcast_fusion
  103.6 13.0 %all_to_all.11.back = bf16[8,16,768]{2,1,0:T(8,128)(2,1)S(1)} all-to-all(bf16[8,16,768]{2,1,0:T(8,128)(2,1)S(1)} %copy_bitcast_fusion), channel_id=1, replica_groups={{224,192,160,128,96,64,32,0},{232,200,168,136,104,72,40,8},{240,208,176..., dimensions={0} | all-to-all | bytes 393216 | tf_op jit(solution)/shard_map/all_to_all | solution.py:25
  116.6 0.8 combine.1
  (11 shorter events, 0.1 us)
Async XLA Ops:
  0.6 43.2 %copy-start = (s32[16,2]{0,1:T(2,128)S(1)}, s32[16,2]{0,1:T(2,128)}, u32[]{:S(2)}) copy-start(s32[16,2]{0,1:T(2,128)} %param.10) | copy-start | bytes 388
  0.6 43.2 %copy-start.1 = (f32[16,2]{0,1:T(2,128)S(1)}, f32[16,2]{0,1:T(2,128)}, u32[]{:S(2)}) copy-start(f32[16,2]{0,1:T(2,128)} %param.9) | copy-start | bytes 388
  18.2 7.0 %collective-permute-start.2 = (bf16[2,64,768]{2,1,0:T(8,128)(2,1)S(1)}, bf16[2,64,768]{2,1,0:T(8,128)(2,1)S(1)}, u32[]{:S(2)}, u32[]{:S(2)}) collective-permute-start(bf16[2,64,768]{2,1,0:T(8,128)(2,1)S(1)} %get-tuple-element.83), channel_id=1, source_target_pairs={{0,24},{1,7},{2,26},{3,5},{4,28},{5,3},{6,30},{7,1},{8,16},{9,15},... | collective-permute-start | bytes 589832 | tf_op jit(solution)/shard_map/ppermute | solution.py:45
  21.3 5.7 %collective-permute-start.1 = (bf16[2,64,768]{2,1,0:T(8,128)(2,1)S(1)}, bf16[2,64,768]{2,1,0:T(8,128)(2,1)S(1)}, u32[]{:S(2)}, u32[]{:S(2)}) collective-permute-start(bf16[2,64,768]{2,1,0:T(8,128)(2,1)S(1)} %get-tuple-element.83), channel_id=1, source_target_pairs={{0,8},{1,3},{2,10},{3,1},{4,12},{5,7},{6,14},{7,5},{8,0},{9,11},{1... | collective-permute-start | bytes 589832 | tf_op jit(solution)/shard_map/ppermute | solution.py:45
  21.4 7.3 %collective-permute-start = (bf16[2,64,768]{2,1,0:T(8,128)(2,1)S(1)}, bf16[2,64,768]{2,1,0:T(8,128)(2,1)S(1)}, u32[]{:S(2)}, u32[]{:S(2)}) collective-permute-start(bf16[2,64,768]{2,1,0:T(8,128)(2,1)S(1)} %get-tuple-element.83), channel_id=1, source_target_pairs={{0,16},{1,5},{2,18},{3,7},{4,20},{5,1},{6,22},{7,3},{8,24},{9,13},... | collective-permute-start | bytes 589832 | tf_op jit(solution)/shard_map/ppermute | solution.py:45
  28.7 1.2 %collective-permute-start.3 = (bf16[8,768]{1,0:T(8,128)(2,1)S(1)}, bf16[8,768]{1,0:T(8,128)(2,1)S(1)}, u32[]{:S(2)}, u32[]{:S(2)}) collective-permute-start(bf16[8,768]{1,0:T(8,128)(2,1)S(1)} %slice_bitcast_fusion.4), channel_id=1, source_target_pairs={{0,1},{1,0},{2,3},{3,2},{4,5},{5,4},{6,7},{7,6},{8,9},{9,8},{10,11... | collective-permute-start | bytes 36872 | tf_op jit(solution)/shard_map/ppermute | solution.py:49
  30.0 13.3 %collective-permute-start.8 = (bf16[4,2,64,768]{3,2,1,0:T(8,128)(2,1)S(1)}, bf16[4,2,64,768]{3,2,1,0:T(8,128)(2,1)S(1)}, u32[]{:S(2)}, u32[]{:S(2)}) collective-permute-start(bf16[4,2,64,768]{3,2,1,0:T(8,128)(2,1)S(1)} %maximum_select_fusion.refs_0_), channel_id=1, source_target_pairs={{0,6},{1,25},{2,4},{3,27},{4,2},{5,29},{6,0},{7,31},{8,14},{9,17},... | collective-permute-start | bytes 2359304 | tf_op jit(solution)/shard_map/ppermute | solution.py:45
  30.6 12.7 %collective-permute-start.6 = (bf16[4,2,64,768]{3,2,1,0:T(8,128)(2,1)S(1)}, bf16[4,2,64,768]{3,2,1,0:T(8,128)(2,1)S(1)}, u32[]{:S(2)}, u32[]{:S(2)}) collective-permute-start(bf16[4,2,64,768]{3,2,1,0:T(8,128)(2,1)S(1)} %maximum_select_fusion.refs_0_), channel_id=1, source_target_pairs={{0,2},{1,9},{2,0},{3,11},{4,6},{5,13},{6,4},{7,15},{8,10},{9,1},{1... | collective-permute-start | bytes 2359304 | tf_op jit(solution)/shard_map/ppermute | solution.py:45
  31.5 17.9 %collective-permute-start.5 = (bf16[4,2,64,768]{3,2,1,0:T(8,128)(2,1)S(1)}, bf16[4,2,64,768]{3,2,1,0:T(8,128)(2,1)S(1)}, u32[]{:S(2)}, u32[]{:S(2)}) collective-permute-start(bf16[4,2,64,768]{3,2,1,0:T(8,128)(2,1)S(1)} %maximum_select_fusion.refs_0_), channel_id=1, source_target_pairs={{0,1},{1,0},{2,3},{3,2},{4,5},{5,4},{6,7},{7,6},{8,9},{9,8},{10,11... | collective-permute-start | bytes 2359304 | tf_op jit(solution)/shard_map/ppermute | solution.py:49
  33.0 20.2 %collective-permute-start.4 = (bf16[4,2,64,768]{3,2,1,0:T(8,128)(2,1)S(1)}, bf16[4,2,64,768]{3,2,1,0:T(8,128)(2,1)S(1)}, u32[]{:S(2)}, u32[]{:S(2)}) collective-permute-start(bf16[4,2,64,768]{3,2,1,0:T(8,128)(2,1)S(1)} %maximum_select_fusion.refs_0_), channel_id=1, source_target_pairs={{0,4},{1,17},{2,6},{3,19},{4,0},{5,21},{6,2},{7,23},{8,12},{9,25},... | collective-permute-start | bytes 2359304 | tf_op jit(solution)/shard_map/ppermute | solution.py:45
  43.3 9.9 %collective-permute-start.9 = (bf16[4,2,64,768]{3,2,1,0:T(8,128)(2,1)S(1)}, bf16[4,2,64,768]{3,2,1,0:T(8,128)(2,1)S(1)}, u32[]{:S(2)}, u32[]{:S(2)}) collective-permute-start(bf16[4,2,64,768]{3,2,1,0:T(8,128)(2,1)S(1)} %collective-permute-done.8.refs_2_), channel_id=1, source_target_pairs={{0,1},{1,0},{2,3},{3,2},{4,5},{5,4},{6,7},{7,6},{8,9},{9,8},{10,11... | collective-permute-start | bytes 2359304 | tf_op jit(solution)/shard_map/ppermute | solution.py:49
  43.3 9.9 %collective-permute-start.7 = (bf16[4,2,64,768]{3,2,1,0:T(8,128)(2,1)S(1)}, bf16[4,2,64,768]{3,2,1,0:T(8,128)(2,1)S(1)}, u32[]{:S(2)}, u32[]{:S(2)}) collective-permute-start(bf16[4,2,64,768]{3,2,1,0:T(8,128)(2,1)S(1)} %collective-permute-done.6.refs_1_), channel_id=1, source_target_pairs={{0,1},{1,0},{2,3},{3,2},{4,5},{5,4},{6,7},{7,6},{8,9},{9,8},{10,11... | collective-permute-start | bytes 2359304 | tf_op jit(solution)/shard_map/ppermute | solution.py:49
  53.2 3.4 %collective-permute-start.10 = (bf16[4,2,64,768]{3,2,1,0:T(8,128)(2,1)S(1)}, bf16[4,2,64,768]{3,2,1,0:T(8,128)(2,1)S(1)}, u32[]{:S(2)}, u32[]{:S(2)}) collective-permute-start(bf16[4,2,64,768]{3,2,1,0:T(8,128)(2,1)S(1)} %collective-permute-done.4.refs_3_), channel_id=1, source_target_pairs={{0,1},{1,0},{2,3},{3,2},{4,5},{5,4},{6,7},{7,6},{8,9},{9,8},{10,11... | collective-permute-start | bytes 2359304 | tf_op jit(solution)/shard_map/ppermute | solution.py:49
  63.0 5.8 %collective-permute-start.11 = (bf16[4,4,2,64,768]{4,3,2,1,0:T(8,128)(2,1)S(1)}, bf16[4,4,2,64,768]{4,3,2,1,0:T(8,128)(2,1)S(1)}, u32[]{:S(2)}, u32[]{:S(2)}) collective-permute-start(bf16[4,4,2,64,768]{4,3,2,1,0:T(8,128)(2,1)S(1)} %get-tuple-element.53), channel_id=1, source_target_pairs={{0,1},{1,0},{2,3},{3,2},{4,5},{5,4},{6,7},{7,6},{8,9},{9,8},{10,11... | collective-permute-start | bytes 9437192 | tf_op jit(solution)/shard_map/ppermute | solution.py:49
  70.1 13.7 %collective-permute-start.12 = (bf16[4,2,64,768]{3,2,1,0:T(8,128)(2,1)S(1)}, bf16[4,2,64,768]{3,2,1,0:T(8,128)(2,1)S(1)}, u32[]{:S(2)}, u32[]{:S(2)}) collective-permute-start(bf16[4,2,64,768]{3,2,1,0:T(8,128)(2,1)S(1)} %get-tuple-element.55), channel_id=1, source_target_pairs={{0,4},{1,17},{2,6},{3,19},{4,0},{5,21},{6,2},{7,23},{8,12},{9,25},... | collective-permute-start | bytes 2359304 | tf_op jit(solution)/shard_map/ppermute | solution.py:45
  70.4 19.6 %collective-permute-start.13 = (bf16[4,2,64,768]{3,2,1,0:T(8,128)(2,1)S(1)}, bf16[4,2,64,768]{3,2,1,0:T(8,128)(2,1)S(1)}, u32[]{:S(2)}, u32[]{:S(2)}) collective-permute-start(bf16[4,2,64,768]{3,2,1,0:T(8,128)(2,1)S(1)} %get-tuple-element.56), channel_id=1, source_target_pairs={{0,2},{1,9},{2,0},{3,11},{4,6},{5,13},{6,4},{7,15},{8,10},{9,1},{1... | collective-permute-start | bytes 2359304 | tf_op jit(solution)/shard_map/ppermute | solution.py:45
  71.5 20.6 %collective-permute-start.14 = (bf16[4,2,64,768]{3,2,1,0:T(8,128)(2,1)S(1)}, bf16[4,2,64,768]{3,2,1,0:T(8,128)(2,1)S(1)}, u32[]{:S(2)}, u32[]{:S(2)}) collective-permute-start(bf16[4,2,64,768]{3,2,1,0:T(8,128)(2,1)S(1)} %get-tuple-element.57), channel_id=1, source_target_pairs={{0,6},{1,25},{2,4},{3,27},{4,2},{5,29},{6,0},{7,31},{8,14},{9,17},... | collective-permute-start | bytes 2359304 | tf_op jit(solution)/shard_map/ppermute | solution.py:45
  92.6 7.3 %collective-permute-start.15 = (bf16[2,64,768]{2,1,0:T(8,128)(2,1)S(1)}, bf16[2,64,768]{2,1,0:T(8,128)(2,1)S(1)}, u32[]{:S(2)}, u32[]{:S(2)}) collective-permute-start(bf16[2,64,768]{2,1,0:T(8,128)(2,1)S(1)} %get-tuple-element.62), channel_id=1, source_target_pairs={{0,16},{1,5},{2,18},{3,7},{4,20},{5,1},{6,22},{7,3},{8,24},{9,13},... | collective-permute-start | bytes 589832 | tf_op jit(solution)/shard_map/ppermute | solution.py:45
  94.7 7.7 %collective-permute-start.16 = (bf16[2,64,768]{2,1,0:T(8,128)(2,1)S(1)}, bf16[2,64,768]{2,1,0:T(8,128)(2,1)S(1)}, u32[]{:S(2)}, u32[]{:S(2)}) collective-permute-start(bf16[2,64,768]{2,1,0:T(8,128)(2,1)S(1)} %get-tuple-element.63), channel_id=1, source_target_pairs={{0,8},{1,3},{2,10},{3,1},{4,12},{5,7},{6,14},{7,5},{8,0},{9,11},{1... | collective-permute-start | bytes 589832 | tf_op jit(solution)/shard_map/ppermute | solution.py:45
  96.6 6.9 %collective-permute-start.17 = (bf16[2,64,768]{2,1,0:T(8,128)(2,1)S(1)}, bf16[2,64,768]{2,1,0:T(8,128)(2,1)S(1)}, u32[]{:S(2)}, u32[]{:S(2)}) collective-permute-start(bf16[2,64,768]{2,1,0:T(8,128)(2,1)S(1)} %get-tuple-element.64), channel_id=1, source_target_pairs={{0,24},{1,7},{2,26},{3,5},{4,28},{5,3},{6,30},{7,1},{8,16},{9,15},... | collective-permute-start | bytes 589832 | tf_op jit(solution)/shard_map/ppermute | solution.py:45

commit v7 on v6

--- a/solution.py
+++ b/solution.py
@@ -136,8 +136,8 @@
 
 
 def gather(v, along_y):
-    far, near, next_ = lax.optimization_barrier(
-        tuple(swap(v, q, along_y) for q in (3, 1, 2))
+    next_, near, far = lax.optimization_barrier(
+        tuple(swap(v, q, along_y) for q in (2, 1, 3))
     )
     return [v, near, next_, far]
 

time: 118 us -> 117 us (level)
    ppermute x6, starting transfers between devices: 2.63 us -> 1.1 us  [to_core(): return lax.ppermute(v, 'cuts', [(i, i ^ 1) for i in range(2 * NX)])]
where the time goes in v7:
time: 117 us
  waiting for transfers between devices  45.1 us (39%)
  blocking collectives  29.4 us (25%)
  Pallas kernels  21.2 us (18%)
  starting transfers between devices  18.5 us (16%)
  other arithmetic  1.94 us (2%)
    ppermute x12, waiting for transfers between devices, swap(): return lax.ppermute(v, ('dp', 'cuts'), perm)  41.9 us
    all_to_all x2, blocking collectives, swap_z(): return lax.all_to_all(v, 'dp', 0, 0, axis_index_groups=Z_GROUPS, tiled=True)  29.4 us
    ppermute x12, starting transfers between devices, swap(): return lax.ppermute(v, ('dp', 'cuts'), perm)  17.4 us
    pallas_call x3, Pallas kernels, call(): pl.pallas_call(body, name=name, out_shape=out, in_specs=[pl.BlockSpec(mem...  13 us
    pallas_call x1, Pallas kernels, load_weights(): pl.pallas_call(weights_kernel, name='weights', out_shape=[jax.ShapeDtypeS...  5.52 us
    ppermute x6, waiting for transfers between devices, to_core(): return lax.ppermute(v, 'cuts', [(i, i ^ 1) for i in range(2 * NX)])  3.19 us
  transfers between devices with their start and end apart: 18, of which 13 were waited for; matrix products, arithmetic and copies ran while one was open for 0% of the time, Pallas kernels for 10%

profile of v7, /device:TPU:6, one launch (start us, length us, event | category | flops | bytes accessed | tf_op | source)
XLA Modules:
  0.0 117.0 jit_solution(16589759611551807514)
XLA Ops:
  0.7 1.8 %send.1 = bf16[8,16,768]{2,1,0:T(8,128)(2,1)} custom-call(bf16[16,768]{1,0:T(8,128)(2,1)} %tokens_in.1, bf16[16,768]{1,0:T(8,128)(2,1)} %dy_in.1, s32[2,16]{1,0:T(2,128)} %bitcast.47, f32[2,16]{1,0:T(2,128)} %bitcast.49), custom_call_target="tpu_custom_call" | custom-call | tf_op jit(solution)/shard_map/send/pallas_call | solution.py:309
  2.5 15.6 %all_to_all.10 = bf16[8,16,768]{2,1,0:T(8,128)(2,1)S(1)} all-to-all(bf16[8,16,768]{2,1,0:T(8,128)(2,1)} %send.1), channel_id=1, replica_groups={{224,192,160,128,96,64,32,0},{232,200,168,136,104,72,40,8},{240,208,176..., dimensions={0} | all-to-all | bytes 393216 | tf_op jit(solution)/shard_map/all_to_all | solution.py:25
  18.2 3.3 %collective-permute-start.2 = (bf16[2,64,768]{2,1,0:T(8,128)(2,1)S(1)}, bf16[2,64,768]{2,1,0:T(8,128)(2,1)S(1)}, u32[]{:S(2)}, u32[]{:S(2)}) collective-permute-start(bf16[2,64,768]{2,1,0:T(8,128)(2,1)S(1)} %get-tuple-element.83), channel_id=1, source_target_pairs={{0,16},{1,5},{2,18},{3,7},{4,20},{5,1},{6,22},{7,3},{8,24},{9,13},... | collective-permute-start | bytes 589832 | tf_op jit(solution)/shard_map/ppermute | solution.py:45
  21.4 0.7 collective-permute-start.1
  22.1 0.4 collective-permute-start
  22.5 2.9 %collective-permute-done.2 = bf16[2,64,768]{2,1,0:T(8,128)(2,1)S(1)} collective-permute-done((bf16[2,64,768]{2,1,0:T(8,128)(2,1)S(1)}, bf16[2,64,768]{2,1,0:T(8,128)(2,1)S(1)}, u32[]{:S(2)}, u32[]{:S(2)}) %collective-permute-start.2) | collective-permute-done | bytes 196640 | tf_op jit(solution)/shard_map/ppermute | solution.py:45
  25.4 2.4 %collective-permute-done.1 = bf16[2,64,768]{2,1,0:T(8,128)(2,1)S(1)} collective-permute-done((bf16[2,64,768]{2,1,0:T(8,128)(2,1)S(1)}, bf16[2,64,768]{2,1,0:T(8,128)(2,1)S(1)}, u32[]{:S(2)}, u32[]{:S(2)}) %collective-permute-start.1) | collective-permute-done | bytes 196640 | tf_op jit(solution)/shard_map/ppermute | solution.py:45
  27.9 1.1 collective-permute-done
  29.0 0.0 collective-permute-start.3
  29.0 1.2 collective-permute-done.3
  30.2 0.1 maximum_select_fusion.refs_0_
  30.3 0.6 collective-permute-start.8
  30.9 0.9 collective-permute-start.6
  31.8 0.1 collective-permute-start.5
  31.8 3.3 %collective-permute-start.4 = (bf16[4,2,64,768]{3,2,1,0:T(8,128)(2,1)S(1)}, bf16[4,2,64,768]{3,2,1,0:T(8,128)(2,1)S(1)}, u32[]{:S(2)}, u32[]{:S(2)}) collective-permute-start(bf16[4,2,64,768]{3,2,1,0:T(8,128)(2,1)S(1)} %maximum_select_fusion.refs_0_), channel_id=1, source_target_pairs={{0,4},{1,17},{2,6},{3,19},{4,0},{5,21},{6,2},{7,23},{8,12},{9,25},... | collective-permute-start | bytes 2359304 | tf_op jit(solution)/shard_map/ppermute | solution.py:45
  35.1 8.5 %collective-permute-done.8.refs_2_ = bf16[4,2,64,768]{3,2,1,0:T(8,128)(2,1)S(1)} collective-permute-done((bf16[4,2,64,768]{3,2,1,0:T(8,128)(2,1)S(1)}, bf16[4,2,64,768]{3,2,1,0:T(8,128)(2,1)S(1)}, u32[]{:S(2)}, u32[]{:S(2)}) %collective-permute-start.8) | collective-permute-done | bytes 786464 | tf_op jit(solution)/shard_map/ppermute | solution.py:45
  43.6 0.0 collective-permute-start.9
  43.6 0.0 collective-permute-done.6.refs_1_
  43.6 0.5 collective-permute-start.7
  44.1 5.5 %weights.1 = (bf16[4,1056,768]{2,1,0:T(8,128)(2,1)S(1)}, bf16[4,1056,768]{2,1,0:T(8,128)(2,1)S(1)}, bf16[3,16,64]{2,1,0:T(8,128)(2,1)S(1)}, bf16[16,64]{1,0:T(8,128)(2,1)S(1)}) custom-call(s32[2,5]{1,0:T(2,128)S(1)} %pad_add_fusion.infos, s32[2,16]{1,0:T(2,128)S(1)} %bitcast.48, f32[2,16]{1,0:T(2,128)S(1)} %bitcast.50, bf16[352,6144]{1,0:T(8,128)(2,1)} %bitcast.51, ...), custom_call_target="tpu_custom_call" | custom-call | bytes 27262976 | tf_op jit(solution)/shard_map/weights/pallas_call | solution.py:183
  49.7 0.0 collective-permute-done.5.refs_0_
  49.7 3.8 %collective-permute-done.4.refs_3_ = bf16[4,2,64,768]{3,2,1,0:T(8,128)(2,1)S(1)} collective-permute-done((bf16[4,2,64,768]{3,2,1,0:T(8,128)(2,1)S(1)}, bf16[4,2,64,768]{3,2,1,0:T(8,128)(2,1)S(1)}, u32[]{:S(2)}, u32[]{:S(2)}) %collective-permute-start.4) | collective-permute-done | bytes 786464 | tf_op jit(solution)/shard_map/ppermute | solution.py:45
  53.5 0.0 collective-permute-done.9.refs_2_
  53.5 0.0 collective-permute-start.10
  53.5 3.4 %own.1.refs_5_ = f32[1056,256]{1,0:T(8,128)S(1)} custom-call(s32[5]{0:T(128)S(1)} %get-tuple-element.73.info, bf16[4,2,64,768]{3,2,1,0:T(8,128)(2,1)S(1)} %maximum_select_fusion.refs_0_, bf16[4,2,64,768]{3,2,1,0:T(8,128)(2,1)S(1)} %collective-permute-done.6.refs_1_, bf16[4,2,64,768]{3,2,1,0:T(8,128)(2,1)S(1)} %collective-permute-done.8.refs_2_, ...), custom_call_target="tpu_custom_call" | custom-call | flops 1660944384 | bytes 7340032 | tf_op jit(solution)/shard_map/own/pallas_call | solution.py:275
  56.9 0.0 collective-permute-done.10.refs_3_
  56.9 6.4 %other.1 = (bf16[4,4,2,64,768]{4,3,2,1,0:T(8,128)(2,1)S(1)}, bf16[256,352]{1,0:T(8,128)(2,1)S(1)}, bf16[256,704]{1,0:T(8,128)(2,1)S(1)}) custom-call(s32[5]{0:T(128)S(1)} %get-tuple-element.72.info, bf16[4,2,64,768]{3,2,1,0:T(8,128)(2,1)S(1)} %collective-permute-done.5.refs_0_, bf16[4,2,64,768]{3,2,1,0:T(8,128)(2,1)S(1)} %collective-permute-done.7.refs_1_, ...), custom_call_target="tpu_custom_call" | custom-call | flops 3321888768 | bytes 7340032 | tf_op jit(solution)/shard_map/other/pallas_call | solution.py:275
  63.3 0.5 collective-permute-start.11
  63.9 3.3 %last.1 = bf16[4,4,2,64,768]{4,3,2,1,0:T(8,128)(2,1)S(1)} custom-call(s32[5]{0:T(128)S(1)} %get-tuple-element.73.info, bf16[256,352]{1,0:T(8,128)(2,1)S(1)} %get-tuple-element.51.hidden, bf16[256,704]{1,0:T(8,128)(2,1)S(1)} %get-tuple-element.52.grads, bf16[4,1056,768]{2,1,0:T(8,128)(2,1)S(1)} %get-tuple-element.50.refs_4_.buf), custom_call_target="tpu_custom_call" | custom-call | flops 1660944384 | bytes 7340032 | tf_op jit(solution)/shard_map/last/pallas_call | solution.py:275
  67.1 2.0 %collective-permute-done.11 = bf16[4,4,2,64,768]{4,3,2,1,0:T(8,128)(2,1)S(1)} collective-permute-done((bf16[4,4,2,64,768]{4,3,2,1,0:T(8,128)(2,1)S(1)}, bf16[4,4,2,64,768]{4,3,2,1,0:T(8,128)(2,1)S(1)}, u32[]{:S(2)}, u32[]{:S(2)}) %collective-permute-start.11) | collective-permute-done | bytes 3145760 | tf_op jit(solution)/shard_map/ppermute | solution.py:49
  69.1 1.2 %fusion.3 = (bf16[4,2,64,768]{3,2,1,0:T(8,128)(2,1)S(1)}, bf16[4,2,64,768]{3,2,1,0:T(8,128)(2,1)S(1)}, bf16[4,2,64,768]{3,2,1,0:T(8,128)(2,1)S(1)}, bf16[4,2,64,768]{3,2,1,0:T(8,128)(2,1)S(1)}) fusion(bf16[4,4,2,64,768]{4,3,2,1,0:T(8,128)(2,1)S(1)} %collective-permute-done.11, bf16[4,4,2,64,768]{4,3,2,1,0:T(8,128)(2,1)S(1)} %last.1), kind=kLoop, calls=%fused_computation.8 | loop fusion | flops 6291456 | bytes 9437184 | tf_op jit(solution)/shard_map/convert_element_type | solution.py:149
  70.4 0.3 collective-permute-start.12
  70.7 1.1 collective-permute-start.13
  71.9 2.7 %collective-permute-start.14 = (bf16[4,2,64,768]{3,2,1,0:T(8,128)(2,1)S(1)}, bf16[4,2,64,768]{3,2,1,0:T(8,128)(2,1)S(1)}, u32[]{:S(2)}, u32[]{:S(2)}) collective-permute-start(bf16[4,2,64,768]{3,2,1,0:T(8,128)(2,1)S(1)} %get-tuple-element.57), channel_id=1, source_target_pairs={{0,6},{1,25},{2,4},{3,27},{4,2},{5,29},{6,0},{7,31},{8,14},{9,17},... | collective-permute-start | bytes 2359304 | tf_op jit(solution)/shard_map/ppermute | solution.py:45
  74.6 9.5 %collective-permute-done.12 = bf16[4,2,64,768]{3,2,1,0:T(8,128)(2,1)S(1)} collective-permute-done((bf16[4,2,64,768]{3,2,1,0:T(8,128)(2,1)S(1)}, bf16[4,2,64,768]{3,2,1,0:T(8,128)(2,1)S(1)}, u32[]{:S(2)}, u32[]{:S(2)}) %collective-permute-start.12) | collective-permute-done | bytes 786464 | tf_op jit(solution)/shard_map/ppermute | solution.py:45
  84.1 6.2 %collective-permute-done.13 = bf16[4,2,64,768]{3,2,1,0:T(8,128)(2,1)S(1)} collective-permute-done((bf16[4,2,64,768]{3,2,1,0:T(8,128)(2,1)S(1)}, bf16[4,2,64,768]{3,2,1,0:T(8,128)(2,1)S(1)}, u32[]{:S(2)}, u32[]{:S(2)}) %collective-permute-start.13) | collective-permute-done | bytes 786464 | tf_op jit(solution)/shard_map/ppermute | solution.py:45
  90.3 2.1 %collective-permute-done.14 = bf16[4,2,64,768]{3,2,1,0:T(8,128)(2,1)S(1)} collective-permute-done((bf16[4,2,64,768]{3,2,1,0:T(8,128)(2,1)S(1)}, bf16[4,2,64,768]{3,2,1,0:T(8,128)(2,1)S(1)}, u32[]{:S(2)}, u32[]{:S(2)}) %collective-permute-start.14) | collective-permute-done | bytes 786464 | tf_op jit(solution)/shard_map/ppermute | solution.py:45
  92.4 0.4 add_convert_fusion
  92.8 0.1 slice_bitcast_fusion
  92.9 1.9 %collective-permute-start.15 = (bf16[2,64,768]{2,1,0:T(8,128)(2,1)S(1)}, bf16[2,64,768]{2,1,0:T(8,128)(2,1)S(1)}, u32[]{:S(2)}, u32[]{:S(2)}) collective-permute-start(bf16[2,64,768]{2,1,0:T(8,128)(2,1)S(1)} %get-tuple-element.62), channel_id=1, source_target_pairs={{0,16},{1,5},{2,18},{3,7},{4,20},{5,1},{6,22},{7,3},{8,24},{9,13},... | collective-permute-start | bytes 589832 | tf_op jit(solution)/shard_map/ppermute | solution.py:45
  94.7 0.7 collective-permute-start.16
  95.4 1.7 %collective-permute-start.17 = (bf16[2,64,768]{2,1,0:T(8,128)(2,1)S(1)}, bf16[2,64,768]{2,1,0:T(8,128)(2,1)S(1)}, u32[]{:S(2)}, u32[]{:S(2)}) collective-permute-start(bf16[2,64,768]{2,1,0:T(8,128)(2,1)S(1)} %get-tuple-element.64), channel_id=1, source_target_pairs={{0,24},{1,7},{2,26},{3,5},{4,28},{5,3},{6,30},{7,1},{8,16},{9,15},... | collective-permute-start | bytes 589832 | tf_op jit(solution)/shard_map/ppermute | solution.py:45
  97.1 3.1 %collective-permute-done.15 = bf16[2,64,768]{2,1,0:T(8,128)(2,1)S(1)} collective-permute-done((bf16[2,64,768]{2,1,0:T(8,128)(2,1)S(1)}, bf16[2,64,768]{2,1,0:T(8,128)(2,1)S(1)}, u32[]{:S(2)}, u32[]{:S(2)}) %collective-permute-start.15) | collective-permute-done | bytes 196640 | tf_op jit(solution)/shard_map/ppermute | solution.py:45
  100.2 1.0 collective-permute-done.16
  101.2 1.1 collective-permute-done.17
  102.3 0.1 copy_bitcast_fusion
  102.4 13.8 %all_to_all.11.back = bf16[8,16,768]{2,1,0:T(8,128)(2,1)S(1)} all-to-all(bf16[8,16,768]{2,1,0:T(8,128)(2,1)S(1)} %copy_bitcast_fusion), channel_id=1, replica_groups={{224,192,160,128,96,64,32,0},{232,200,168,136,104,72,40,8},{240,208,176..., dimensions={0} | all-to-all | bytes 393216 | tf_op jit(solution)/shard_map/all_to_all | solution.py:25
  116.2 0.8 combine.1
  (11 shorter events, 0.1 us)
Async XLA Ops:
  0.6 43.5 %copy-start = (s32[16,2]{0,1:T(2,128)S(1)}, s32[16,2]{0,1:T(2,128)}, u32[]{:S(2)}) copy-start(s32[16,2]{0,1:T(2,128)} %param.10) | copy-start | bytes 388
  0.6 43.5 %copy-start.1 = (f32[16,2]{0,1:T(2,128)S(1)}, f32[16,2]{0,1:T(2,128)}, u32[]{:S(2)}) copy-start(f32[16,2]{0,1:T(2,128)} %param.9) | copy-start | bytes 388
  18.2 7.3 %collective-permute-start.2 = (bf16[2,64,768]{2,1,0:T(8,128)(2,1)S(1)}, bf16[2,64,768]{2,1,0:T(8,128)(2,1)S(1)}, u32[]{:S(2)}, u32[]{:S(2)}) collective-permute-start(bf16[2,64,768]{2,1,0:T(8,128)(2,1)S(1)} %get-tuple-element.83), channel_id=1, source_target_pairs={{0,16},{1,5},{2,18},{3,7},{4,20},{5,1},{6,22},{7,3},{8,24},{9,13},... | collective-permute-start | bytes 589832 | tf_op jit(solution)/shard_map/ppermute | solution.py:45
  21.4 6.4 %collective-permute-start.1 = (bf16[2,64,768]{2,1,0:T(8,128)(2,1)S(1)}, bf16[2,64,768]{2,1,0:T(8,128)(2,1)S(1)}, u32[]{:S(2)}, u32[]{:S(2)}) collective-permute-start(bf16[2,64,768]{2,1,0:T(8,128)(2,1)S(1)} %get-tuple-element.83), channel_id=1, source_target_pairs={{0,8},{1,3},{2,10},{3,1},{4,12},{5,7},{6,14},{7,5},{8,0},{9,11},{1... | collective-permute-start | bytes 589832 | tf_op jit(solution)/shard_map/ppermute | solution.py:45
  22.1 6.9 %collective-permute-start = (bf16[2,64,768]{2,1,0:T(8,128)(2,1)S(1)}, bf16[2,64,768]{2,1,0:T(8,128)(2,1)S(1)}, u32[]{:S(2)}, u32[]{:S(2)}) collective-permute-start(bf16[2,64,768]{2,1,0:T(8,128)(2,1)S(1)} %get-tuple-element.83), channel_id=1, source_target_pairs={{0,24},{1,7},{2,26},{3,5},{4,28},{5,3},{6,30},{7,1},{8,16},{9,15},... | collective-permute-start | bytes 589832 | tf_op jit(solution)/shard_map/ppermute | solution.py:45
  29.0 1.2 %collective-permute-start.3 = (bf16[8,768]{1,0:T(8,128)(2,1)S(1)}, bf16[8,768]{1,0:T(8,128)(2,1)S(1)}, u32[]{:S(2)}, u32[]{:S(2)}) collective-permute-start(bf16[8,768]{1,0:T(8,128)(2,1)S(1)} %slice_bitcast_fusion.4), channel_id=1, source_target_pairs={{0,1},{1,0},{2,3},{3,2},{4,5},{5,4},{6,7},{7,6},{8,9},{9,8},{10,11... | collective-permute-start | bytes 36872 | tf_op jit(solution)/shard_map/ppermute | solution.py:49
  30.3 13.3 %collective-permute-start.8 = (bf16[4,2,64,768]{3,2,1,0:T(8,128)(2,1)S(1)}, bf16[4,2,64,768]{3,2,1,0:T(8,128)(2,1)S(1)}, u32[]{:S(2)}, u32[]{:S(2)}) collective-permute-start(bf16[4,2,64,768]{3,2,1,0:T(8,128)(2,1)S(1)} %maximum_select_fusion.refs_0_), channel_id=1, source_target_pairs={{0,6},{1,25},{2,4},{3,27},{4,2},{5,29},{6,0},{7,31},{8,14},{9,17},... | collective-permute-start | bytes 2359304 | tf_op jit(solution)/shard_map/ppermute | solution.py:45
  30.9 12.7 %collective-permute-start.6 = (bf16[4,2,64,768]{3,2,1,0:T(8,128)(2,1)S(1)}, bf16[4,2,64,768]{3,2,1,0:T(8,128)(2,1)S(1)}, u32[]{:S(2)}, u32[]{:S(2)}) collective-permute-start(bf16[4,2,64,768]{3,2,1,0:T(8,128)(2,1)S(1)} %maximum_select_fusion.refs_0_), channel_id=1, source_target_pairs={{0,2},{1,9},{2,0},{3,11},{4,6},{5,13},{6,4},{7,15},{8,10},{9,1},{1... | collective-permute-start | bytes 2359304 | tf_op jit(solution)/shard_map/ppermute | solution.py:45
  31.8 17.9 %collective-permute-start.5 = (bf16[4,2,64,768]{3,2,1,0:T(8,128)(2,1)S(1)}, bf16[4,2,64,768]{3,2,1,0:T(8,128)(2,1)S(1)}, u32[]{:S(2)}, u32[]{:S(2)}) collective-permute-start(bf16[4,2,64,768]{3,2,1,0:T(8,128)(2,1)S(1)} %maximum_select_fusion.refs_0_), channel_id=1, source_target_pairs={{0,1},{1,0},{2,3},{3,2},{4,5},{5,4},{6,7},{7,6},{8,9},{9,8},{10,11... | collective-permute-start | bytes 2359304 | tf_op jit(solution)/shard_map/ppermute | solution.py:49
  31.8 21.7 %collective-permute-start.4 = (bf16[4,2,64,768]{3,2,1,0:T(8,128)(2,1)S(1)}, bf16[4,2,64,768]{3,2,1,0:T(8,128)(2,1)S(1)}, u32[]{:S(2)}, u32[]{:S(2)}) collective-permute-start(bf16[4,2,64,768]{3,2,1,0:T(8,128)(2,1)S(1)} %maximum_select_fusion.refs_0_), channel_id=1, source_target_pairs={{0,4},{1,17},{2,6},{3,19},{4,0},{5,21},{6,2},{7,23},{8,12},{9,25},... | collective-permute-start | bytes 2359304 | tf_op jit(solution)/shard_map/ppermute | solution.py:45
  43.6 9.9 %collective-permute-start.9 = (bf16[4,2,64,768]{3,2,1,0:T(8,128)(2,1)S(1)}, bf16[4,2,64,768]{3,2,1,0:T(8,128)(2,1)S(1)}, u32[]{:S(2)}, u32[]{:S(2)}) collective-permute-start(bf16[4,2,64,768]{3,2,1,0:T(8,128)(2,1)S(1)} %collective-permute-done.8.refs_2_), channel_id=1, source_target_pairs={{0,1},{1,0},{2,3},{3,2},{4,5},{5,4},{6,7},{7,6},{8,9},{9,8},{10,11... | collective-permute-start | bytes 2359304 | tf_op jit(solution)/shard_map/ppermute | solution.py:49
  43.6 9.9 %collective-permute-start.7 = (bf16[4,2,64,768]{3,2,1,0:T(8,128)(2,1)S(1)}, bf16[4,2,64,768]{3,2,1,0:T(8,128)(2,1)S(1)}, u32[]{:S(2)}, u32[]{:S(2)}) collective-permute-start(bf16[4,2,64,768]{3,2,1,0:T(8,128)(2,1)S(1)} %collective-permute-done.6.refs_1_), channel_id=1, source_target_pairs={{0,1},{1,0},{2,3},{3,2},{4,5},{5,4},{6,7},{7,6},{8,9},{9,8},{10,11... | collective-permute-start | bytes 2359304 | tf_op jit(solution)/shard_map/ppermute | solution.py:49
  53.5 3.4 %collective-permute-start.10 = (bf16[4,2,64,768]{3,2,1,0:T(8,128)(2,1)S(1)}, bf16[4,2,64,768]{3,2,1,0:T(8,128)(2,1)S(1)}, u32[]{:S(2)}, u32[]{:S(2)}) collective-permute-start(bf16[4,2,64,768]{3,2,1,0:T(8,128)(2,1)S(1)} %collective-permute-done.4.refs_3_), channel_id=1, source_target_pairs={{0,1},{1,0},{2,3},{3,2},{4,5},{5,4},{6,7},{7,6},{8,9},{9,8},{10,11... | collective-permute-start | bytes 2359304 | tf_op jit(solution)/shard_map/ppermute | solution.py:49
  63.3 5.8 %collective-permute-start.11 = (bf16[4,4,2,64,768]{4,3,2,1,0:T(8,128)(2,1)S(1)}, bf16[4,4,2,64,768]{4,3,2,1,0:T(8,128)(2,1)S(1)}, u32[]{:S(2)}, u32[]{:S(2)}) collective-permute-start(bf16[4,4,2,64,768]{4,3,2,1,0:T(8,128)(2,1)S(1)} %get-tuple-element.53), channel_id=1, source_target_pairs={{0,1},{1,0},{2,3},{3,2},{4,5},{5,4},{6,7},{7,6},{8,9},{9,8},{10,11... | collective-permute-start | bytes 9437192 | tf_op jit(solution)/shard_map/ppermute | solution.py:49
  70.4 13.7 %collective-permute-start.12 = (bf16[4,2,64,768]{3,2,1,0:T(8,128)(2,1)S(1)}, bf16[4,2,64,768]{3,2,1,0:T(8,128)(2,1)S(1)}, u32[]{:S(2)}, u32[]{:S(2)}) collective-permute-start(bf16[4,2,64,768]{3,2,1,0:T(8,128)(2,1)S(1)} %get-tuple-element.55), channel_id=1, source_target_pairs={{0,4},{1,17},{2,6},{3,19},{4,0},{5,21},{6,2},{7,23},{8,12},{9,25},... | collective-permute-start | bytes 2359304 | tf_op jit(solution)/shard_map/ppermute | solution.py:45
  70.7 19.6 %collective-permute-start.13 = (bf16[4,2,64,768]{3,2,1,0:T(8,128)(2,1)S(1)}, bf16[4,2,64,768]{3,2,1,0:T(8,128)(2,1)S(1)}, u32[]{:S(2)}, u32[]{:S(2)}) collective-permute-start(bf16[4,2,64,768]{3,2,1,0:T(8,128)(2,1)S(1)} %get-tuple-element.56), channel_id=1, source_target_pairs={{0,2},{1,9},{2,0},{3,11},{4,6},{5,13},{6,4},{7,15},{8,10},{9,1},{1... | collective-permute-start | bytes 2359304 | tf_op jit(solution)/shard_map/ppermute | solution.py:45
  71.9 20.6 %collective-permute-start.14 = (bf16[4,2,64,768]{3,2,1,0:T(8,128)(2,1)S(1)}, bf16[4,2,64,768]{3,2,1,0:T(8,128)(2,1)S(1)}, u32[]{:S(2)}, u32[]{:S(2)}) collective-permute-start(bf16[4,2,64,768]{3,2,1,0:T(8,128)(2,1)S(1)} %get-tuple-element.57), channel_id=1, source_target_pairs={{0,6},{1,25},{2,4},{3,27},{4,2},{5,29},{6,0},{7,31},{8,14},{9,17},... | collective-permute-start | bytes 2359304 | tf_op jit(solution)/shard_map/ppermute | solution.py:45
  92.9 7.3 %collective-permute-start.15 = (bf16[2,64,768]{2,1,0:T(8,128)(2,1)S(1)}, bf16[2,64,768]{2,1,0:T(8,128)(2,1)S(1)}, u32[]{:S(2)}, u32[]{:S(2)}) collective-permute-start(bf16[2,64,768]{2,1,0:T(8,128)(2,1)S(1)} %get-tuple-element.62), channel_id=1, source_target_pairs={{0,16},{1,5},{2,18},{3,7},{4,20},{5,1},{6,22},{7,3},{8,24},{9,13},... | collective-permute-start | bytes 589832 | tf_op jit(solution)/shard_map/ppermute | solution.py:45
  94.7 6.4 %collective-permute-start.16 = (bf16[2,64,768]{2,1,0:T(8,128)(2,1)S(1)}, bf16[2,64,768]{2,1,0:T(8,128)(2,1)S(1)}, u32[]{:S(2)}, u32[]{:S(2)}) collective-permute-start(bf16[2,64,768]{2,1,0:T(8,128)(2,1)S(1)} %get-tuple-element.63), channel_id=1, source_target_pairs={{0,8},{1,3},{2,10},{3,1},{4,12},{5,7},{6,14},{7,5},{8,0},{9,11},{1... | collective-permute-start | bytes 589832 | tf_op jit(solution)/shard_map/ppermute | solution.py:45
  95.4 6.9 %collective-permute-start.17 = (bf16[2,64,768]{2,1,0:T(8,128)(2,1)S(1)}, bf16[2,64,768]{2,1,0:T(8,128)(2,1)S(1)}, u32[]{:S(2)}, u32[]{:S(2)}) collective-permute-start(bf16[2,64,768]{2,1,0:T(8,128)(2,1)S(1)} %get-tuple-element.64), channel_id=1, source_target_pairs={{0,24},{1,7},{2,26},{3,5},{4,28},{5,3},{6,30},{7,1},{8,16},{9,15},... | collective-permute-start | bytes 589832 | tf_op jit(solution)/shard_map/ppermute | solution.py:45
